TPU v7x, 32 devices: a whole 2x2x4 slice. The times are simulated.
32 devices in a mesh: seq: 16 (over z, y, x), head: 2 (over core).
Axes of the slice: x: 2, y: 2, z: 4, core: 2. Of those that a mesh axis runs over, the one named last changes fastest.
Arguments:
- queries: bfloat16 [2048, 4096], P('seq', 'head'), may hold values from -6 to 6
- keys: bfloat16 [2048, 4096], P('seq', 'head'), may hold values from -6 to 6
- values: bfloat16 [2048, 4096], P('seq', 'head'), may hold values from -6 to 6
- level_index: int32 [2048, 8], P('seq'), may hold values from 0 to 15
- level_table: float32 [32, 16], P('head'), may hold values from 0.25 to 4
- out_weight: bfloat16 [4096, 4096], P('head', 'seq'), may hold values from -0.09375 to 0.09375
Outputs:
- output: bfloat16 [2048, 4096], P('seq', 'head')
All inputs are finite; a program needn't handle non-finite values.
Results may differ from a plain program's by a relative error of at most 0.0057.
Values may be sent and summed in bfloat16 or wider, within the bound.
No kernel may reach another device: no remote copies, remote signals or barrier semaphores. Data moves between devices by JAX's collectives and lax.ppermute only.
A program may use at most 64 MiB of HBM per device.

v0:
```python
import math

import jax
import jax.numpy as jnp
from jax import lax
from jax.sharding import PartitionSpec as P

DH = 128
VALS = 16


def swap(value, mask):
    pairs = [(source, source ^ mask) for source in range(lax.axis_size("seq"))]
    return lax.ppermute(value, "seq", pairs)


def lift(value, mask):
    pairs = [(source, source ^ mask) for source in range(lax.axis_size("seq")) if not source & mask]
    return lax.ppermute(value, "seq", pairs)


def swap_cores(value):
    return lax.ppermute(value, "head", [(0, 1), (1, 0)])


def send_home(value, mask, top):
    pairs = []
    for source in range(lax.axis_size("seq")):
        for core in range(2):
            target = source ^ mask ^ (core << top)
            pairs.append((source * 2 + core, target * 2 + (source >> top & 1)))
    return lax.ppermute(value, ("seq", "head"), pairs)


def masks_of(bits):
    out = [0]
    for bit in bits:
        out = out + [mask | 1 << bit for mask in out]
    return out


def spread(own, bits):
    pieces = {0: own}
    for bit in bits:
        for mask in list(pieces):
            pieces[mask | 1 << bit] = swap(pieces[mask], 1 << bit)
    return pieces


def absolute(pieces, bits, position):
    for bit in bits:
        flag = position >> bit & 1 == 1
        pieces = {mask: jnp.where(flag, pieces[mask ^ 1 << bit], piece) for mask, piece in pieces.items()}
    return pieces


def groups(depth):
    low_token_bits = [1] if depth < 6 else [1, 2]
    column_bits = [bit for bit in range(depth - 1) if bit not in low_token_bits][::-1]
    return low_token_bits, column_bits


def level_states(state, position, depth):
    top = depth - 1
    wide = lambda value: value.astype(jnp.float32)
    set_at = lambda level: position >> level & 1 == 1
    none = jnp.bfloat16(0)
    own = [part.astype(jnp.bfloat16) for part in state]
    near, side, corner = [None, None], [None, None], [None, None]
    near[0] = swap(own[0], 1)
    side[0] = swap(own[1], 2)
    corner[0] = swap(side[0], 1)
    side[1] = swap(own[0], 2)
    near[1] = swap(own[1], 1)
    corner[1] = swap(near[0], 2)
    read = []
    for part in range(2):
        pair = wide(side[part]) + wide(corner[part])
        block = state[part] + wide(near[part]) + pair
        mine = [
            jnp.where(set_at(0), near[part], none),
            jnp.where(set_at(1), pair, 0.0).astype(jnp.bfloat16),
        ]
        for level in range(2, top):
            if part == 1 and level == top - 1:
                mine.append(lift(block.astype(jnp.bfloat16), 1 << level))
            else:
                other = swap(block.astype(jnp.bfloat16), 1 << level)
                mine.append(jnp.where(set_at(level), other, none))
                block = block + wide(other)
        if part == 0:
            last = lift(block.astype(jnp.bfloat16), 1 << top)
            mine.append(last)
        else:
            mine.append(swap(last, 2))
        read.append(mine)
    return read


def shards(queries, keys, values, level_index, level_table, out_weight):
    rows = queries.shape[0]
    heads_here = level_table.shape[0]
    half = heads_here // 2
    position = lax.axis_index("seq")
    core = lax.axis_index("head")
    depth = lax.axis_size("seq").bit_length() - 1
    top = depth - 1
    low_token_bits, column_bits = groups(depth)

    flip = position >> 1 & 1
    flipped = flip == 1
    starts = [flip * half, (1 - flip) * half]

    def halves(value):
        return [
            lax.dynamic_slice_in_dim(value, start * DH, half * DH, 1).reshape(rows, half, DH)
            for start in starts
        ]

    query_heads, key_heads, value_heads = halves(queries), halves(keys), halves(values)
    state = [
        jnp.einsum("tha,thb->hab", key, value, preferred_element_type=jnp.float32)
        for key, value in zip(key_heads, value_heads)
    ]
    weights_of = spread(out_weight, column_bits)
    read = level_states(state, position, depth)

    onehot = (level_index[:, :, None] == jnp.arange(VALS, dtype=jnp.int32)[None, None, :]).astype(
        jnp.float32
    )
    level_weight = jnp.einsum("tlv,hv->tlh", onehot, level_table, precision=lax.Precision.HIGHEST)
    inv_root = 1.0 / math.sqrt(DH)
    causal = jnp.arange(rows)[:, None] >= jnp.arange(rows)[None, :]
    normed = []
    for part in range(2):
        lam = lax.dynamic_slice_in_dim(level_weight, starts[part], half, 2)
        scores = jnp.einsum(
            "tha,sha->hts", query_heads[part], key_heads[part], preferred_element_type=jnp.float32
        )
        factor = jnp.transpose(lam[:, 0, :]) * (inv_root / math.sqrt(rows))
        weights = jnp.where(causal[None], scores * factor[:, :, None], 0.0).astype(jnp.bfloat16)
        total = jnp.einsum("hts,shb->thb", weights, value_heads[part], preferred_element_type=jnp.float32)
        for level in range(depth):
            reads = jnp.einsum("tha,hab->thb", query_heads[part], read[part][level], preferred_element_type=jnp.float32)
            scale = lam[:, level + 1, :] * (inv_root / math.sqrt(rows * 2**level))
            total = total + reads * scale[:, :, None]
        square = jnp.mean(total * total, axis=-1, keepdims=True)
        normed.append((total * lax.rsqrt(square + 1e-06)).astype(jnp.bfloat16).reshape(rows, half * DH))

    pieces = {0: tuple(normed)}
    for bit in [top] + low_token_bits:
        for mask in list(pieces):
            new = mask | 1 << bit
            got = [swap(pieces[mask][part], 1 << bit) for part in range(2)]
            pieces[new] = tuple(got[::-1] if bit == 1 else got)
    token_masks = masks_of(low_token_bits)
    token_masks = token_masks + [mask | 1 << top for mask in token_masks]
    tokens = jnp.concatenate(
        [
            jnp.where(
                flipped,
                jnp.concatenate(pieces[mask][::-1], axis=1),
                jnp.concatenate(pieces[mask], axis=1),
            )
            for mask in token_masks
        ],
        axis=0,
    )
    column_masks = sorted(weights_of)
    kept = tokens.shape[0] // 2
    first_core = core == 0
    sums = {}
    for mask in column_masks:
        part = jnp.dot(tokens, weights_of[mask], preferred_element_type=jnp.float32)
        keep = jnp.where(first_core, part[:kept], part[kept:])
        give = jnp.where(first_core, part[kept:], part[:kept]).astype(jnp.bfloat16)
        sums[mask] = (keep + swap_cores(give).astype(jnp.float32)).astype(jnp.bfloat16)
    sums = absolute(sums, column_bits, position)
    summed = jnp.concatenate([sums[mask] for mask in column_masks], axis=1)
    landed = {}
    for at, mask in enumerate(masks_of(low_token_bits)):
        landed[mask] = send_home(summed[at * rows : (at + 1) * rows], mask, top)
    landed = absolute(landed, low_token_bits, position)
    width = out_weight.shape[1]
    columns = {}
    for mask, piece in landed.items():
        for at, column_mask in enumerate(column_masks):
            columns[mask | column_mask] = piece[:, at * width : (at + 1) * width]
    return jnp.concatenate([columns[mask] for mask in sorted(columns)], axis=1)


def solution(mesh):
    placed = (
        P("seq", "head"),
        P("seq", "head"),
        P("seq", "head"),
        P("seq", None),
        P("head", None),
        P("head", "seq"),
    )
    return jax.shard_map(
        shards, mesh=mesh, in_specs=placed, out_specs=P("seq", "head"), check_vma=False
    )
```

profile of v0, /device:TPU:9, one launch (start us, length us, event | category | flops | bytes accessed | tf_op | source)
XLA Modules:
  0.0 123.8 jit_solution(3059736694213215126)
XLA Ops:
  1.1 2.0 %constant_dynamic-slice_fusion = (bf16[128,1024]{1,0:T(8,128)(2,1)S(1)}, bf16[128,1024]{1,0:T(8,128)(2,1)}, bf16[128,1024]{1,0:T(8,128)(2,1)S(1)}, bf16[128,1024]{1,0:T(8,128)(2,1)S(1)}) fusion(bf16[128,2048]{1,0:T(8,128)(2,1)} %param.6, s32[]{:T(128)S(6)} %select_n.170, s32[]{:T(128)S(6)} %select_n.164, bf16[128,2048]{1,0:T(8,128)(2,1)} %param.8), kind=kLoop, calls=%fused_computation.115 | loop fusion | bytes 2097160 | tf_op jit(solution)/shard_map/dynamic_slice | solution.py:116
  4.5 1.2 collective-permute-start.2
  5.7 1.2 collective-permute-start.1
  9.2 9.3 %collective-permute-done.5 = bf16[8,128,128]{2,1,0:T(8,128)(2,1)S(1)} collective-permute-done((bf16[8,128,128]{2,1,0:T(8,128)(2,1)}, bf16[8,128,128]{2,1,0:T(8,128)(2,1)S(1)}, u32[]{:S(2)}, u32[]{:S(2)}) %collective-permute-start.5) | collective-permute-done | bytes 262176 | tf_op jit(solution)/shard_map/ppermute | solution.py:14
  18.8 1.3 %convolution_bitcast_fusion.4 = f32[128,8,128]{0,2,1:T(8,128)} fusion(bf16[128,8,128]{0,2,1:T(8,128)(2,1)S(1)} %bitcast.131, bf16[128,8,128]{0,2,1:T(8,128)(2,1)S(1)} %bitcast.121, bf16[128,8,128]{0,2,1:T(8,128)(2,1)S(1)} %bitcast.133, f32[8,128]{1,0:T(8,128)S(1)} %get-tuple-element.30, pred[128,128]{1,0:T(8,128)(4,1)S(1)} %iota_compare_fusion.1), kind=kOutput, calls=%fused_computation.5 | convolution fusion | flops 67502080 | bytes 1331200 | tf_op jit(solution)/shard_map/hts,shb->thb/dot_general | solution.py:142
  21.2 1.3 %convolution_bitcast_fusion.9 = f32[128,8,128]{0,2,1:T(8,128)} fusion(bf16[128,8,128]{0,2,1:T(8,128)(2,1)S(1)} %bitcast.127, bf16[128,8,128]{0,2,1:T(8,128)(2,1)S(1)} %bitcast.116, bf16[128,8,128]{0,2,1:T(8,128)(2,1)S(1)} %bitcast.129, f32[8,128]{1,0:T(8,128)S(1)} %get-tuple-element.34, pred[128,128]{1,0:T(8,128)(4,1)S(1)} %iota_compare_fusion.1), kind=kOutput, calls=%fused_computation.10 | convolution fusion | flops 67502080 | bytes 1331200 | tf_op jit(solution)/shard_map/hts,shb->thb/dot_general | solution.py:142
  22.5 1.2 %collective-permute-start.3 = (bf16[8,128,128]{2,1,0:T(8,128)(2,1)S(1)}, bf16[8,128,128]{2,1,0:T(8,128)(2,1)S(1)}, u32[]{:S(2)}, u32[]{:S(2)}) collective-permute-start(bf16[8,128,128]{2,1,0:T(8,128)(2,1)S(1)} %collective-permute-done.2), channel_id=1, source_target_pairs={{0,4},{2,6},{4,0},{6,2},{8,12},{10,14},{12,8},{14,10},{16,20},{18,... | collective-permute-start | bytes 786440 | tf_op jit(solution)/shard_map/ppermute | solution.py:14
  25.2 3.3 %collective-permute-done.3 = bf16[8,128,128]{2,1,0:T(8,128)(2,1)S(1)} collective-permute-done((bf16[8,128,128]{2,1,0:T(8,128)(2,1)S(1)}, bf16[8,128,128]{2,1,0:T(8,128)(2,1)S(1)}, u32[]{:S(2)}, u32[]{:S(2)}) %collective-permute-start.3) | collective-permute-done | bytes 262176 | tf_op jit(solution)/shard_map/ppermute | solution.py:14
  29.5 1.3 %collective-permute-start.4 = (bf16[8,128,128]{2,1,0:T(8,128)(2,1)S(1)}, bf16[8,128,128]{2,1,0:T(8,128)(2,1)S(1)}, u32[]{:S(2)}, u32[]{:S(2)}) collective-permute-start(bf16[8,128,128]{2,1,0:T(8,128)(2,1)S(1)} %add_convert_fusion.1), channel_id=1, source_target_pairs={{0,8},{2,10},{4,12},{6,14},{16,24},{18,26},{20,28},{22,30},{1,9},{... | collective-permute-start | bytes 786440 | tf_op jit(solution)/shard_map/ppermute | solution.py:19
  31.1 1.3 %fusion.4 = f32[128,8,128]{0,2,1:T(8,128)S(1)} fusion(bf16[128,8,128]{0,2,1:T(8,128)(2,1)S(1)} %bitcast.117, bf16[8,128,128]{2,1,0:T(8,128)(2,1)S(1)} %collective-permute-done.3, bf16[8,128,128]{2,1,0:T(8,128)(2,1)} %collective-permute-done.1, f32[128,8]{0,1:T(8,128)S(1)} %get-tuple-element.32, pred[]{:T(512)S(6)} %eq.14), kind=kOutput, calls=%fused_computation.15 | convolution fusion | flops 34340864 | bytes 1314817 | tf_op jit(solution)/shard_map/tha,hab->thb/dot_general | solution.py:144
  32.4 5.1 %collective-permute-done.7 = bf16[8,128,128]{2,1,0:T(8,128)(2,1)S(1)} collective-permute-done((bf16[8,128,128]{2,1,0:T(8,128)(2,1)S(1)}, bf16[8,128,128]{2,1,0:T(8,128)(2,1)S(1)}, u32[]{:S(2)}, u32[]{:S(2)}) %collective-permute-start.7) | collective-permute-done | bytes 262176 | tf_op jit(solution)/shard_map/ppermute | solution.py:14
  37.7 4.2 %collective-permute-start.8 = (bf16[8,128,128]{2,1,0:T(8,128)(2,1)S(1)}, bf16[8,128,128]{2,1,0:T(8,128)(2,1)S(1)}, u32[]{:S(2)}, u32[]{:S(2)}) collective-permute-start(bf16[8,128,128]{2,1,0:T(8,128)(2,1)S(1)} %add_convert_fusion), channel_id=1, source_target_pairs={{0,16},{2,18},{4,20},{6,22},{8,24},{10,26},{12,28},{14,30},{1,17},... | collective-permute-start | bytes 786440 | tf_op jit(solution)/shard_map/ppermute | solution.py:19
  41.9 1.2 collective-permute-done.4
  44.0 7.4 %collective-permute-done.8 = bf16[8,128,128]{2,1,0:T(8,128)(2,1)S(1)} collective-permute-done((bf16[8,128,128]{2,1,0:T(8,128)(2,1)S(1)}, bf16[8,128,128]{2,1,0:T(8,128)(2,1)S(1)}, u32[]{:S(2)}, u32[]{:S(2)}) %collective-permute-start.8) | collective-permute-done | bytes 262176 | tf_op jit(solution)/shard_map/ppermute | solution.py:19
  51.5 1.3 %collective-permute-start.9 = (bf16[8,128,128]{2,1,0:T(8,128)(2,1)S(1)}, bf16[8,128,128]{2,1,0:T(8,128)(2,1)S(1)}, u32[]{:S(2)}, u32[]{:S(2)}) collective-permute-start(bf16[8,128,128]{2,1,0:T(8,128)(2,1)S(1)} %collective-permute-done.8), channel_id=1, source_target_pairs={{0,4},{2,6},{4,0},{6,2},{8,12},{10,14},{12,8},{14,10},{16,20},{18,... | collective-permute-start | bytes 786440 | tf_op jit(solution)/shard_map/ppermute | solution.py:14
  53.4 3.2 %collective-permute-start.13 = (bf16[128,1024]{0,1:T(8,128)(2,1)S(1)}, bf16[128,1024]{0,1:T(8,128)(2,1)S(1)}, u32[]{:S(2)}, u32[]{:S(2)}) collective-permute-start(bf16[128,1024]{0,1:T(8,128)(2,1)S(1)} %bitcast.134), channel_id=1, source_target_pairs={{0,16},{2,18},{4,20},{6,22},{8,24},{10,26},{12,28},{14,30},{16,0},... | collective-permute-start | bytes 786440 | tf_op jit(solution)/shard_map/ppermute | solution.py:14
  57.1 3.2 %collective-permute-start.12 = (bf16[128,1024]{0,1:T(8,128)(2,1)S(1)}, bf16[128,1024]{0,1:T(8,128)(2,1)S(1)}, u32[]{:S(2)}, u32[]{:S(2)}) collective-permute-start(bf16[128,1024]{0,1:T(8,128)(2,1)S(1)} %bitcast.137), channel_id=1, source_target_pairs={{0,16},{2,18},{4,20},{6,22},{8,24},{10,26},{12,28},{14,30},{16,0},... | collective-permute-start | bytes 786440 | tf_op jit(solution)/shard_map/ppermute | solution.py:14
  60.2 1.2 collective-permute-start.19
  61.4 1.5 %collective-permute-start.10 = (bf16[128,1024]{0,1:T(8,128)(2,1)S(1)}, bf16[128,1024]{0,1:T(8,128)(2,1)S(1)}, u32[]{:S(2)}, u32[]{:S(2)}) collective-permute-start(bf16[128,1024]{0,1:T(8,128)(2,1)S(1)} %bitcast.135), channel_id=1, source_target_pairs={{0,4},{2,6},{4,0},{6,2},{8,12},{10,14},{12,8},{14,10},{16,20},{18,... | collective-permute-start | bytes 786440 | tf_op jit(solution)/shard_map/ppermute | solution.py:14
  63.1 5.0 %collective-permute-done.13 = bf16[128,1024]{0,1:T(8,128)(2,1)S(1)} collective-permute-done((bf16[128,1024]{0,1:T(8,128)(2,1)S(1)}, bf16[128,1024]{0,1:T(8,128)(2,1)S(1)}, u32[]{:S(2)}, u32[]{:S(2)}) %collective-permute-start.13) | collective-permute-done | bytes 262176 | tf_op jit(solution)/shard_map/ppermute | solution.py:14
  68.9 2.0 %collective-permute-done.12 = bf16[128,1024]{0,1:T(8,128)(2,1)S(1)} collective-permute-done((bf16[128,1024]{0,1:T(8,128)(2,1)S(1)}, bf16[128,1024]{0,1:T(8,128)(2,1)S(1)}, u32[]{:S(2)}, u32[]{:S(2)}) %collective-permute-start.12) | collective-permute-done | bytes 262176 | tf_op jit(solution)/shard_map/ppermute | solution.py:14
  71.8 1.3 %collective-permute-start.17 = (bf16[2048,256]{1,0:T(8,128)(2,1)}, bf16[2048,256]{1,0:T(8,128)(2,1)S(1)}, u32[]{:S(2)}, u32[]{:S(2)}) collective-permute-start(bf16[2048,256]{1,0:T(8,128)(2,1)} %collective-permute-done.16), channel_id=1, source_target_pairs={{0,2},{2,0},{4,6},{6,4},{8,10},{10,8},{12,14},{14,12},{16,18},{18,... | collective-permute-start | bytes 3145736 | tf_op jit(solution)/shard_map/ppermute | solution.py:14
  73.2 2.1 %collective-permute-done.14 = bf16[128,1024]{0,1:T(8,128)(2,1)S(1)} collective-permute-done((bf16[128,1024]{0,1:T(8,128)(2,1)S(1)}, bf16[128,1024]{0,1:T(8,128)(2,1)S(1)}, u32[]{:S(2)}, u32[]{:S(2)}) %collective-permute-start.14) | collective-permute-done | bytes 262176 | tf_op jit(solution)/shard_map/ppermute | solution.py:14
  75.3 2.6 %collective-permute-done.15 = bf16[128,1024]{0,1:T(8,128)(2,1)S(1)} collective-permute-done((bf16[128,1024]{0,1:T(8,128)(2,1)S(1)}, bf16[128,1024]{0,1:T(8,128)(2,1)S(1)}, u32[]{:S(2)}, u32[]{:S(2)}) %collective-permute-start.15) | collective-permute-done | bytes 262176 | tf_op jit(solution)/shard_map/ppermute | solution.py:14
  79.1 19.4 %collective-permute-start.20 = (bf16[256,256]{0,1:T(8,128)(2,1)S(1)}, bf16[256,256]{0,1:T(8,128)(2,1)S(1)}, u32[]{:S(2)}, u32[]{:S(2)}) collective-permute-start(bf16[256,256]{0,1:T(8,128)(2,1)S(1)} %select_convert_fusion.6), channel_id=1, source_target_pairs={{0,1},{1,0},{2,3},{3,2},{4,5},{5,4},{6,7},{7,6},{8,9},{9,8},{10,11... | collective-permute-start | bytes 393224 | tf_op jit(solution)/shard_map/ppermute | solution.py:23
  98.5 2.0 %fusion.67 = f32[512,256]{0,1:T(8,128)S(1)} fusion(bf16[512,2048]{0,1:T(8,128)(2,1)S(1)} %pad_maximum_fusion, bf16[2048,256]{1,0:T(8,128)(2,1)} %collective-permute-done.16), kind=kOutput, calls=%fused_computation.135 | convolution fusion | flops 536870912 | bytes 3670016 | tf_op jit(solution)/shard_map/dot_general | solution.py:174
  100.7 2.0 %fusion.68 = f32[512,256]{0,1:T(8,128)S(1)} fusion(bf16[512,2048]{0,1:T(8,128)(2,1)S(1)} %pad_maximum_fusion, bf16[2048,256]{1,0:T(8,128)(2,1)} %param.11), kind=kOutput, calls=%fused_computation.136 | convolution fusion | flops 536870912 | bytes 3670016 | tf_op jit(solution)/shard_map/dot_general | solution.py:174
  104.0 5.7 %collective-permute-start.18 = (bf16[256,256]{0,1:T(8,128)(2,1)S(1)}, bf16[256,256]{0,1:T(8,128)(2,1)S(1)}, u32[]{:S(2)}, u32[]{:S(2)}) collective-permute-start(bf16[256,256]{0,1:T(8,128)(2,1)S(1)} %select_convert_fusion.7), channel_id=1, source_target_pairs={{0,1},{1,0},{2,3},{3,2},{4,5},{5,4},{6,7},{7,6},{8,9},{9,8},{10,11... | collective-permute-start | bytes 393224 | tf_op jit(solution)/shard_map/ppermute | solution.py:23
  111.1 3.5 %collective-permute-start.23 = (bf16[128,1024]{0,1:T(8,128)(2,1)S(1)}, bf16[128,1024]{0,1:T(8,128)(2,1)S(1)}, u32[]{:S(2)}, u32[]{:S(2)}) collective-permute-start(bf16[128,1024]{0,1:T(8,128)(2,1)S(1)} %get-tuple-element.12), channel_id=1, source_target_pairs={{0,4},{1,20},{2,6},{3,22},{4,0},{5,16},{6,2},{7,18},{8,12},{9,28},... | collective-permute-start | bytes 786440 | tf_op jit(solution)/shard_map/ppermute | solution.py:32
  114.6 2.2 %collective-permute-start.24 = (bf16[128,1024]{0,1:T(8,128)(2,1)S(1)}, bf16[128,1024]{0,1:T(8,128)(2,1)S(1)}, u32[]{:S(2)}, u32[]{:S(2)}) collective-permute-start(bf16[128,1024]{0,1:T(8,128)(2,1)S(1)} %get-tuple-element.13), channel_id=1, source_target_pairs={{0,0},{1,16},{2,2},{3,18},{4,4},{5,20},{6,6},{7,22},{8,8},{9,24},{... | collective-permute-start | bytes 786440 | tf_op jit(solution)/shard_map/ppermute | solution.py:32
  116.9 1.4 %collective-permute-done.23 = bf16[128,1024]{0,1:T(8,128)(2,1)S(1)} collective-permute-done((bf16[128,1024]{0,1:T(8,128)(2,1)S(1)}, bf16[128,1024]{0,1:T(8,128)(2,1)S(1)}, u32[]{:S(2)}, u32[]{:S(2)}) %collective-permute-start.23) | collective-permute-done | bytes 262176 | tf_op jit(solution)/shard_map/ppermute | solution.py:32
  118.3 4.3 %collective-permute-done.24 = bf16[128,1024]{0,1:T(8,128)(2,1)S(1)} collective-permute-done((bf16[128,1024]{0,1:T(8,128)(2,1)S(1)}, bf16[128,1024]{0,1:T(8,128)(2,1)S(1)}, u32[]{:S(2)}, u32[]{:S(2)}) %collective-permute-start.24) | collective-permute-done | bytes 262176 | tf_op jit(solution)/shard_map/ppermute | solution.py:32
  (78 shorter events, 18.1 us)
Async XLA Ops:
  0.0 8.8 %copy-start = (f32[16,16]{1,0:T(8,128)S(1)}, f32[16,16]{1,0:T(8,128)}, u32[]{:S(2)}) copy-start(f32[16,16]{1,0:T(8,128)} %param.10) | copy-start | bytes 3076
  3.3 5.5 %copy-start.3 = (s32[128,8]{0,1:T(8,128)S(1)}, s32[128,8]{0,1:T(8,128)}, u32[]{:S(2)}) copy-start(s32[128,8]{0,1:T(8,128)} %param.9) | copy-start | bytes 12292
  4.5 18.0 %collective-permute-start.2 = (bf16[8,128,128]{2,1,0:T(8,128)(2,1)}, bf16[8,128,128]{2,1,0:T(8,128)(2,1)S(1)}, u32[]{:S(2)}, u32[]{:S(2)}) collective-permute-start(bf16[8,128,128]{2,1,0:T(8,128)(2,1)} %get-tuple-element.39), channel_id=1, source_target_pairs={{0,2},{2,0},{4,6},{6,4},{8,10},{10,8},{12,14},{14,12},{16,18},{18,... | collective-permute-start | bytes 786440 | tf_op jit(solution)/shard_map/ppermute | solution.py:14
  5.7 19.5 %collective-permute-start.1 = (bf16[8,128,128]{2,1,0:T(8,128)(2,1)}, bf16[8,128,128]{2,1,0:T(8,128)(2,1)}, u32[]{:S(2)}, u32[]{:S(2)}) collective-permute-start(bf16[8,128,128]{2,1,0:T(8,128)(2,1)} %get-tuple-element.39), channel_id=1, source_target_pairs={{0,4},{2,6},{4,0},{6,2},{8,12},{10,14},{12,8},{14,10},{16,20},{18,... | collective-permute-start | bytes 786440 | tf_op jit(solution)/shard_map/ppermute | solution.py:14
  8.3 10.2 %collective-permute-start.5 = (bf16[8,128,128]{2,1,0:T(8,128)(2,1)}, bf16[8,128,128]{2,1,0:T(8,128)(2,1)S(1)}, u32[]{:S(2)}, u32[]{:S(2)}) collective-permute-start(bf16[8,128,128]{2,1,0:T(8,128)(2,1)} %get-tuple-element.37), channel_id=1, source_target_pairs={{0,4},{2,6},{4,0},{6,2},{8,12},{10,14},{12,8},{14,10},{16,20},{18,... | collective-permute-start | bytes 786440 | tf_op jit(solution)/shard_map/ppermute | solution.py:14
  8.5 16.7 %collective-permute-start = (bf16[8,128,128]{2,1,0:T(8,128)(2,1)}, bf16[8,128,128]{2,1,0:T(8,128)(2,1)S(1)}, u32[]{:S(2)}, u32[]{:S(2)}) collective-permute-start(bf16[8,128,128]{2,1,0:T(8,128)(2,1)} %get-tuple-element.37), channel_id=1, source_target_pairs={{0,2},{2,0},{4,6},{6,4},{8,10},{10,8},{12,14},{14,12},{16,18},{18,... | collective-permute-start | bytes 786440 | tf_op jit(solution)/shard_map/ppermute | solution.py:14
  8.8 54.2 %collective-permute-start.16 = (bf16[2048,256]{1,0:T(8,128)(2,1)}, bf16[2048,256]{1,0:T(8,128)(2,1)}, u32[]{:S(2)}, u32[]{:S(2)}) collective-permute-start(bf16[2048,256]{1,0:T(8,128)(2,1)} %param.11), channel_id=1, source_target_pairs={{0,8},{2,10},{4,12},{6,14},{8,0},{10,2},{12,4},{14,6},{16,24},{18,... | collective-permute-start | bytes 3145736 | tf_op jit(solution)/shard_map/ppermute | solution.py:14
  18.5 6.3 %collective-permute-start.6 = (bf16[8,128,128]{2,1,0:T(8,128)(2,1)S(1)}, bf16[8,128,128]{2,1,0:T(8,128)(2,1)S(1)}, u32[]{:S(2)}, u32[]{:S(2)}) collective-permute-start(bf16[8,128,128]{2,1,0:T(8,128)(2,1)S(1)} %collective-permute-done.5), channel_id=1, source_target_pairs={{0,2},{2,0},{4,6},{6,4},{8,10},{10,8},{12,14},{14,12},{16,18},{18,... | collective-permute-start | bytes 786440 | tf_op jit(solution)/shard_map/ppermute | solution.py:14
  22.5 6.0 %collective-permute-start.3 = (bf16[8,128,128]{2,1,0:T(8,128)(2,1)S(1)}, bf16[8,128,128]{2,1,0:T(8,128)(2,1)S(1)}, u32[]{:S(2)}, u32[]{:S(2)}) collective-permute-start(bf16[8,128,128]{2,1,0:T(8,128)(2,1)S(1)} %collective-permute-done.2), channel_id=1, source_target_pairs={{0,4},{2,6},{4,0},{6,2},{8,12},{10,14},{12,8},{14,10},{16,20},{18,... | collective-permute-start | bytes 786440 | tf_op jit(solution)/shard_map/ppermute | solution.py:14
  24.9 12.6 %collective-permute-start.7 = (bf16[8,128,128]{2,1,0:T(8,128)(2,1)S(1)}, bf16[8,128,128]{2,1,0:T(8,128)(2,1)S(1)}, u32[]{:S(2)}, u32[]{:S(2)}) collective-permute-start(bf16[8,128,128]{2,1,0:T(8,128)(2,1)S(1)} %fusion.40), channel_id=1, source_target_pairs={{0,8},{2,10},{4,12},{6,14},{8,0},{10,2},{12,4},{14,6},{16,24},{18,... | collective-permute-start | bytes 786440 | tf_op jit(solution)/shard_map/ppermute | solution.py:14
  29.5 13.6 %collective-permute-start.4 = (bf16[8,128,128]{2,1,0:T(8,128)(2,1)S(1)}, bf16[8,128,128]{2,1,0:T(8,128)(2,1)S(1)}, u32[]{:S(2)}, u32[]{:S(2)}) collective-permute-start(bf16[8,128,128]{2,1,0:T(8,128)(2,1)S(1)} %add_convert_fusion.1), channel_id=1, source_target_pairs={{0,8},{2,10},{4,12},{6,14},{16,24},{18,26},{20,28},{22,30},{1,9},{... | collective-permute-start | bytes 786440 | tf_op jit(solution)/shard_map/ppermute | solution.py:19
  31.1 12.3 %copy-start.2 = (f32[128,8,128]{0,2,1:T(8,128)S(1)}, f32[128,8,128]{0,2,1:T(8,128)}, u32[]{:S(2)}) copy-start(f32[128,8,128]{0,2,1:T(8,128)} %convolution_bitcast_fusion.9) | copy-start | bytes 1572868
  37.7 13.8 %collective-permute-start.8 = (bf16[8,128,128]{2,1,0:T(8,128)(2,1)S(1)}, bf16[8,128,128]{2,1,0:T(8,128)(2,1)S(1)}, u32[]{:S(2)}, u32[]{:S(2)}) collective-permute-start(bf16[8,128,128]{2,1,0:T(8,128)(2,1)S(1)} %add_convert_fusion), channel_id=1, source_target_pairs={{0,16},{2,18},{4,20},{6,22},{8,24},{10,26},{12,28},{14,30},{1,17},... | collective-permute-start | bytes 786440 | tf_op jit(solution)/shard_map/ppermute | solution.py:19
  43.4 9.6 %copy-start.1 = (f32[128,8,128]{0,2,1:T(8,128)S(1)}, f32[128,8,128]{0,2,1:T(8,128)}, u32[]{:S(2)}) copy-start(f32[128,8,128]{0,2,1:T(8,128)} %convolution_bitcast_fusion.4) | copy-start | bytes 1572868
  51.5 5.2 %collective-permute-start.9 = (bf16[8,128,128]{2,1,0:T(8,128)(2,1)S(1)}, bf16[8,128,128]{2,1,0:T(8,128)(2,1)S(1)}, u32[]{:S(2)}, u32[]{:S(2)}) collective-permute-start(bf16[8,128,128]{2,1,0:T(8,128)(2,1)S(1)} %collective-permute-done.8), channel_id=1, source_target_pairs={{0,4},{2,6},{4,0},{6,2},{8,12},{10,14},{12,8},{14,10},{16,20},{18,... | collective-permute-start | bytes 786440 | tf_op jit(solution)/shard_map/ppermute | solution.py:14
  53.4 14.7 %collective-permute-start.13 = (bf16[128,1024]{0,1:T(8,128)(2,1)S(1)}, bf16[128,1024]{0,1:T(8,128)(2,1)S(1)}, u32[]{:S(2)}, u32[]{:S(2)}) collective-permute-start(bf16[128,1024]{0,1:T(8,128)(2,1)S(1)} %bitcast.134), channel_id=1, source_target_pairs={{0,16},{2,18},{4,20},{6,22},{8,24},{10,26},{12,28},{14,30},{16,0},... | collective-permute-start | bytes 786440 | tf_op jit(solution)/shard_map/ppermute | solution.py:14
  57.1 13.8 %collective-permute-start.12 = (bf16[128,1024]{0,1:T(8,128)(2,1)S(1)}, bf16[128,1024]{0,1:T(8,128)(2,1)S(1)}, u32[]{:S(2)}, u32[]{:S(2)}) collective-permute-start(bf16[128,1024]{0,1:T(8,128)(2,1)S(1)} %bitcast.137), channel_id=1, source_target_pairs={{0,16},{2,18},{4,20},{6,22},{8,24},{10,26},{12,28},{14,30},{16,0},... | collective-permute-start | bytes 786440 | tf_op jit(solution)/shard_map/ppermute | solution.py:14
  60.2 18.1 %collective-permute-start.19 = (bf16[2048,256]{1,0:T(8,128)(2,1)}, bf16[2048,256]{1,0:T(8,128)(2,1)S(1)}, u32[]{:S(2)}, u32[]{:S(2)}) collective-permute-start(bf16[2048,256]{1,0:T(8,128)(2,1)} %param.11), channel_id=1, source_target_pairs={{0,2},{2,0},{4,6},{6,4},{8,10},{10,8},{12,14},{14,12},{16,18},{18,... | collective-permute-start | bytes 3145736 | tf_op jit(solution)/shard_map/ppermute | solution.py:14
  61.4 10.4 %collective-permute-start.10 = (bf16[128,1024]{0,1:T(8,128)(2,1)S(1)}, bf16[128,1024]{0,1:T(8,128)(2,1)S(1)}, u32[]{:S(2)}, u32[]{:S(2)}) collective-permute-start(bf16[128,1024]{0,1:T(8,128)(2,1)S(1)} %bitcast.135), channel_id=1, source_target_pairs={{0,4},{2,6},{4,0},{6,2},{8,12},{10,14},{12,8},{14,10},{16,20},{18,... | collective-permute-start | bytes 786440 | tf_op jit(solution)/shard_map/ppermute | solution.py:14
  62.9 10.2 %collective-permute-start.11 = (bf16[128,1024]{0,1:T(8,128)(2,1)S(1)}, bf16[128,1024]{0,1:T(8,128)(2,1)S(1)}, u32[]{:S(2)}, u32[]{:S(2)}) collective-permute-start(bf16[128,1024]{0,1:T(8,128)(2,1)S(1)} %bitcast.138), channel_id=1, source_target_pairs={{0,4},{2,6},{4,0},{6,2},{8,12},{10,14},{12,8},{14,10},{16,20},{18,... | collective-permute-start | bytes 786440 | tf_op jit(solution)/shard_map/ppermute | solution.py:14
  68.1 7.2 %collective-permute-start.14 = (bf16[128,1024]{0,1:T(8,128)(2,1)S(1)}, bf16[128,1024]{0,1:T(8,128)(2,1)S(1)}, u32[]{:S(2)}, u32[]{:S(2)}) collective-permute-start(bf16[128,1024]{0,1:T(8,128)(2,1)S(1)} %collective-permute-done.13), channel_id=1, source_target_pairs={{0,4},{2,6},{4,0},{6,2},{8,12},{10,14},{12,8},{14,10},{16,20},{18,... | collective-permute-start | bytes 786440 | tf_op jit(solution)/shard_map/ppermute | solution.py:14
  70.9 7.0 %collective-permute-start.15 = (bf16[128,1024]{0,1:T(8,128)(2,1)S(1)}, bf16[128,1024]{0,1:T(8,128)(2,1)S(1)}, u32[]{:S(2)}, u32[]{:S(2)}) collective-permute-start(bf16[128,1024]{0,1:T(8,128)(2,1)S(1)} %collective-permute-done.12), channel_id=1, source_target_pairs={{0,4},{2,6},{4,0},{6,2},{8,12},{10,14},{12,8},{14,10},{16,20},{18,... | collective-permute-start | bytes 786440 | tf_op jit(solution)/shard_map/ppermute | solution.py:14
  71.8 31.4 %collective-permute-start.17 = (bf16[2048,256]{1,0:T(8,128)(2,1)}, bf16[2048,256]{1,0:T(8,128)(2,1)S(1)}, u32[]{:S(2)}, u32[]{:S(2)}) collective-permute-start(bf16[2048,256]{1,0:T(8,128)(2,1)} %collective-permute-done.16), channel_id=1, source_target_pairs={{0,2},{2,0},{4,6},{6,4},{8,10},{10,8},{12,14},{14,12},{16,18},{18,... | collective-permute-start | bytes 3145736 | tf_op jit(solution)/shard_map/ppermute | solution.py:14
  79.1 30.6 %collective-permute-start.20 = (bf16[256,256]{0,1:T(8,128)(2,1)S(1)}, bf16[256,256]{0,1:T(8,128)(2,1)S(1)}, u32[]{:S(2)}, u32[]{:S(2)}) collective-permute-start(bf16[256,256]{0,1:T(8,128)(2,1)S(1)} %select_convert_fusion.6), channel_id=1, source_target_pairs={{0,1},{1,0},{2,3},{3,2},{4,5},{5,4},{6,7},{7,6},{8,9},{9,8},{10,11... | collective-permute-start | bytes 393224 | tf_op jit(solution)/shard_map/ppermute | solution.py:23
  100.6 9.2 %collective-permute-start.21 = (bf16[256,256]{0,1:T(8,128)(2,1)S(1)}, bf16[256,256]{0,1:T(8,128)(2,1)S(1)}, u32[]{:S(2)}, u32[]{:S(2)}) collective-permute-start(bf16[256,256]{0,1:T(8,128)(2,1)S(1)} %select_convert_fusion.5), channel_id=1, source_target_pairs={{0,1},{1,0},{2,3},{3,2},{4,5},{5,4},{6,7},{7,6},{8,9},{9,8},{10,11... | collective-permute-start | bytes 393224 | tf_op jit(solution)/shard_map/ppermute | solution.py:23
  102.7 7.1 %collective-permute-start.22 = (bf16[256,256]{0,1:T(8,128)(2,1)S(1)}, bf16[256,256]{0,1:T(8,128)(2,1)S(1)}, u32[]{:S(2)}, u32[]{:S(2)}) collective-permute-start(bf16[256,256]{0,1:T(8,128)(2,1)S(1)} %select_convert_fusion.4), channel_id=1, source_target_pairs={{0,1},{1,0},{2,3},{3,2},{4,5},{5,4},{6,7},{7,6},{8,9},{9,8},{10,11... | collective-permute-start | bytes 393224 | tf_op jit(solution)/shard_map/ppermute | solution.py:23
  104.0 6.7 %collective-permute-start.18 = (bf16[256,256]{0,1:T(8,128)(2,1)S(1)}, bf16[256,256]{0,1:T(8,128)(2,1)S(1)}, u32[]{:S(2)}, u32[]{:S(2)}) collective-permute-start(bf16[256,256]{0,1:T(8,128)(2,1)S(1)} %select_convert_fusion.7), channel_id=1, source_target_pairs={{0,1},{1,0},{2,3},{3,2},{4,5},{5,4},{6,7},{7,6},{8,9},{9,8},{10,11... | collective-permute-start | bytes 393224 | tf_op jit(solution)/shard_map/ppermute | solution.py:23
  111.1 7.2 %collective-permute-start.23 = (bf16[128,1024]{0,1:T(8,128)(2,1)S(1)}, bf16[128,1024]{0,1:T(8,128)(2,1)S(1)}, u32[]{:S(2)}, u32[]{:S(2)}) collective-permute-start(bf16[128,1024]{0,1:T(8,128)(2,1)S(1)} %get-tuple-element.12), channel_id=1, source_target_pairs={{0,4},{1,20},{2,6},{3,22},{4,0},{5,16},{6,2},{7,18},{8,12},{9,28},... | collective-permute-start | bytes 786440 | tf_op jit(solution)/shard_map/ppermute | solution.py:32
  114.6 8.0 %collective-permute-start.24 = (bf16[128,1024]{0,1:T(8,128)(2,1)S(1)}, bf16[128,1024]{0,1:T(8,128)(2,1)S(1)}, u32[]{:S(2)}, u32[]{:S(2)}) collective-permute-start(bf16[128,1024]{0,1:T(8,128)(2,1)S(1)} %get-tuple-element.13), channel_id=1, source_target_pairs={{0,0},{1,16},{2,2},{3,18},{4,4},{5,20},{6,6},{7,22},{8,8},{9,24},{... | collective-permute-start | bytes 786440 | tf_op jit(solution)/shard_map/ppermute | solution.py:32
where the time goes:
time: 124 us
  starting transfers between devices  54.8 us (44%)
  waiting for transfers between devices  45.9 us (37%)
  matrix products  13.6 us (11%)
  local copies, waits for them, and re-layouts  6.15 us (5%)
  other arithmetic  2.87 us (2%)
    ppermute x17, waiting for transfers between devices, swap(): return lax.ppermute(value, 'seq', pairs)  30.5 us
    ppermute x4, starting transfers between devices, swap_cores(): return lax.ppermute(value, 'head', [(0, 1), (1, 0)])  25.8 us
    ppermute x17, starting transfers between devices, swap(): return lax.ppermute(value, 'seq', pairs)  17.8 us
    ppermute x2, waiting for transfers between devices, lift(): return lax.ppermute(value, 'seq', pairs)  8.64 us
    ppermute x2, waiting for transfers between devices, send_home(): return lax.ppermute(value, ('seq', 'head'), pairs)  5.78 us
    ppermute x2, starting transfers between devices, send_home(): return lax.ppermute(value, ('seq', 'head'), pairs)  5.72 us
    ppermute x2, starting transfers between devices, lift(): return lax.ppermute(value, 'seq', pairs)  5.51 us
    dot_general x4, matrix products, shards(): part = jnp.dot(tokens, weights_of[mask], preferred_element_type=jnp.float32)  5.47 us
  transfers between devices with their start and end apart: 25, of which 14 were waited for; matrix products, arithmetic and copies ran while one was open for 13% of the time, Pallas kernels for 0%

commit v1 on v0

v1 whole, which is shorter than its diff:
```python
import math

import jax
import jax.numpy as jnp
from jax import lax
from jax.sharding import PartitionSpec as P

DH = 128
VALS = 16


def swap(value, mask):
    pairs = [(source, source ^ mask) for source in range(lax.axis_size("seq"))]
    return lax.ppermute(value, "seq", pairs)


def lift(value, clear, need, mask):
    pairs = [
        (source, source ^ mask)
        for source in range(lax.axis_size("seq"))
        if not source & clear and source & need == need
    ]
    return lax.ppermute(value, "seq", pairs)


def swap_cores(value):
    return lax.ppermute(value, "head", [(0, 1), (1, 0)])


def masks_of(bits):
    out = [0]
    for bit in bits:
        out = out + [mask | 1 << bit for mask in out]
    return out


def absolute(pieces, bits, position):
    for bit in bits:
        flag = position >> bit & 1 == 1
        pieces = {mask: jnp.where(flag, pieces[mask ^ 1 << bit], piece) for mask, piece in pieces.items()}
    return pieces


def groups(depth):
    top = depth - 1
    token_bits = [1, top - 1] if depth < 6 else [1, 2, top - 1]
    column_bits = [bit for bit in range(top) if bit not in token_bits][::-1]
    return token_bits, column_bits


def level_states(state, position, depth):
    top = depth - 1
    wide = lambda value: value.astype(jnp.float32)
    set_at = lambda level: position >> level & 1 == 1
    none = jnp.bfloat16(0)
    own = [part.astype(jnp.bfloat16) for part in state]
    near, side, corner = [None, None], [None, None], [None, None]
    side[0] = swap(own[1], 2)
    near[0] = swap(own[0], 1)
    side[1] = swap(own[0], 2)
    corner[0] = swap(side[0], 1)
    near[1] = swap(own[1], 1)
    corner[1] = swap(near[0], 2)
    read = []
    for part in range(2):
        pair = wide(side[part]) + wide(corner[part])
        block = state[part] + wide(near[part]) + pair
        mine = [
            jnp.where(set_at(0), near[part], none),
            jnp.where(set_at(1), pair, 0.0).astype(jnp.bfloat16),
        ]
        for level in range(2, top):
            sent = block.astype(jnp.bfloat16)
            if level == top - 1 and part == 0:
                other = lift(sent, 1 << level | 1 << top, 0, 1 << level)
                upper = lift(sent, 1 << level, 1 << top, 1 << level)
                mine.append(other + upper)
            elif level == top - 1:
                other = lift(sent, 1 << level, 0, 1 << level)
                mine.append(other)
            else:
                other = swap(sent, 1 << level)
                mine.append(jnp.where(set_at(level), other, none))
            block = block + wide(other)
        if part == 0:
            sent = block.astype(jnp.bfloat16)
            below = 1 << top - 1
            far = lift(sent, 1 << top, below, 1 << top)
            close = lift(sent, 1 << top, below, 1 << top | below)
            last = far + close
            mine.append(last)
        else:
            mine.append(swap(last, 2))
        read.append(mine)
    return read


def shards(queries, keys, values, level_index, level_table, out_weight):
    rows = queries.shape[0]
    heads_here = level_table.shape[0]
    half = heads_here // 2
    position = lax.axis_index("seq")
    core = lax.axis_index("head")
    depth = lax.axis_size("seq").bit_length() - 1
    top = depth - 1
    token_bits, column_bits = groups(depth)

    flip = position >> 1 & 1
    starts = [flip * half, (1 - flip) * half]

    def halves(value):
        return [
            lax.dynamic_slice_in_dim(value, start * DH, half * DH, 1).reshape(rows, half, DH)
            for start in starts
        ]

    query_heads, key_heads, value_heads = halves(queries), halves(keys), halves(values)
    state = [
        jnp.einsum("tha,thb->hab", key, value, preferred_element_type=jnp.float32)
        for key, value in zip(key_heads, value_heads)
    ]
    ordered = jnp.concatenate(
        [lax.dynamic_slice_in_dim(out_weight, start * DH, half * DH, 0) for start in starts], axis=0
    )
    split = ordered.shape[0] * 5 // 8
    parts = (ordered[:split], ordered[split:])
    weights_of = {1 << top: tuple(swap(part, 1 << top) for part in parts)}
    weights_of[0] = parts
    for bit in column_bits:
        for mask in list(weights_of):
            new = mask | 1 << bit
            weights_of[new] = tuple(swap(part, 1 << bit) for part in weights_of[mask])
    read = level_states(state, position, depth)

    onehot = (level_index[:, :, None] == jnp.arange(VALS, dtype=jnp.int32)[None, None, :]).astype(
        jnp.float32
    )
    level_weight = jnp.einsum("tlv,hv->tlh", onehot, level_table, precision=lax.Precision.HIGHEST)
    inv_root = 1.0 / math.sqrt(DH)
    causal = jnp.arange(rows)[:, None] >= jnp.arange(rows)[None, :]
    normed = []
    for part in range(2):
        lam = lax.dynamic_slice_in_dim(level_weight, starts[part], half, 2)
        scores = jnp.einsum(
            "tha,sha->hts", query_heads[part], key_heads[part], preferred_element_type=jnp.float32
        )
        factor = jnp.transpose(lam[:, 0, :]) * (inv_root / math.sqrt(rows))
        weights = jnp.where(causal[None], scores * factor[:, :, None], 0.0).astype(jnp.bfloat16)
        total = jnp.einsum("hts,shb->thb", weights, value_heads[part], preferred_element_type=jnp.float32)
        for level in range(depth):
            reads = jnp.einsum("tha,hab->thb", query_heads[part], read[part][level], preferred_element_type=jnp.float32)
            scale = lam[:, level + 1, :] * (inv_root / math.sqrt(rows * 2**level))
            total = total + reads * scale[:, :, None]
        square = jnp.mean(total * total, axis=-1, keepdims=True)
        normed.append((total * lax.rsqrt(square + 1e-06)).astype(jnp.bfloat16).reshape(rows, half * DH))

    pieces = {0: tuple(normed)}
    for mask in masks_of(token_bits)[1:]:
        bits = [bit for bit in token_bits if mask >> bit & 1]
        got = []
        for part in range(2):
            bit = bits[0] if part else bits[-1]
            source = 1 - part if bit == 1 else part
            got.append(swap(pieces[mask ^ 1 << bit][source], 1 << bit))
        pieces[mask] = tuple(got)
    token_masks = sorted(pieces)
    tokens = jnp.concatenate(
        [jnp.concatenate([pieces[mask][part] for part in range(2)], axis=1) for mask in token_masks],
        axis=0,
    )
    mine = (position >> top & 1) == core

    def product(mask):
        first, second = weights_of[mask]
        return jnp.dot(tokens[:, :split], first, preferred_element_type=jnp.float32) + jnp.dot(
            tokens[:, split:], second, preferred_element_type=jnp.float32
        )

    landed = {}
    for mask in masks_of(column_bits):
        near_half, far_half = lax.optimization_barrier((product(mask), product(mask | 1 << top)))
        keep = jnp.where(mine, near_half, far_half)
        give = jnp.where(mine, far_half, near_half).astype(jnp.bfloat16)
        summed = (keep + swap_cores(give).astype(jnp.float32)).astype(jnp.bfloat16)
        for at, token_mask in enumerate(token_masks):
            piece = summed[at * rows : (at + 1) * rows]
            whole = mask | token_mask
            landed[whole] = swap(piece, token_mask) if token_mask else piece
    landed = absolute(landed, token_bits + column_bits, position)
    return jnp.concatenate([landed[mask] for mask in sorted(landed)], axis=1)


def solution(mesh):
    placed = (
        P("seq", "head"),
        P("seq", "head"),
        P("seq", "head"),
        P("seq", None),
        P("head", None),
        P("head", "seq"),
    )
    return jax.shard_map(
        shards, mesh=mesh, in_specs=placed, out_specs=P("seq", "head"), check_vma=False
    )
```

time: 124 us -> 151 us (1.22)
  the two profiles are of different devices: /device:TPU:9 before, /device:TPU:0 now
where the time goes in v1:
time: 151 us; the launch traced here: 150 us
  starting transfers between devices  74.1 us (49%)
  waiting for transfers between devices  41.6 us (28%)
  matrix products  14.3 us (9%)
  local copies, waits for them, and re-layouts  9.83 us (7%)
  other arithmetic  9.72 us (6%)
    ppermute x25, starting transfers between devices, swap(): return lax.ppermute(value, 'seq', pairs)  64.8 us
    ppermute x25, waiting for transfers between devices, swap(): return lax.ppermute(value, 'seq', pairs)  32.6 us
    ppermute x5, starting transfers between devices, lift(): return lax.ppermute(value, 'seq', pairs)  9.19 us
    ppermute x5, waiting for transfers between devices, lift(): return lax.ppermute(value, 'seq', pairs)  9.03 us
    concatenate x1, other arithmetic, shards(): jnp.concatenate([jnp.concatenate([pieces[mask][part] for part in range(2)...  4.77 us
    dot_general x4, matrix products, product(): jnp.dot(tokens[:, split:], second, preferred_element_type=jnp.float32)  3.61 us
    dot_general x8, matrix products, shards(): jnp.einsum('tha,hab->thb', query_heads[part], read[part][level], preferre...  3.38 us
    dot_general x4, matrix products, product(): jnp.dot(tokens[:, :split], first, preferred_element_type=jnp.float32)  3.26 us
  transfers between devices with their start and end apart: 32, of which 12 were waited for; matrix products, arithmetic and copies ran while one was open for 19% of the time, Pallas kernels for 0%

profile of v1, /device:TPU:0, one launch (start us, length us, event | category | flops | bytes accessed | tf_op | source)
XLA Modules:
  0.0 150.1 jit_solution(15802399921809327813)
XLA Ops:
  0.0 2.1 %constant_dynamic-slice_fusion.12 = (bf16[128,1024]{1,0:T(8,128)(2,1)}, bf16[128,1024]{1,0:T(8,128)(2,1)}, bf16[128,1024]{1,0:T(8,128)(2,1)S(1)}, bf16[128,1024]{1,0:T(8,128)(2,1)S(1)}) fusion(bf16[128,2048]{1,0:T(8,128)(2,1)} %param.6, s32[]{:T(128)S(6)} %select_n.183, s32[]{:T(128)S(6)} %select_n.177, bf16[128,2048]{1,0:T(8,128)(2,1)} %param.7), kind=kLoop, calls=%fused_computation.117 | loop fusion | bytes 2097160 | tf_op jit(solution)/shard_map/dynamic_slice | solution.py:113
  3.6 3.0 %collective-permute-start.1 = (bf16[8,128,128]{2,1,0:T(8,128)(2,1)}, bf16[8,128,128]{2,1,0:T(8,128)(2,1)S(1)}, u32[]{:S(2)}, u32[]{:S(2)}) collective-permute-start(bf16[8,128,128]{2,1,0:T(8,128)(2,1)} %get-tuple-element.47), channel_id=1, source_target_pairs={{0,4},{2,6},{4,0},{6,2},{8,12},{10,14},{12,8},{14,10},{16,20},{18,... | collective-permute-start | bytes 786440 | tf_op jit(solution)/shard_map/ppermute | solution.py:14
  6.6 1.5 collective-permute-start.7
  10.0 1.8 %constant_dynamic-slice_fusion.3 = bf16[768,256]{1,0:T(8,128)(2,1)} fusion(bf16[2048,256]{1,0:T(8,128)(2,1)} %param.11, s32[]{:T(128)S(6)} %add.140), kind=kLoop, calls=%fused_computation.108 | loop fusion | bytes 786436 | tf_op jit(solution)/shard_map/slice | solution.py:126
  11.8 3.1 %collective-permute-start.22 = (bf16[768,256]{1,0:T(8,128)(2,1)}, bf16[768,256]{1,0:T(8,128)(2,1)}, u32[]{:S(2)}, u32[]{:S(2)}) collective-permute-start(bf16[768,256]{1,0:T(8,128)(2,1)} %constant_dynamic-slice_fusion.3), channel_id=1, source_target_pairs={{0,16},{2,18},{4,20},{6,22},{8,24},{10,26},{12,28},{14,30},{16,0},... | collective-permute-start | bytes 1179656 | tf_op jit(solution)/shard_map/ppermute | solution.py:14
  14.9 2.1 %constant_dynamic-slice_fusion.10 = (bf16[1024,256]{1,0:T(8,128)(2,1)S(1)}, bf16[1024,256]{1,0:T(8,128)(2,1)}) fusion(bf16[2048,256]{1,0:T(8,128)(2,1)} %param.11, s32[]{:T(128)S(6)} %select_n.177, s32[]{:T(128)S(6)} %select_n.183), kind=kLoop, calls=%fused_computation.115 | loop fusion | bytes 2097160 | tf_op jit(solution)/shard_map/dynamic_slice | solution.py:123
  19.6 1.5 %collective-permute-start.2 = (bf16[8,128,128]{2,1,0:T(8,128)(2,1)S(1)}, bf16[8,128,128]{2,1,0:T(8,128)(2,1)S(1)}, u32[]{:S(2)}, u32[]{:S(2)}) collective-permute-start(bf16[8,128,128]{2,1,0:T(8,128)(2,1)S(1)} %collective-permute-done.1), channel_id=1, source_target_pairs={{0,2},{2,0},{4,6},{6,4},{8,10},{10,8},{12,14},{14,12},{16,18},{18,... | collective-permute-start | bytes 786440 | tf_op jit(solution)/shard_map/ppermute | solution.py:14
  21.1 1.8 %pad_maximum_fusion = bf16[1280,256]{1,0:T(8,128)(2,1)} fusion(bf16[1024,256]{1,0:T(8,128)(2,1)} %get-tuple-element.24, bf16[1024,256]{1,0:T(8,128)(2,1)S(1)} %get-tuple-element.23), kind=kLoop, calls=%fused_computation.42 | loop fusion | flops 1310720 | bytes 1703936 | tf_op jit(solution)/shard_map/concatenate | solution.py:122
  26.3 1.5 %collective-permute-start.9 = (bf16[8,128,128]{2,1,0:T(8,128)(2,1)S(1)}, bf16[8,128,128]{2,1,0:T(8,128)(2,1)S(1)}, u32[]{:S(2)}, u32[]{:S(2)}) collective-permute-start(bf16[8,128,128]{2,1,0:T(8,128)(2,1)S(1)} %collective-permute-done), channel_id=1, source_target_pairs={{0,4},{2,6},{4,0},{6,2},{8,12},{10,14},{12,8},{14,10},{16,20},{18,... | collective-permute-start | bytes 786440 | tf_op jit(solution)/shard_map/ppermute | solution.py:14
  27.9 3.5 %collective-permute-start.3 = (bf16[8,128,128]{2,1,0:T(8,128)(2,1)S(1)}, bf16[8,128,128]{2,1,0:T(8,128)(2,1)S(1)}, u32[]{:S(2)}, u32[]{:S(2)}) collective-permute-start(bf16[8,128,128]{2,1,0:T(8,128)(2,1)S(1)} %fusion.42), channel_id=1, source_target_pairs={{0,8},{2,10},{4,12},{6,14},{1,9},{3,11},{5,13},{7,15}} | collective-permute-start | bytes 786440 | tf_op jit(solution)/shard_map/ppermute | solution.py:23
  33.8 3.5 %collective-permute-start.10 = (bf16[8,128,128]{2,1,0:T(8,128)(2,1)S(1)}, bf16[8,128,128]{2,1,0:T(8,128)(2,1)S(1)}, u32[]{:S(2)}, u32[]{:S(2)}) collective-permute-start(bf16[8,128,128]{2,1,0:T(8,128)(2,1)S(1)} %add_convert_fusion.2), channel_id=1, source_target_pairs={{0,8},{2,10},{4,12},{6,14},{16,24},{18,26},{20,28},{22,30},{1,9},{... | collective-permute-start | bytes 786440 | tf_op jit(solution)/shard_map/ppermute | solution.py:23
  38.9 7.0 %collective-permute-done.3 = bf16[8,128,128]{2,1,0:T(8,128)(2,1)S(1)} collective-permute-done((bf16[8,128,128]{2,1,0:T(8,128)(2,1)S(1)}, bf16[8,128,128]{2,1,0:T(8,128)(2,1)S(1)}, u32[]{:S(2)}, u32[]{:S(2)}) %collective-permute-start.3) | collective-permute-done | bytes 262176 | tf_op jit(solution)/shard_map/ppermute | solution.py:23
  46.8 2.0 %collective-permute-done.10 = bf16[8,128,128]{2,1,0:T(8,128)(2,1)S(1)} collective-permute-done((bf16[8,128,128]{2,1,0:T(8,128)(2,1)S(1)}, bf16[8,128,128]{2,1,0:T(8,128)(2,1)S(1)}, u32[]{:S(2)}, u32[]{:S(2)}) %collective-permute-start.10) | collective-permute-done | bytes 262176 | tf_op jit(solution)/shard_map/ppermute | solution.py:23
  50.3 1.6 %collective-permute-start.11 = (bf16[8,128,128]{2,1,0:T(8,128)(2,1)S(1)}, bf16[8,128,128]{2,1,0:T(8,128)(2,1)S(1)}, u32[]{:S(2)}, u32[]{:S(2)}) collective-permute-start(bf16[8,128,128]{2,1,0:T(8,128)(2,1)S(1)} %add.114), channel_id=1, source_target_pairs={{0,4},{2,6},{4,0},{6,2},{8,12},{10,14},{12,8},{14,10},{16,20},{18,... | collective-permute-start | bytes 786440 | tf_op jit(solution)/shard_map/ppermute | solution.py:14
  52.6 27.0 %collective-permute-start.14 = (bf16[128,1024]{0,1:T(8,128)(2,1)S(1)}, bf16[128,1024]{0,1:T(8,128)(2,1)S(1)}, u32[]{:S(2)}, u32[]{:S(2)}) collective-permute-start(bf16[128,1024]{0,1:T(8,128)(2,1)S(1)} %bitcast.138), channel_id=1, source_target_pairs={{0,8},{2,10},{4,12},{6,14},{8,0},{10,2},{12,4},{14,6},{16,24},{18,... | collective-permute-start | bytes 786440 | tf_op jit(solution)/shard_map/ppermute | solution.py:14
  80.8 1.6 %collective-permute-start.13 = (bf16[128,1024]{0,1:T(8,128)(2,1)S(1)}, bf16[128,1024]{0,1:T(8,128)(2,1)S(1)}, u32[]{:S(2)}, u32[]{:S(2)}) collective-permute-start(bf16[128,1024]{0,1:T(8,128)(2,1)S(1)} %bitcast.139), channel_id=1, source_target_pairs={{0,4},{2,6},{4,0},{6,2},{8,12},{10,14},{12,8},{14,10},{16,20},{18,... | collective-permute-start | bytes 786440 | tf_op jit(solution)/shard_map/ppermute | solution.py:14
  82.4 1.5 %collective-permute-done.14 = bf16[128,1024]{0,1:T(8,128)(2,1)S(1)} collective-permute-done((bf16[128,1024]{0,1:T(8,128)(2,1)S(1)}, bf16[128,1024]{0,1:T(8,128)(2,1)S(1)}, u32[]{:S(2)}, u32[]{:S(2)}) %collective-permute-start.14) | collective-permute-done | bytes 262176 | tf_op jit(solution)/shard_map/ppermute | solution.py:14
  84.4 3.6 %collective-permute-start.15 = (bf16[128,1024]{0,1:T(8,128)(2,1)S(1)}, bf16[128,1024]{0,1:T(8,128)(2,1)S(1)}, u32[]{:S(2)}, u32[]{:S(2)}) collective-permute-start(bf16[128,1024]{0,1:T(8,128)(2,1)S(1)} %bitcast.143), channel_id=1, source_target_pairs={{0,8},{2,10},{4,12},{6,14},{8,0},{10,2},{12,4},{14,6},{16,24},{18,... | collective-permute-start | bytes 786440 | tf_op jit(solution)/shard_map/ppermute | solution.py:14
  88.0 1.6 %collective-permute-done.12 = bf16[128,1024]{0,1:T(8,128)(2,1)S(1)} collective-permute-done((bf16[128,1024]{0,1:T(8,128)(2,1)S(1)}, bf16[128,1024]{0,1:T(8,128)(2,1)S(1)}, u32[]{:S(2)}, u32[]{:S(2)}) %collective-permute-start.12) | collective-permute-done | bytes 262176 | tf_op jit(solution)/shard_map/ppermute | solution.py:14
  89.6 4.0 %collective-permute-start.16 = (bf16[128,1024]{0,1:T(8,128)(2,1)S(1)}, bf16[128,1024]{0,1:T(8,128)(2,1)S(1)}, u32[]{:S(2)}, u32[]{:S(2)}) collective-permute-start(bf16[128,1024]{0,1:T(8,128)(2,1)S(1)} %collective-permute-done.12), channel_id=1, source_target_pairs={{0,8},{2,10},{4,12},{6,14},{8,0},{10,2},{12,4},{14,6},{16,24},{18,... | collective-permute-start | bytes 786440 | tf_op jit(solution)/shard_map/ppermute | solution.py:14
  93.6 3.4 %collective-permute-start.19 = (bf16[768,256]{1,0:T(8,128)(2,1)}, bf16[768,256]{1,0:T(8,128)(2,1)S(1)}, u32[]{:S(2)}, u32[]{:S(2)}) collective-permute-start(bf16[768,256]{1,0:T(8,128)(2,1)} %constant_dynamic-slice_fusion.3), channel_id=1, source_target_pairs={{0,2},{2,0},{4,6},{6,4},{8,10},{10,8},{12,14},{14,12},{16,18},{18,... | collective-permute-start | bytes 1179656 | tf_op jit(solution)/shard_map/ppermute | solution.py:14
  98.2 2.8 %collective-permute-start.23 = (bf16[768,256]{1,0:T(8,128)(2,1)}, bf16[768,256]{1,0:T(8,128)(2,1)S(1)}, u32[]{:S(2)}, u32[]{:S(2)}) collective-permute-start(bf16[768,256]{1,0:T(8,128)(2,1)} %collective-permute-done.22), channel_id=1, source_target_pairs={{0,2},{2,0},{4,6},{6,4},{8,10},{10,8},{12,14},{14,12},{16,18},{18,... | collective-permute-start | bytes 1179656 | tf_op jit(solution)/shard_map/ppermute | solution.py:14
  102.5 4.8 %maximum_maximum_fusion = bf16[512,2048]{0,1:T(8,128)(2,1)S(1)} fusion(bf16[128,1024]{0,1:T(8,128)(2,1)S(1)} %collective-permute-done.17, bf16[128,1024]{0,1:T(8,128)(2,1)S(1)} %collective-permute-done.16, bf16[128,1024]{0,1:T(8,128)(2,1)S(1)} %collective-permute-done.15, bf16[128,1024]{0,1:T(8,128)(2,1)S(1)} %collective-permute-done.14, ...), kind=kLoop, calls=%fused_computation | loop fusion | flops 16777216 | bytes 4194304 | tf_op jit(solution)/shard_map/concatenate | solution.py:167
  107.9 1.4 fusion.78
  109.3 1.6 %convolution_add_fusion = f32[512,256]{1,0:T(8,128)S(1)} fusion(f32[512,256]{1,0:T(8,128)S(1)} %fusion.78, bf16[1280,256]{1,0:T(8,128)(2,1)} %collective-permute-done.20, bf16[512,2048]{0,1:T(8,128)(2,1)S(1)} %maximum_maximum_fusion), kind=kOutput, calls=%fused_computation.1 | convolution fusion | flops 335675392 | bytes 3014656 | tf_op jit(solution)/shard_map/dot_general | solution.py:175
  111.5 17.9 %collective-permute-done.23 = bf16[768,256]{1,0:T(8,128)(2,1)S(1)} collective-permute-done((bf16[768,256]{1,0:T(8,128)(2,1)}, bf16[768,256]{1,0:T(8,128)(2,1)S(1)}, u32[]{:S(2)}, u32[]{:S(2)}) %collective-permute-start.23) | collective-permute-done | bytes 393248 | tf_op jit(solution)/shard_map/ppermute | solution.py:14
  130.3 6.0 %collective-permute-done.21 = bf16[1280,256]{1,0:T(8,128)(2,1)S(1)} collective-permute-done((bf16[1280,256]{1,0:T(8,128)(2,1)}, bf16[1280,256]{1,0:T(8,128)(2,1)S(1)}, u32[]{:S(2)}, u32[]{:S(2)}) %collective-permute-start.21) | collective-permute-done | bytes 655392 | tf_op jit(solution)/shard_map/ppermute | solution.py:14
  137.2 1.5 %collective-permute-start.31 = (bf16[128,256]{1,0:T(8,128)(2,1)S(1)}, bf16[128,256]{1,0:T(8,128)(2,1)S(1)}, u32[]{:S(2)}, u32[]{:S(2)}) collective-permute-start(bf16[128,256]{1,0:T(8,128)(2,1)S(1)} %get-tuple-element.35), channel_id=1, source_target_pairs={{0,4},{2,6},{4,0},{6,2},{8,12},{10,14},{12,8},{14,10},{16,20},{18,... | collective-permute-start | bytes 196616 | tf_op jit(solution)/shard_map/ppermute | solution.py:14
  138.8 1.5 collective-permute-start.29
  140.9 1.5 %collective-permute-start.27 = (bf16[128,256]{1,0:T(8,128)(2,1)S(1)}, bf16[128,256]{1,0:T(8,128)(2,1)S(1)}, u32[]{:S(2)}, u32[]{:S(2)}) collective-permute-start(bf16[128,256]{1,0:T(8,128)(2,1)S(1)} %get-tuple-element.32), channel_id=1, source_target_pairs={{0,4},{2,6},{4,0},{6,2},{8,12},{10,14},{12,8},{14,10},{16,20},{18,... | collective-permute-start | bytes 196616 | tf_op jit(solution)/shard_map/ppermute | solution.py:14
  142.4 1.5 collective-permute-start.25
  145.3 2.3 %collective-permute-done.25 = bf16[128,256]{1,0:T(8,128)(2,1)S(1)} collective-permute-done((bf16[128,256]{1,0:T(8,128)(2,1)S(1)}, bf16[128,256]{1,0:T(8,128)(2,1)S(1)}, u32[]{:S(2)}, u32[]{:S(2)}) %collective-permute-start.25) | collective-permute-done | bytes 65568 | tf_op jit(solution)/shard_map/ppermute | solution.py:14
  (102 shorter events, 28.0 us)
Async XLA Ops:
  3.6 16.0 %collective-permute-start.1 = (bf16[8,128,128]{2,1,0:T(8,128)(2,1)}, bf16[8,128,128]{2,1,0:T(8,128)(2,1)S(1)}, u32[]{:S(2)}, u32[]{:S(2)}) collective-permute-start(bf16[8,128,128]{2,1,0:T(8,128)(2,1)} %get-tuple-element.47), channel_id=1, source_target_pairs={{0,4},{2,6},{4,0},{6,2},{8,12},{10,14},{12,8},{14,10},{16,20},{18,... | collective-permute-start | bytes 786440 | tf_op jit(solution)/shard_map/ppermute | solution.py:14
  6.6 21.3 %collective-permute-start.7 = (bf16[8,128,128]{2,1,0:T(8,128)(2,1)}, bf16[8,128,128]{2,1,0:T(8,128)(2,1)}, u32[]{:S(2)}, u32[]{:S(2)}) collective-permute-start(bf16[8,128,128]{2,1,0:T(8,128)(2,1)} %get-tuple-element.47), channel_id=1, source_target_pairs={{0,2},{2,0},{4,6},{6,4},{8,10},{10,8},{12,14},{14,12},{16,18},{18,... | collective-permute-start | bytes 786440 | tf_op jit(solution)/shard_map/ppermute | solution.py:14
  9.5 15.1 %collective-permute-start = (bf16[8,128,128]{2,1,0:T(8,128)(2,1)}, bf16[8,128,128]{2,1,0:T(8,128)(2,1)S(1)}, u32[]{:S(2)}, u32[]{:S(2)}) collective-permute-start(bf16[8,128,128]{2,1,0:T(8,128)(2,1)} %get-tuple-element.49), channel_id=1, source_target_pairs={{0,2},{2,0},{4,6},{6,4},{8,10},{10,8},{12,14},{14,12},{16,18},{18,... | collective-permute-start | bytes 786440 | tf_op jit(solution)/shard_map/ppermute | solution.py:14
  10.0 21.5 %collective-permute-start.8 = (bf16[8,128,128]{2,1,0:T(8,128)(2,1)}, bf16[8,128,128]{2,1,0:T(8,128)(2,1)}, u32[]{:S(2)}, u32[]{:S(2)}) collective-permute-start(bf16[8,128,128]{2,1,0:T(8,128)(2,1)} %get-tuple-element.49), channel_id=1, source_target_pairs={{0,4},{2,6},{4,0},{6,2},{8,12},{10,14},{12,8},{14,10},{16,20},{18,... | collective-permute-start | bytes 786440 | tf_op jit(solution)/shard_map/ppermute | solution.py:14
  11.8 72.6 %collective-permute-start.22 = (bf16[768,256]{1,0:T(8,128)(2,1)}, bf16[768,256]{1,0:T(8,128)(2,1)}, u32[]{:S(2)}, u32[]{:S(2)}) collective-permute-start(bf16[768,256]{1,0:T(8,128)(2,1)} %constant_dynamic-slice_fusion.3), channel_id=1, source_target_pairs={{0,16},{2,18},{4,20},{6,22},{8,24},{10,26},{12,28},{14,30},{16,0},... | collective-permute-start | bytes 1179656 | tf_op jit(solution)/shard_map/ppermute | solution.py:14
  19.6 6.7 %collective-permute-start.2 = (bf16[8,128,128]{2,1,0:T(8,128)(2,1)S(1)}, bf16[8,128,128]{2,1,0:T(8,128)(2,1)S(1)}, u32[]{:S(2)}, u32[]{:S(2)}) collective-permute-start(bf16[8,128,128]{2,1,0:T(8,128)(2,1)S(1)} %collective-permute-done.1), channel_id=1, source_target_pairs={{0,2},{2,0},{4,6},{6,4},{8,10},{10,8},{12,14},{14,12},{16,18},{18,... | collective-permute-start | bytes 786440 | tf_op jit(solution)/shard_map/ppermute | solution.py:14
  24.5 69.0 %collective-permute-start.20 = (bf16[1280,256]{1,0:T(8,128)(2,1)}, bf16[1280,256]{1,0:T(8,128)(2,1)}, u32[]{:S(2)}, u32[]{:S(2)}) collective-permute-start(bf16[1280,256]{1,0:T(8,128)(2,1)} %pad_maximum_fusion), channel_id=1, source_target_pairs={{0,16},{2,18},{4,20},{6,22},{8,24},{10,26},{12,28},{14,30},{16,0},... | collective-permute-start | bytes 1966088 | tf_op jit(solution)/shard_map/ppermute | solution.py:14
  26.3 6.4 %collective-permute-start.9 = (bf16[8,128,128]{2,1,0:T(8,128)(2,1)S(1)}, bf16[8,128,128]{2,1,0:T(8,128)(2,1)S(1)}, u32[]{:S(2)}, u32[]{:S(2)}) collective-permute-start(bf16[8,128,128]{2,1,0:T(8,128)(2,1)S(1)} %collective-permute-done), channel_id=1, source_target_pairs={{0,4},{2,6},{4,0},{6,2},{8,12},{10,14},{12,8},{14,10},{16,20},{18,... | collective-permute-start | bytes 786440 | tf_op jit(solution)/shard_map/ppermute | solution.py:14
  27.9 18.0 %collective-permute-start.3 = (bf16[8,128,128]{2,1,0:T(8,128)(2,1)S(1)}, bf16[8,128,128]{2,1,0:T(8,128)(2,1)S(1)}, u32[]{:S(2)}, u32[]{:S(2)}) collective-permute-start(bf16[8,128,128]{2,1,0:T(8,128)(2,1)S(1)} %fusion.42), channel_id=1, source_target_pairs={{0,8},{2,10},{4,12},{6,14},{1,9},{3,11},{5,13},{7,15}} | collective-permute-start | bytes 786440 | tf_op jit(solution)/shard_map/ppermute | solution.py:23
  31.5 18.5 %collective-permute-start.4 = (bf16[8,128,128]{2,1,0:T(8,128)(2,1)S(1)}, bf16[8,128,128]{2,1,0:T(8,128)(2,1)S(1)}, u32[]{:S(2)}, u32[]{:S(2)}) collective-permute-start(bf16[8,128,128]{2,1,0:T(8,128)(2,1)S(1)} %fusion.42), channel_id=1, source_target_pairs={{16,24},{18,26},{20,28},{22,30},{17,25},{19,27},{21,29},{23,31}} | collective-permute-start | bytes 786440 | tf_op jit(solution)/shard_map/ppermute | solution.py:23
  33.8 14.9 %collective-permute-start.10 = (bf16[8,128,128]{2,1,0:T(8,128)(2,1)S(1)}, bf16[8,128,128]{2,1,0:T(8,128)(2,1)S(1)}, u32[]{:S(2)}, u32[]{:S(2)}) collective-permute-start(bf16[8,128,128]{2,1,0:T(8,128)(2,1)S(1)} %add_convert_fusion.2), channel_id=1, source_target_pairs={{0,8},{2,10},{4,12},{6,14},{16,24},{18,26},{20,28},{22,30},{1,9},{... | collective-permute-start | bytes 786440 | tf_op jit(solution)/shard_map/ppermute | solution.py:23
  46.1 4.1 %collective-permute-start.5 = (bf16[8,128,128]{2,1,0:T(8,128)(2,1)S(1)}, bf16[8,128,128]{2,1,0:T(8,128)(2,1)S(1)}, u32[]{:S(2)}, u32[]{:S(2)}) collective-permute-start(bf16[8,128,128]{2,1,0:T(8,128)(2,1)S(1)} %add_convert_fusion.3), channel_id=1, source_target_pairs={{8,24},{10,26},{12,28},{14,30},{9,25},{11,27},{13,29},{15,31}} | collective-permute-start | bytes 786440 | tf_op jit(solution)/shard_map/ppermute | solution.py:23
  48.8 1.5 collective-permute-start.6
  50.3 29.3 %collective-permute-start.11 = (bf16[8,128,128]{2,1,0:T(8,128)(2,1)S(1)}, bf16[8,128,128]{2,1,0:T(8,128)(2,1)S(1)}, u32[]{:S(2)}, u32[]{:S(2)}) collective-permute-start(bf16[8,128,128]{2,1,0:T(8,128)(2,1)S(1)} %add.114), channel_id=1, source_target_pairs={{0,4},{2,6},{4,0},{6,2},{8,12},{10,14},{12,8},{14,10},{16,20},{18,... | collective-permute-start | bytes 786440 | tf_op jit(solution)/shard_map/ppermute | solution.py:14
  52.6 31.4 %collective-permute-start.14 = (bf16[128,1024]{0,1:T(8,128)(2,1)S(1)}, bf16[128,1024]{0,1:T(8,128)(2,1)S(1)}, u32[]{:S(2)}, u32[]{:S(2)}) collective-permute-start(bf16[128,1024]{0,1:T(8,128)(2,1)S(1)} %bitcast.138), channel_id=1, source_target_pairs={{0,8},{2,10},{4,12},{6,14},{8,0},{10,2},{12,4},{14,6},{16,24},{18,... | collective-permute-start | bytes 786440 | tf_op jit(solution)/shard_map/ppermute | solution.py:14
  80.3 9.2 %collective-permute-start.12 = (bf16[128,1024]{0,1:T(8,128)(2,1)S(1)}, bf16[128,1024]{0,1:T(8,128)(2,1)S(1)}, u32[]{:S(2)}, u32[]{:S(2)}) collective-permute-start(bf16[128,1024]{0,1:T(8,128)(2,1)S(1)} %bitcast.142), channel_id=1, source_target_pairs={{0,4},{2,6},{4,0},{6,2},{8,12},{10,14},{12,8},{14,10},{16,20},{18,... | collective-permute-start | bytes 786440 | tf_op jit(solution)/shard_map/ppermute | solution.py:14
  80.8 16.1 %collective-permute-start.13 = (bf16[128,1024]{0,1:T(8,128)(2,1)S(1)}, bf16[128,1024]{0,1:T(8,128)(2,1)S(1)}, u32[]{:S(2)}, u32[]{:S(2)}) collective-permute-start(bf16[128,1024]{0,1:T(8,128)(2,1)S(1)} %bitcast.139), channel_id=1, source_target_pairs={{0,4},{2,6},{4,0},{6,2},{8,12},{10,14},{12,8},{14,10},{16,20},{18,... | collective-permute-start | bytes 786440 | tf_op jit(solution)/shard_map/ppermute | solution.py:14
  84.0 14.2 %collective-permute-start.17 = (bf16[128,1024]{0,1:T(8,128)(2,1)S(1)}, bf16[128,1024]{0,1:T(8,128)(2,1)S(1)}, u32[]{:S(2)}, u32[]{:S(2)}) collective-permute-start(bf16[128,1024]{0,1:T(8,128)(2,1)S(1)} %collective-permute-done.14), channel_id=1, source_target_pairs={{0,4},{2,6},{4,0},{6,2},{8,12},{10,14},{12,8},{14,10},{16,20},{18,... | collective-permute-start | bytes 786440 | tf_op jit(solution)/shard_map/ppermute | solution.py:14
  84.4 16.6 %collective-permute-start.15 = (bf16[128,1024]{0,1:T(8,128)(2,1)S(1)}, bf16[128,1024]{0,1:T(8,128)(2,1)S(1)}, u32[]{:S(2)}, u32[]{:S(2)}) collective-permute-start(bf16[128,1024]{0,1:T(8,128)(2,1)S(1)} %bitcast.143), channel_id=1, source_target_pairs={{0,8},{2,10},{4,12},{6,14},{8,0},{10,2},{12,4},{14,6},{16,24},{18,... | collective-permute-start | bytes 786440 | tf_op jit(solution)/shard_map/ppermute | solution.py:14
  89.6 11.4 %collective-permute-start.16 = (bf16[128,1024]{0,1:T(8,128)(2,1)S(1)}, bf16[128,1024]{0,1:T(8,128)(2,1)S(1)}, u32[]{:S(2)}, u32[]{:S(2)}) collective-permute-start(bf16[128,1024]{0,1:T(8,128)(2,1)S(1)} %collective-permute-done.12), channel_id=1, source_target_pairs={{0,8},{2,10},{4,12},{6,14},{8,0},{10,2},{12,4},{14,6},{16,24},{18,... | collective-permute-start | bytes 786440 | tf_op jit(solution)/shard_map/ppermute | solution.py:14
  93.6 17.5 %collective-permute-start.19 = (bf16[768,256]{1,0:T(8,128)(2,1)}, bf16[768,256]{1,0:T(8,128)(2,1)S(1)}, u32[]{:S(2)}, u32[]{:S(2)}) collective-permute-start(bf16[768,256]{1,0:T(8,128)(2,1)} %constant_dynamic-slice_fusion.3), channel_id=1, source_target_pairs={{0,2},{2,0},{4,6},{6,4},{8,10},{10,8},{12,14},{14,12},{16,18},{18,... | collective-permute-start | bytes 1179656 | tf_op jit(solution)/shard_map/ppermute | solution.py:14
  97.0 32.8 %collective-permute-start.18 = (bf16[1280,256]{1,0:T(8,128)(2,1)}, bf16[1280,256]{1,0:T(8,128)(2,1)S(1)}, u32[]{:S(2)}, u32[]{:S(2)}) collective-permute-start(bf16[1280,256]{1,0:T(8,128)(2,1)} %pad_maximum_fusion), channel_id=1, source_target_pairs={{0,2},{2,0},{4,6},{6,4},{8,10},{10,8},{12,14},{14,12},{16,18},{18,... | collective-permute-start | bytes 1966088 | tf_op jit(solution)/shard_map/ppermute | solution.py:14
  98.2 31.2 %collective-permute-start.23 = (bf16[768,256]{1,0:T(8,128)(2,1)}, bf16[768,256]{1,0:T(8,128)(2,1)S(1)}, u32[]{:S(2)}, u32[]{:S(2)}) collective-permute-start(bf16[768,256]{1,0:T(8,128)(2,1)} %collective-permute-done.22), channel_id=1, source_target_pairs={{0,2},{2,0},{4,6},{6,4},{8,10},{10,8},{12,14},{14,12},{16,18},{18,... | collective-permute-start | bytes 1179656 | tf_op jit(solution)/shard_map/ppermute | solution.py:14
  101.0 35.4 %collective-permute-start.21 = (bf16[1280,256]{1,0:T(8,128)(2,1)}, bf16[1280,256]{1,0:T(8,128)(2,1)S(1)}, u32[]{:S(2)}, u32[]{:S(2)}) collective-permute-start(bf16[1280,256]{1,0:T(8,128)(2,1)} %collective-permute-done.20), channel_id=1, source_target_pairs={{0,2},{2,0},{4,6},{6,4},{8,10},{10,8},{12,14},{14,12},{16,18},{18,... | collective-permute-start | bytes 1966088 | tf_op jit(solution)/shard_map/ppermute | solution.py:14
  111.0 26.1 %collective-permute-start.28 = (bf16[512,256]{1,0:T(8,128)(2,1)S(1)}, bf16[512,256]{1,0:T(8,128)(2,1)S(1)}, u32[]{:S(2)}, u32[]{:S(2)}) collective-permute-start(bf16[512,256]{1,0:T(8,128)(2,1)S(1)} %select_convert_fusion), channel_id=1, source_target_pairs={{0,1},{1,0},{2,3},{3,2},{4,5},{5,4},{6,7},{7,6},{8,9},{9,8},{10,11... | collective-permute-start | bytes 786440 | tf_op jit(solution)/shard_map/ppermute | solution.py:27
  137.0 3.8 %collective-permute-start.24 = (bf16[512,256]{1,0:T(8,128)(2,1)S(1)}, bf16[512,256]{1,0:T(8,128)(2,1)S(1)}, u32[]{:S(2)}, u32[]{:S(2)}) collective-permute-start(bf16[512,256]{1,0:T(8,128)(2,1)S(1)} %select_convert_fusion.1), channel_id=1, source_target_pairs={{0,1},{1,0},{2,3},{3,2},{4,5},{5,4},{6,7},{7,6},{8,9},{9,8},{10,11... | collective-permute-start | bytes 786440 | tf_op jit(solution)/shard_map/ppermute | solution.py:27
  137.2 6.7 %collective-permute-start.31 = (bf16[128,256]{1,0:T(8,128)(2,1)S(1)}, bf16[128,256]{1,0:T(8,128)(2,1)S(1)}, u32[]{:S(2)}, u32[]{:S(2)}) collective-permute-start(bf16[128,256]{1,0:T(8,128)(2,1)S(1)} %get-tuple-element.35), channel_id=1, source_target_pairs={{0,4},{2,6},{4,0},{6,2},{8,12},{10,14},{12,8},{14,10},{16,20},{18,... | collective-permute-start | bytes 196616 | tf_op jit(solution)/shard_map/ppermute | solution.py:14
  138.8 5.7 %collective-permute-start.29 = (bf16[128,256]{1,0:T(8,128)(2,1)S(1)}, bf16[128,256]{1,0:T(8,128)(2,1)S(1)}, u32[]{:S(2)}, u32[]{:S(2)}) collective-permute-start(bf16[128,256]{1,0:T(8,128)(2,1)S(1)} %get-tuple-element.36), channel_id=1, source_target_pairs={{0,12},{2,14},{4,8},{6,10},{8,4},{10,6},{12,0},{14,2},{16,28},{18,... | collective-permute-start | bytes 196616 | tf_op jit(solution)/shard_map/ppermute | solution.py:14
  140.2 4.4 %collective-permute-start.30 = (bf16[128,256]{1,0:T(8,128)(2,1)S(1)}, bf16[128,256]{1,0:T(8,128)(2,1)S(1)}, u32[]{:S(2)}, u32[]{:S(2)}) collective-permute-start(bf16[128,256]{1,0:T(8,128)(2,1)S(1)} %get-tuple-element.34), channel_id=1, source_target_pairs={{0,8},{2,10},{4,12},{6,14},{8,0},{10,2},{12,4},{14,6},{16,24},{18,... | collective-permute-start | bytes 196616 | tf_op jit(solution)/shard_map/ppermute | solution.py:14
  140.9 4.4 %collective-permute-start.27 = (bf16[128,256]{1,0:T(8,128)(2,1)S(1)}, bf16[128,256]{1,0:T(8,128)(2,1)S(1)}, u32[]{:S(2)}, u32[]{:S(2)}) collective-permute-start(bf16[128,256]{1,0:T(8,128)(2,1)S(1)} %get-tuple-element.32), channel_id=1, source_target_pairs={{0,4},{2,6},{4,0},{6,2},{8,12},{10,14},{12,8},{14,10},{16,20},{18,... | collective-permute-start | bytes 196616 | tf_op jit(solution)/shard_map/ppermute | solution.py:14
  142.4 5.2 %collective-permute-start.25 = (bf16[128,256]{1,0:T(8,128)(2,1)S(1)}, bf16[128,256]{1,0:T(8,128)(2,1)S(1)}, u32[]{:S(2)}, u32[]{:S(2)}) collective-permute-start(bf16[128,256]{1,0:T(8,128)(2,1)S(1)} %get-tuple-element.33), channel_id=1, source_target_pairs={{0,12},{2,14},{4,8},{6,10},{8,4},{10,6},{12,0},{14,2},{16,28},{18,... | collective-permute-start | bytes 196616 | tf_op jit(solution)/shard_map/ppermute | solution.py:14
  143.9 4.3 %collective-permute-start.26 = (bf16[128,256]{1,0:T(8,128)(2,1)S(1)}, bf16[128,256]{1,0:T(8,128)(2,1)S(1)}, u32[]{:S(2)}, u32[]{:S(2)}) collective-permute-start(bf16[128,256]{1,0:T(8,128)(2,1)S(1)} %get-tuple-element.31), channel_id=1, source_target_pairs={{0,8},{2,10},{4,12},{6,14},{8,0},{10,2},{12,4},{14,6},{16,24},{18,... | collective-permute-start | bytes 196616 | tf_op jit(solution)/shard_map/ppermute | solution.py:14
  (6 other events, 36.0 us)

commit v2 on v1

v2 whole, which is shorter than its diff:
```python
import math

import jax
import jax.numpy as jnp
from jax import lax
from jax.experimental import pallas as pl
from jax.experimental.pallas import tpu as pltpu
from jax.sharding import PartitionSpec as P

DH = 128


def swap(value, mask):
    pairs = [(source, source ^ mask) for source in range(lax.axis_size("seq"))]
    return lax.ppermute(value, "seq", pairs)


def lift(value, clear, need, mask):
    pairs = [
        (source, source ^ mask)
        for source in range(lax.axis_size("seq"))
        if not source & clear and source & need == need
    ]
    return lax.ppermute(value, "seq", pairs)


def swap_some(value, mask, half, upper):
    pairs = [
        (source, source ^ mask)
        for source in range(lax.axis_size("seq"))
        if (source & half != 0) == bool(upper)
    ]
    return lax.ppermute(value, "seq", pairs)


def swap_cores(value):
    return lax.ppermute(value, "head", [(0, 1), (1, 0)])


def masks_of(bits):
    out = [0]
    for bit in bits:
        out = out + [mask | 1 << bit for mask in out]
    return out


def groups(depth):
    top = depth - 1
    token_bits = [1, top - 1] if depth < 6 else [1, 2, top - 1]
    column_bits = [bit for bit in range(top) if bit not in token_bits][::-1]
    return token_bits, column_bits


HERE = pl.BlockSpec(memory_space=pltpu.VMEM)
FLAT = pl.BlockSpec(memory_space=pltpu.SMEM)
SMALL = pltpu.CompilerParams(vmem_limit_bytes=8 << 20)
F32, BF16 = jnp.float32, jnp.bfloat16


def local(kernel, scalars, operands, results):
    placed = [pltpu.with_memory_space_constraint(operand, pltpu.VMEM) for operand in operands]
    return pl.pallas_call(
        kernel,
        out_shape=tuple(pltpu.VMEM(shape, dtype) for shape, dtype in results),
        in_specs=[FLAT] * len(scalars) + [HERE] * len(operands),
        out_specs=tuple(HERE for _ in results),
        compiler_params=SMALL,
    )(*scalars, *placed)


def head_slice(start, head):
    return pl.ds(pl.multiple_of((start + head) * DH, DH), DH)


def states(flip, keys, values, half):
    rows, depth = keys.shape[0], half * DH

    def kernel(flip_ref, key_hbm, value_hbm, sum1_ref, own1_ref, sum0_ref, own0_ref, key_ref, value_ref, sems):
        copies = {}
        for part in (1, 0):
            start = pl.multiple_of(jnp.where(flip_ref[0] == part, 0, depth), depth)
            for at, (source, target) in enumerate(((key_hbm, key_ref), (value_hbm, value_ref))):
                copies[part, at] = pltpu.make_async_copy(
                    source.at[:, pl.ds(start, depth)], target.at[part], sems.at[part, at]
                )
                copies[part, at].start()
        for part, sum_ref, own_ref in ((1, sum1_ref, own1_ref), (0, sum0_ref, own0_ref)):
            copies[part, 0].wait()
            copies[part, 1].wait()
            for head in range(half):
                cut = slice(head * DH, (head + 1) * DH)
                state = lax.dot_general(
                    key_ref[part, :, cut],
                    value_ref[part, :, cut],
                    (((0,), (0,)), ((), ())),
                    preferred_element_type=F32,
                )
                sum_ref[head] = state
                own_ref[head] = state.astype(BF16)

    shape = (half, DH, DH)
    anywhere = pl.BlockSpec(memory_space=pltpu.HBM)
    made = pl.pallas_call(
        kernel,
        out_shape=(jax.ShapeDtypeStruct(shape, F32), pltpu.VMEM(shape, BF16)) * 2,
        in_specs=[FLAT, anywhere, anywhere],
        out_specs=(HERE,) * 4,
        scratch_shapes=[
            pltpu.VMEM((2, rows, depth), BF16),
            pltpu.VMEM((2, rows, depth), BF16),
            pltpu.SemaphoreType.DMA((2, 2)),
        ],
        compiler_params=SMALL,
        name="state",
    )(flip, *(pltpu.with_memory_space_constraint(operand, pltpu.HBM) for operand in (keys, values)))
    return [made[2:], made[:2]]


def merge(down, up):
    def kernel(down_ref, up_ref, out_ref):
        out_ref[...] = down_ref[...] + up_ref[...]

    return local(kernel, [], [down, up], [(down.shape, BF16)])[0]


def order_rows(flip, weight, split):
    depth, width = weight.shape
    half = depth // 2
    sizes = (split, depth - split)

    def kernel(flip_ref, weight_ref, *refs):
        out_refs, sems = refs[:2], refs[2]
        copies = []
        for out, (low, size) in enumerate(((0, split), (split, depth - split))):
            for which in range(2):
                begin, end = max(low, which * half), min(low + size, (which + 1) * half)
                if begin < end:
                    start = pl.multiple_of(jnp.where(flip_ref[0] == which, 0, half), half)
                    copies.append(
                        pltpu.make_async_copy(
                            weight_ref.at[pl.ds(start + begin - which * half, end - begin)],
                            out_refs[out].at[pl.ds(begin - low, end - begin)],
                            sems.at[len(copies)],
                        )
                    )
        for copy in copies:
            copy.start()
        for copy in copies:
            copy.wait()

    return pl.pallas_call(
        kernel,
        out_shape=tuple(pltpu.VMEM((size, width), weight.dtype) for size in sizes),
        in_specs=[FLAT, pl.BlockSpec(memory_space=pltpu.HBM)],
        out_specs=(HERE, HERE),
        scratch_shapes=[pltpu.SemaphoreType.DMA((4,))],
        compiler_params=SMALL,
        name="order",
    )(flip, pltpu.with_memory_space_constraint(weight, pltpu.HBM))


def level_scales(flip, position, level_index, level_table, roots, flags, half):
    rows, values = level_index.shape[0], level_table.shape[1]

    def kernel(flip_ref, position_ref, index_ref, table_ref, *out_refs):
        for part, out_ref in enumerate(out_refs):
            start = pl.multiple_of(jnp.where(flip_ref[0] == part, 0, half), half)
            table = table_ref[pl.ds(start, half), :]
            for level, root in enumerate(roots):
                chosen = index_ref[:, level : level + 1] == lax.broadcasted_iota(
                    jnp.int32, (rows, values), 1
                )
                lam = lax.dot_general(
                    chosen.astype(F32),
                    table,
                    (((1,), (1,)), ((), ())),
                    precision=lax.Precision.HIGHEST,
                    preferred_element_type=F32,
                )
                scale = lam * root
                if flags[level] is not None:
                    scale = jnp.where(position_ref[0] >> flags[level] & 1 == 1, scale, 0.0)
                out_ref[level] = scale

    shape = (len(roots), rows, half)
    return local(kernel, [flip, position], [level_index, level_table], [(shape, F32), (shape, F32)])


def block_sum(state, near, side, corner):
    def kernel(state_ref, near_ref, side_ref, corner_ref, sent_ref, block_ref):
        for head in range(state.shape[0]):
            pair = side_ref[head].astype(F32) + corner_ref[head].astype(F32)
            block = state_ref[head] + near_ref[head].astype(F32) + pair
            sent_ref[head] = block.astype(BF16)
            block_ref[head] = block

    results = [(state.shape, BF16), (state.shape, F32)]
    return local(kernel, [], [state, near, side, corner], results)


def add_block(block, other, wide):
    def kernel(block_ref, other_ref, *out_refs):
        for head in range(block.shape[0]):
            total = block_ref[head].astype(F32) + other_ref[head].astype(F32)
            for out_ref in out_refs:
                out_ref[head] = total.astype(out_ref.dtype)

    results = [(block.shape, BF16)] + [(block.shape, F32)] * wide
    return local(kernel, [], [block, other], results)


def first_reads(flip, queries, keys, values, scales, levels, half, part):
    rows = queries.shape[0]

    def kernel(flip_ref, query_ref, key_ref, value_ref, scale_ref, *refs):
        level_refs, total_ref = refs[:-1], refs[-1]
        start = jnp.where(flip_ref[0] == part, 0, half)
        causal = lax.broadcasted_iota(jnp.int32, (rows, rows), 0) >= lax.broadcasted_iota(
            jnp.int32, (rows, rows), 1
        )
        for head in range(half):
            cut = head_slice(start, head)
            query = query_ref[:, cut]
            scores = lax.dot_general(
                query, key_ref[:, cut], (((1,), (1,)), ((), ())), preferred_element_type=F32
            )
            weights = jnp.where(causal, scores * scale_ref[0, :, head : head + 1], 0.0).astype(BF16)
            total = jnp.dot(weights, value_ref[:, cut], preferred_element_type=F32)
            pair = (level_refs[1][head].astype(F32) + level_refs[2][head].astype(F32)).astype(BF16)
            found = [level_refs[0][head], pair] + [level_ref[head] for level_ref in level_refs[3:]]
            for at, level in enumerate(found):
                reads = jnp.dot(query, level, preferred_element_type=F32)
                total = total + reads * scale_ref[at + 1, :, head : head + 1]
            total_ref[:, head * DH : (head + 1) * DH] = total

    return local(kernel, [flip], [queries, keys, values, scales, *levels], [((rows, half * DH), F32)])[0]


def last_reads(flip, queries, scales, total, levels, half, part):
    rows = queries.shape[0]
    index = [at for _, at in levels]

    def kernel(flip_ref, query_ref, scale_ref, total_ref, *refs):
        level_refs, normed_ref = refs[:-1], refs[-1]
        start = jnp.where(flip_ref[0] == part, 0, half)
        for head in range(half):
            here = slice(head * DH, (head + 1) * DH)
            query, sums = query_ref[:, head_slice(start, head)], total_ref[:, here]
            for at, level_ref in zip(index, level_refs):
                reads = jnp.dot(query, level_ref[head], preferred_element_type=F32)
                sums = sums + reads * scale_ref[at, :, head : head + 1]
            square = jnp.mean(sums * sums, axis=-1, keepdims=True)
            normed_ref[:, here] = (sums * lax.rsqrt(square + 1e-06)).astype(BF16)

    arrays = [array for array, _ in levels]
    return local(kernel, [flip], [queries, scales, total, *arrays], [((rows, half * DH), BF16)])[0]


def project(mine, tokens, weights, jobs):
    rows, half = tokens[0][0].shape
    width = weights[0][0].shape[1]
    counts = [len(parts) for parts in weights]
    total_rows = rows * len(jobs)

    def kernel(mine_ref, *refs):
        token_refs, refs = refs[: 2 * len(tokens)], refs[2 * len(tokens) :]
        weight_refs = []
        for count in counts:
            weight_refs.append(refs[:count])
            refs = refs[count:]
        keep_ref, give_ref = refs
        ours = mine_ref[0] == 1

        def product(piece, part_refs):
            total, at = None, 0
            for part_ref in part_refs:
                end = at + part_ref.shape[0]
                for which in range(2):
                    low, high = max(at, which * half), min(end, (which + 1) * half)
                    if low < high:
                        one = jnp.dot(
                            token_refs[2 * piece + which][:, low - which * half : high - which * half],
                            part_ref[low - at : high - at, :],
                            preferred_element_type=F32,
                        )
                        total = one if total is None else total + one
                at = end
            return total

        for at, (piece, near, far) in enumerate(jobs):
            here = slice(at * rows, (at + 1) * rows)
            close, away = product(piece, weight_refs[near]), product(piece, weight_refs[far])
            keep_ref[here, :] = jnp.where(ours, close, away)
            give_ref[here, :] = jnp.where(ours, away, close).astype(BF16)

    shape = (total_rows, width)
    flat = [half_piece for pair in tokens for half_piece in pair] + [part for parts in weights for part in parts]
    return local(kernel, [mine], flat, [(shape, F32), (shape, BF16)])


def add_cores(keep, got, rows, groups):
    width = keep.shape[1]

    def kernel(keep_ref, got_ref, *out_refs):
        for group, out_ref in zip(groups, out_refs):
            for at, job in enumerate(group):
                here = slice(job * rows, (job + 1) * rows)
                total = keep_ref[here, :] + got_ref[here, :].astype(F32)
                out_ref[:, at * width : (at + 1) * width] = total.astype(BF16)

    return local(kernel, [], [keep, got], [((rows, width * len(group)), BF16) for group in groups])


def assemble(place, landed, width):
    rows = landed[0].shape[0]
    blocks = [piece.shape[1] // width for piece in landed]

    def copy_kernel(place_ref, *refs):
        out_ref, sems, at, copies = refs[-2], refs[-1], 0, []
        for ref, count in zip(refs, blocks):
            for block in range(count):
                column = pl.multiple_of(place_ref[at] * width, width)
                source = ref.at[:, block * width : (block + 1) * width]
                copies.append(pltpu.make_async_copy(source, out_ref.at[:, pl.ds(column, width)], sems.at[at]))
                copies[-1].start()
                at += 1
        for copy in copies:
            copy.wait()

    if width % 128:
        out, at = jnp.zeros((rows, width * sum(blocks)), BF16), 0
        for piece, count in zip(landed, blocks):
            for block in range(count):
                part = piece[:, block * width : (block + 1) * width]
                out = lax.dynamic_update_slice_in_dim(out, part, place[at] * width, 1)
                at += 1
        return out
    placed = [pltpu.with_memory_space_constraint(piece, pltpu.VMEM) for piece in landed]
    return pl.pallas_call(
        copy_kernel,
        out_shape=jax.ShapeDtypeStruct((rows, width * sum(blocks)), BF16),
        in_specs=[FLAT] + [HERE] * len(landed),
        out_specs=pl.BlockSpec(memory_space=pltpu.HBM),
        scratch_shapes=[pltpu.SemaphoreType.DMA((sum(blocks),))],
        compiler_params=SMALL,
        name="assemble",
    )(place, *placed)


def level_states(made, depth):
    top = depth - 1
    state, own = [part[0] for part in made], [part[1] for part in made]
    near, side, corner = [None, None], [None, None], [None, None]
    side[0] = swap(own[1], 2)
    near[0] = swap(own[0], 1)
    side[1] = swap(own[0], 2)
    corner[0] = swap(side[0], 1)
    near[1] = swap(own[1], 1)
    corner[1] = swap(near[0], 2)
    first, last = [], []
    for part in range(2):
        sent, block = block_sum(state[part], near[part], side[part], corner[part])
        early, late = [near[part], side[part], corner[part]], []
        for level in range(2, top - 1):
            other = swap(sent, 1 << level)
            early.append(other)
            sent, block = add_block(block, other, 1)
        level = top - 1
        if part == 0:
            other = lift(sent, 1 << level | 1 << top, 0, 1 << level)
            early.append(other)
            late.append((lift(sent, 1 << level, 1 << top, 1 << level), level + 1))
            (sent,) = add_block(block, other, 0)
            below = 1 << top - 1
            after = lift(sent, 1 << top, below, 1 << top)
            close = lift(sent, 1 << top, below, 1 << top | below)
            (got,) = add_block(after, close, 0)
            late.append((got, top + 1))
        else:
            late.append((lift(sent, 1 << level, 0, 1 << level), level + 1))
            late.append((swap(got, 2), top + 1))
        first.append(early)
        last.append(late)
    return first, last


def shards(queries, keys, values, level_index, level_table, out_weight):
    rows = queries.shape[0]
    heads_here = level_table.shape[0]
    half = heads_here // 2
    position = lax.axis_index("seq")
    core = lax.axis_index("head")
    depth = lax.axis_size("seq").bit_length() - 1
    top = depth - 1
    token_bits, column_bits = groups(depth)

    flip = position >> 1 & 1

    turn = jnp.full((1,), flip, jnp.int32)
    made = states(turn, keys, values, half)
    split = out_weight.shape[0] * 5 // 8
    parts = order_rows(turn, out_weight, split)
    far = swap(parts[0], 1 << top)
    down = lift(parts[1], 0, 1 << top, 1 << top)
    up = lift(parts[1], 1 << top, 0, 1 << top)
    weights_of = {0: parts, 1 << top: (far, down, up)}
    for bit in column_bits:
        for mask in list(weights_of):
            new, got = mask | 1 << bit, []
            for at, part in enumerate(weights_of[mask]):
                if at == 0 or not mask & 1 << top:
                    got.append(swap(part, 1 << bit))
                else:
                    got.append(swap_some(part, 1 << bit, 1 << top, at - 1))
            weights_of[new] = tuple(got)
    first, last = level_states(made, depth)

    inv_root = 1.0 / math.sqrt(DH)
    roots = [inv_root / math.sqrt(rows)] + [inv_root / math.sqrt(rows * 2**level) for level in range(depth)]
    flags = [None] + [level if level < top - 1 else None for level in range(depth)]
    spot = jnp.full((1,), position, jnp.int32)
    scales = level_scales(turn, spot, level_index, level_table, roots, flags, half)
    normed = []
    for part in range(2):
        total = first_reads(turn, queries, keys, values, scales[part], first[part], half, part)
        normed.append(last_reads(turn, queries, scales[part], total, last[part], half, part))

    pieces = {0: tuple(normed)}
    for mask in masks_of(token_bits)[1:]:
        bits = [bit for bit in token_bits if mask >> bit & 1]
        got = []
        for part in range(2):
            bit = bits[0] if part else bits[-1]
            source = 1 - part if bit == 1 else part
            got.append(swap(pieces[mask ^ 1 << bit][source], 1 << bit))
        pieces[mask] = tuple(got)
    token_masks = sorted(pieces)
    tokens = [pieces[mask] for mask in token_masks]
    mine = ((position >> top & 1) == core).astype(jnp.int32)[None]
    column_masks = masks_of(column_bits)
    staged = {mask: both if len(both) == 2 else (both[0], merge(both[1], both[2])) for mask, both in weights_of.items()}
    width, count, low = out_weight.shape[1], len(token_masks), (1 << top) - 1
    keep, give = project(mine, tokens[:-1], [staged[0], staged[1 << top]], [(at, 0, 1) for at in range(count - 1)])
    got = swap_cores(give)
    out, blocks = [], []
    sums = add_cores(keep, got, rows, [[at] for at in range(count - 1)])
    for mask, piece in zip(token_masks, sums):
        out.append(swap(piece, mask) if mask else piece)
        blocks.append(mask)
    jobs, groups_of = [], [[] for _ in range(count)]
    for at, mask in enumerate(column_masks):
        for piece in range(count):
            if at or piece == count - 1:
                groups_of[piece].append(len(jobs))
                jobs.append((piece, 2 * at, 2 * at + 1))
    weights = [staged[full] for mask in column_masks for full in (mask, mask | 1 << top)]
    keep, give = project(mine, tokens, weights, jobs)
    got = swap_cores(give)
    for piece, part in enumerate(add_cores(keep, got, rows, groups_of)):
        mask = token_masks[piece]
        out.append(swap(part, mask) if mask else part)
        blocks += [mask | column_mask for column_mask in column_masks[piece < count - 1 :]]
    place = jnp.stack([position & low ^ block for block in blocks]).astype(jnp.int32)
    return assemble(place, out, width)


def solution(mesh):
    placed = (
        P("seq", "head"),
        P("seq", "head"),
        P("seq", "head"),
        P("seq", None),
        P("head", None),
        P("head", "seq"),
    )
    return jax.shard_map(
        shards, mesh=mesh, in_specs=placed, out_specs=P("seq", "head"), check_vma=False
    )
```

time: 151 us -> 142 us (0.940)
  starting transfers between devices: 74.1 us -> 54.6 us
  waiting for transfers between devices: 41.6 us -> 59.3 us
  Pallas kernels: 0 us -> 16.8 us
  matrix products: 14.3 us -> 0 us
  other arithmetic: 9.72 us -> 0 us
    ppermute x25 -> x22, starting transfers between devices: 64.8 us -> 24.4 us  [swap(): return lax.ppermute(value, 'seq', pairs)]
    ppermute x5 -> x7, waiting for transfers between devices: 9.03 us -> 32.2 us  [lift(): return lax.ppermute(value, 'seq', pairs)]
    pallas_call x0 -> x18, Pallas kernels: none -> 16.8 us  [the longest x15 12.6 us: local(): pl.pallas_call(kernel, out_shape=tuple((pltpu.VMEM(shape, dtype) for shap...]
    ppermute x5 -> x7, starting transfers between devices: 9.19 us -> 24.7 us  [lift(): return lax.ppermute(value, 'seq', pairs)]
    dot_general x21 -> x0, matrix products: 14.3 us -> none  [the longest x4 3.61 us: product(): jnp.dot(tokens[:, split:], second, preferred_element_type=jnp.float32)]
    concatenate x3 -> x0, other arithmetic: 7.22 us -> none  [the longest x1 4.77 us: shards(): jnp.concatenate([jnp.concatenate([pieces[mask][part] for part in range(2)...]
    ppermute x25 -> x22, waiting for transfers between devices: 32.6 us -> 27 us  [swap(): return lax.ppermute(value, 'seq', pairs)]
    unnamed x15 -> x53, local copies, waits for them, and re-layouts: 3.22 us -> 8.72 us
  transfers between devices with their start and end apart: 32 -> 33, of which waited for: 12 -> 12; matrix products, arithmetic and copies ran while one was open for 19% -> 1% of each run, Pallas kernels for 0% -> 8%
where the time goes in v2:
time: 142 us; the launch traced here: 140 us
  waiting for transfers between devices  59.3 us (42%)
  starting transfers between devices  54.6 us (38%)
  Pallas kernels  16.8 us (12%)
  local copies, waits for them, and re-layouts  8.8 us (6%)
    ppermute x7, waiting for transfers between devices, lift(): return lax.ppermute(value, 'seq', pairs)  32.2 us
    ppermute x22, waiting for transfers between devices, swap(): return lax.ppermute(value, 'seq', pairs)  27 us
    ppermute x7, starting transfers between devices, lift(): return lax.ppermute(value, 'seq', pairs)  24.7 us
    ppermute x22, starting transfers between devices, swap(): return lax.ppermute(value, 'seq', pairs)  24.4 us
    pallas_call x15, Pallas kernels, local(): pl.pallas_call(kernel, out_shape=tuple((pltpu.VMEM(shape, dtype) for shap...  12.6 us
    unnamed x53, local copies, waits for them, and re-layouts  8.72 us
    ppermute x2, starting transfers between devices, swap_some(): return lax.ppermute(value, 'seq', pairs)  4.81 us
  transfers between devices with their start and end apart: 33, of which 12 were waited for; matrix products, arithmetic and copies ran while one was open for 1% of the time, Pallas kernels for 8%

profile of v2, /device:TPU:0, one launch (start us, length us, event | category | flops | bytes accessed | tf_op | source)
XLA Modules:
  0.0 139.8 jit_solution(4404237729805904634)
XLA Ops:
  0.0 1.6 %state.1 = (f32[8,128,128]{2,1,0:T(8,128)S(1)}, bf16[8,128,128]{2,1,0:T(8,128)(2,1)S(1)}, f32[8,128,128]{2,1,0:T(8,128)S(1)}, bf16[8,128,128]{2,1,0:T(8,128)(2,1)S(1)}) custom-call(s32[1]{0:T(128)} %bitcast.9.flip_ref, bf16[128,2048]{1,0:T(8,128)(2,1)} %key_ref.3, bf16[128,2048]{1,0:T(8,128)(2,1)} %value_ref.3), custom_call_target="tpu_custom_call" | custom-call | tf_op jit(solution)/shard_map/state/pallas_call | solution.py:103
  1.6 3.1 %collective-permute-start.1 = (bf16[8,128,128]{2,1,0:T(8,128)(2,1)S(1)}, bf16[8,128,128]{2,1,0:T(8,128)(2,1)S(1)}, u32[]{:S(2)}, u32[]{:S(2)}) collective-permute-start(bf16[8,128,128]{2,1,0:T(8,128)(2,1)S(1)} %get-tuple-element.29), channel_id=1, source_target_pairs={{0,4},{2,6},{4,0},{6,2},{8,12},{10,14},{12,8},{14,10},{16,20},{18,... | collective-permute-start | bytes 786440 | tf_op jit(solution)/shard_map/ppermute | solution.py:15
  4.7 1.5 %collective-permute-start = (bf16[8,128,128]{2,1,0:T(8,128)(2,1)S(1)}, bf16[8,128,128]{2,1,0:T(8,128)(2,1)S(1)}, u32[]{:S(2)}, u32[]{:S(2)}) collective-permute-start(bf16[8,128,128]{2,1,0:T(8,128)(2,1)S(1)} %get-tuple-element.28), channel_id=1, source_target_pairs={{0,2},{2,0},{4,6},{6,4},{8,10},{10,8},{12,14},{14,12},{16,18},{18,... | collective-permute-start | bytes 786440 | tf_op jit(solution)/shard_map/ppermute | solution.py:15
  6.2 4.8 %collective-permute-done.1.side_ref.refs_1_ = bf16[8,128,128]{2,1,0:T(8,128)(2,1)S(1)} collective-permute-done((bf16[8,128,128]{2,1,0:T(8,128)(2,1)S(1)}, bf16[8,128,128]{2,1,0:T(8,128)(2,1)S(1)}, u32[]{:S(2)}, u32[]{:S(2)}) %collective-permute-start.1) | collective-permute-done | bytes 262176 | tf_op jit(solution)/shard_map/ppermute | solution.py:15
  11.0 1.7 %collective-permute-start.2 = (bf16[8,128,128]{2,1,0:T(8,128)(2,1)S(1)}, bf16[8,128,128]{2,1,0:T(8,128)(2,1)S(1)}, u32[]{:S(2)}, u32[]{:S(2)}) collective-permute-start(bf16[8,128,128]{2,1,0:T(8,128)(2,1)S(1)} %collective-permute-done.1.side_ref.refs_1_), channel_id=1, source_target_pairs={{0,2},{2,0},{4,6},{6,4},{8,10},{10,8},{12,14},{14,12},{16,18},{18,... | collective-permute-start | bytes 786440 | tf_op jit(solution)/shard_map/ppermute | solution.py:15
  12.7 5.8 %collective-permute-done.2.corner_ref.refs_2_ = bf16[8,128,128]{2,1,0:T(8,128)(2,1)S(1)} collective-permute-done((bf16[8,128,128]{2,1,0:T(8,128)(2,1)S(1)}, bf16[8,128,128]{2,1,0:T(8,128)(2,1)S(1)}, u32[]{:S(2)}, u32[]{:S(2)}) %collective-permute-start.2) | collective-permute-done | bytes 262176 | tf_op jit(solution)/shard_map/ppermute | solution.py:15
  19.1 3.4 %collective-permute-start.3 = (bf16[8,128,128]{2,1,0:T(8,128)(2,1)S(1)}, bf16[8,128,128]{2,1,0:T(8,128)(2,1)S(1)}, u32[]{:S(2)}, u32[]{:S(2)}) collective-permute-start(bf16[8,128,128]{2,1,0:T(8,128)(2,1)S(1)} %get-tuple-element.31), channel_id=1, source_target_pairs={{0,8},{2,10},{4,12},{6,14},{1,9},{3,11},{5,13},{7,15}} | collective-permute-start | bytes 786440 | tf_op jit(solution)/shard_map/ppermute | solution.py:24
  22.6 1.6 %collective-permute-start.7 = (bf16[8,128,128]{2,1,0:T(8,128)(2,1)S(1)}, bf16[8,128,128]{2,1,0:T(8,128)(2,1)S(1)}, u32[]{:S(2)}, u32[]{:S(2)}) collective-permute-start(bf16[8,128,128]{2,1,0:T(8,128)(2,1)S(1)} %get-tuple-element.29), channel_id=1, source_target_pairs={{0,2},{2,0},{4,6},{6,4},{8,10},{10,8},{12,14},{14,12},{16,18},{18,... | collective-permute-start | bytes 786440 | tf_op jit(solution)/shard_map/ppermute | solution.py:15
  24.1 1.5 %collective-permute-start.8 = (bf16[8,128,128]{2,1,0:T(8,128)(2,1)S(1)}, bf16[8,128,128]{2,1,0:T(8,128)(2,1)S(1)}, u32[]{:S(2)}, u32[]{:S(2)}) collective-permute-start(bf16[8,128,128]{2,1,0:T(8,128)(2,1)S(1)} %get-tuple-element.28), channel_id=1, source_target_pairs={{0,4},{2,6},{4,0},{6,2},{8,12},{10,14},{12,8},{14,10},{16,20},{18,... | collective-permute-start | bytes 786440 | tf_op jit(solution)/shard_map/ppermute | solution.py:15
  29.6 1.3 collective-permute-start.17
  30.9 1.8 %collective-permute-done.8.refs_1_.side_ref = bf16[8,128,128]{2,1,0:T(8,128)(2,1)S(1)} collective-permute-done((bf16[8,128,128]{2,1,0:T(8,128)(2,1)S(1)}, bf16[8,128,128]{2,1,0:T(8,128)(2,1)S(1)}, u32[]{:S(2)}, u32[]{:S(2)}) %collective-permute-start.8) | collective-permute-done | bytes 262176 | tf_op jit(solution)/shard_map/ppermute | solution.py:15
  32.7 5.2 %collective-permute-start.18 = (bf16[768,256]{1,0:T(8,128)(2,1)S(1)}, bf16[768,256]{1,0:T(8,128)(2,1)}, u32[]{:S(2)}, u32[]{:S(2)}) collective-permute-start(bf16[768,256]{1,0:T(8,128)(2,1)S(1)} %get-tuple-element.37.refs_7_.refs_9_), channel_id=1, source_target_pairs={{0,16},{2,18},{4,20},{6,22},{8,24},{10,26},{12,28},{14,30},{1,17},... | collective-permute-start | bytes 1179656 | tf_op jit(solution)/shard_map/ppermute | solution.py:24
  38.6 2.5 %collective-permute-start.24 = (bf16[1280,256]{1,0:T(8,128)(2,1)S(1)}, bf16[1280,256]{1,0:T(8,128)(2,1)}, u32[]{:S(2)}, u32[]{:S(2)}) collective-permute-start(bf16[1280,256]{1,0:T(8,128)(2,1)S(1)} %get-tuple-element.36.refs_6_.refs_8_), channel_id=1, source_target_pairs={{0,2},{2,0},{4,6},{6,4},{8,10},{10,8},{12,14},{14,12},{16,18},{18,... | collective-permute-start | bytes 1966088 | tf_op jit(solution)/shard_map/ppermute | solution.py:15
  42.2 29.7 %collective-permute-done.17.down_ref = bf16[768,256]{1,0:T(8,128)(2,1)} collective-permute-done((bf16[768,256]{1,0:T(8,128)(2,1)S(1)}, bf16[768,256]{1,0:T(8,128)(2,1)}, u32[]{:S(2)}, u32[]{:S(2)}) %collective-permute-start.17) | collective-permute-done | bytes 393248 | tf_op jit(solution)/shard_map/ppermute | solution.py:24
  71.9 12.8 %collective-permute-start.10 = (bf16[8,128,128]{2,1,0:T(8,128)(2,1)S(1)}, bf16[8,128,128]{2,1,0:T(8,128)(2,1)S(1)}, u32[]{:S(2)}, u32[]{:S(2)}) collective-permute-start(bf16[8,128,128]{2,1,0:T(8,128)(2,1)S(1)} %get-tuple-element.35), channel_id=1, source_target_pairs={{0,8},{2,10},{4,12},{6,14},{16,24},{18,26},{20,28},{22,30},{1,9},{... | collective-permute-start | bytes 786440 | tf_op jit(solution)/shard_map/ppermute | solution.py:24
  86.7 1.9 %collective-permute-done.10.refs_0_ = bf16[8,128,128]{2,1,0:T(8,128)(2,1)S(1)} collective-permute-done((bf16[8,128,128]{2,1,0:T(8,128)(2,1)S(1)}, bf16[8,128,128]{2,1,0:T(8,128)(2,1)S(1)}, u32[]{:S(2)}, u32[]{:S(2)}) %collective-permute-start.10) | collective-permute-done | bytes 262176 | tf_op jit(solution)/shard_map/ppermute | solution.py:24
  89.3 3.4 %collective-permute-start.27 = (bf16[768,256]{1,0:T(8,128)(2,1)}, bf16[768,256]{1,0:T(8,128)(2,1)}, u32[]{:S(2)}, u32[]{:S(2)}) collective-permute-start(bf16[768,256]{1,0:T(8,128)(2,1)} %collective-permute-done.17.down_ref), channel_id=1, source_target_pairs={{0,2},{2,0},{4,6},{6,4},{8,10},{10,8},{12,14},{14,12},{1,3},{3,1},... | collective-permute-start | bytes 1179656 | tf_op jit(solution)/shard_map/ppermute | solution.py:33
  93.4 1.4 %collective-permute-start.28 = (bf16[768,256]{1,0:T(8,128)(2,1)}, bf16[768,256]{1,0:T(8,128)(2,1)}, u32[]{:S(2)}, u32[]{:S(2)}) collective-permute-start(bf16[768,256]{1,0:T(8,128)(2,1)} %collective-permute-done.18.up_ref), channel_id=1, source_target_pairs={{16,18},{18,16},{20,22},{22,20},{24,26},{26,24},{28,30},{30,28},{1... | collective-permute-start | bytes 1179656 | tf_op jit(solution)/shard_map/ppermute | solution.py:33
  101.2 1.4 shard_map.70.total_ref
  105.8 2.5 %collective-permute-start.14 = (bf16[128,1024]{1,0:T(8,128)(2,1)S(1)}, bf16[128,1024]{1,0:T(8,128)(2,1)S(1)}, u32[]{:S(2)}, u32[]{:S(2)}) collective-permute-start(bf16[128,1024]{1,0:T(8,128)(2,1)S(1)} %shard_map.69.refs_0_), channel_id=1, source_target_pairs={{0,8},{2,10},{4,12},{6,14},{8,0},{10,2},{12,4},{14,6},{16,24},{18,... | collective-permute-start | bytes 786440 | tf_op jit(solution)/shard_map/ppermute | solution.py:15
  108.9 1.5 %collective-permute-start.13 = (bf16[128,1024]{1,0:T(8,128)(2,1)S(1)}, bf16[128,1024]{1,0:T(8,128)(2,1)S(1)}, u32[]{:S(2)}, u32[]{:S(2)}) collective-permute-start(bf16[128,1024]{1,0:T(8,128)(2,1)S(1)} %shard_map.69.refs_0_), channel_id=1, source_target_pairs={{0,4},{2,6},{4,0},{6,2},{8,12},{10,14},{12,8},{14,10},{16,20},{18,... | collective-permute-start | bytes 786440 | tf_op jit(solution)/shard_map/ppermute | solution.py:15
  110.5 5.0 %collective-permute-done.14.refs_4_ = bf16[128,1024]{1,0:T(8,128)(2,1)S(1)} collective-permute-done((bf16[128,1024]{1,0:T(8,128)(2,1)S(1)}, bf16[128,1024]{1,0:T(8,128)(2,1)S(1)}, u32[]{:S(2)}, u32[]{:S(2)}) %collective-permute-start.14) | collective-permute-done | bytes 262176 | tf_op jit(solution)/shard_map/ppermute | solution.py:15
  116.0 1.5 %collective-permute-done.12.refs_2_ = bf16[128,1024]{1,0:T(8,128)(2,1)S(1)} collective-permute-done((bf16[128,1024]{1,0:T(8,128)(2,1)S(1)}, bf16[128,1024]{1,0:T(8,128)(2,1)S(1)}, u32[]{:S(2)}, u32[]{:S(2)}) %collective-permute-start.12) | collective-permute-done | bytes 262176 | tf_op jit(solution)/shard_map/ppermute | solution.py:15
  120.0 1.4 %collective-permute-done.13.refs_3_ = bf16[128,1024]{1,0:T(8,128)(2,1)S(1)} collective-permute-done((bf16[128,1024]{1,0:T(8,128)(2,1)S(1)}, bf16[128,1024]{1,0:T(8,128)(2,1)S(1)}, u32[]{:S(2)}, u32[]{:S(2)}) %collective-permute-start.13) | collective-permute-done | bytes 262176 | tf_op jit(solution)/shard_map/ppermute | solution.py:15
  121.5 2.8 %collective-permute-done.23.refs_7_ = bf16[128,1024]{1,0:T(8,128)(2,1)S(1)} collective-permute-done((bf16[128,1024]{1,0:T(8,128)(2,1)S(1)}, bf16[128,1024]{1,0:T(8,128)(2,1)S(1)}, u32[]{:S(2)}, u32[]{:S(2)}) %collective-permute-start.23) | collective-permute-done | bytes 262176 | tf_op jit(solution)/shard_map/ppermute | solution.py:15
  124.3 3.0 %shard_map.77 = (f32[640,256]{1,0:T(8,128)S(1)}, bf16[640,256]{1,0:T(8,128)(2,1)S(1)}) custom-call(s32[1]{0:T(128)} %bitcast.8.mine_ref, bf16[128,1024]{1,0:T(8,128)(2,1)S(1)} %shard_map.69.refs_0_, bf16[128,1024]{1,0:T(8,128)(2,1)S(1)} %shard_map.72.refs_1_, bf16[128,1024]{1,0:T(8,128)(2,1)S(1)} %collective-permute-done.12.refs_2_, ...), custom_call_target="tpu_custom_call" | custom-call | tf_op jit(solution)/shard_map/pallas_call | solution.py:62
  129.1 1.3 collective-permute-start.32
  131.1 1.6 %collective-permute-start.21 = (bf16[128,256]{1,0:T(8,128)(2,1)S(1)}, bf16[128,256]{1,0:T(8,128)(2,1)S(1)}, u32[]{:S(2)}, u32[]{:S(2)}) collective-permute-start(bf16[128,256]{1,0:T(8,128)(2,1)S(1)} %get-tuple-element.42), channel_id=1, source_target_pairs={{0,8},{2,10},{4,12},{6,14},{8,0},{10,2},{12,4},{14,6},{16,24},{18,... | collective-permute-start | bytes 196616 | tf_op jit(solution)/shard_map/ppermute | solution.py:15
  133.0 1.5 %collective-permute-start.31 = (bf16[128,256]{1,0:T(8,128)(2,1)S(1)}, bf16[128,256]{1,0:T(8,128)(2,1)S(1)}, u32[]{:S(2)}, u32[]{:S(2)}) collective-permute-start(bf16[128,256]{1,0:T(8,128)(2,1)S(1)} %get-tuple-element.47), channel_id=1, source_target_pairs={{0,8},{2,10},{4,12},{6,14},{8,0},{10,2},{12,4},{14,6},{16,24},{18,... | collective-permute-start | bytes 196616 | tf_op jit(solution)/shard_map/ppermute | solution.py:15
  134.6 2.5 %collective-permute-done.20.refs_1_ = bf16[128,256]{1,0:T(8,128)(2,1)S(1)} collective-permute-done((bf16[128,256]{1,0:T(8,128)(2,1)S(1)}, bf16[128,256]{1,0:T(8,128)(2,1)S(1)}, u32[]{:S(2)}, u32[]{:S(2)}) %collective-permute-start.20) | collective-permute-done | bytes 65568 | tf_op jit(solution)/shard_map/ppermute | solution.py:15
  137.1 1.3 collective-permute-done.30.refs_4_
  138.4 1.4 assemble.1
  (106 shorter events, 25.7 us)
Async XLA Ops:
  1.6 9.4 %collective-permute-start.1 = (bf16[8,128,128]{2,1,0:T(8,128)(2,1)S(1)}, bf16[8,128,128]{2,1,0:T(8,128)(2,1)S(1)}, u32[]{:S(2)}, u32[]{:S(2)}) collective-permute-start(bf16[8,128,128]{2,1,0:T(8,128)(2,1)S(1)} %get-tuple-element.29), channel_id=1, source_target_pairs={{0,4},{2,6},{4,0},{6,2},{8,12},{10,14},{12,8},{14,10},{16,20},{18,... | collective-permute-start | bytes 786440 | tf_op jit(solution)/shard_map/ppermute | solution.py:15
  4.7 8.0 %collective-permute-start = (bf16[8,128,128]{2,1,0:T(8,128)(2,1)S(1)}, bf16[8,128,128]{2,1,0:T(8,128)(2,1)S(1)}, u32[]{:S(2)}, u32[]{:S(2)}) collective-permute-start(bf16[8,128,128]{2,1,0:T(8,128)(2,1)S(1)} %get-tuple-element.28), channel_id=1, source_target_pairs={{0,2},{2,0},{4,6},{6,4},{8,10},{10,8},{12,14},{14,12},{16,18},{18,... | collective-permute-start | bytes 786440 | tf_op jit(solution)/shard_map/ppermute | solution.py:15
  11.0 7.5 %collective-permute-start.2 = (bf16[8,128,128]{2,1,0:T(8,128)(2,1)S(1)}, bf16[8,128,128]{2,1,0:T(8,128)(2,1)S(1)}, u32[]{:S(2)}, u32[]{:S(2)}) collective-permute-start(bf16[8,128,128]{2,1,0:T(8,128)(2,1)S(1)} %collective-permute-done.1.side_ref.refs_1_), channel_id=1, source_target_pairs={{0,2},{2,0},{4,6},{6,4},{8,10},{10,8},{12,14},{14,12},{16,18},{18,... | collective-permute-start | bytes 786440 | tf_op jit(solution)/shard_map/ppermute | solution.py:15
  19.1 9.1 %collective-permute-start.3 = (bf16[8,128,128]{2,1,0:T(8,128)(2,1)S(1)}, bf16[8,128,128]{2,1,0:T(8,128)(2,1)S(1)}, u32[]{:S(2)}, u32[]{:S(2)}) collective-permute-start(bf16[8,128,128]{2,1,0:T(8,128)(2,1)S(1)} %get-tuple-element.31), channel_id=1, source_target_pairs={{0,8},{2,10},{4,12},{6,14},{1,9},{3,11},{5,13},{7,15}} | collective-permute-start | bytes 786440 | tf_op jit(solution)/shard_map/ppermute | solution.py:24
  22.6 7.0 %collective-permute-start.7 = (bf16[8,128,128]{2,1,0:T(8,128)(2,1)S(1)}, bf16[8,128,128]{2,1,0:T(8,128)(2,1)S(1)}, u32[]{:S(2)}, u32[]{:S(2)}) collective-permute-start(bf16[8,128,128]{2,1,0:T(8,128)(2,1)S(1)} %get-tuple-element.29), channel_id=1, source_target_pairs={{0,2},{2,0},{4,6},{6,4},{8,10},{10,8},{12,14},{14,12},{16,18},{18,... | collective-permute-start | bytes 786440 | tf_op jit(solution)/shard_map/ppermute | solution.py:15
  24.1 8.6 %collective-permute-start.8 = (bf16[8,128,128]{2,1,0:T(8,128)(2,1)S(1)}, bf16[8,128,128]{2,1,0:T(8,128)(2,1)S(1)}, u32[]{:S(2)}, u32[]{:S(2)}) collective-permute-start(bf16[8,128,128]{2,1,0:T(8,128)(2,1)S(1)} %get-tuple-element.28), channel_id=1, source_target_pairs={{0,4},{2,6},{4,0},{6,2},{8,12},{10,14},{12,8},{14,10},{16,20},{18,... | collective-permute-start | bytes 786440 | tf_op jit(solution)/shard_map/ppermute | solution.py:15
  26.9 58.5 %collective-permute-start.16 = (bf16[1280,256]{1,0:T(8,128)(2,1)S(1)}, bf16[1280,256]{1,0:T(8,128)(2,1)S(1)}, u32[]{:S(2)}, u32[]{:S(2)}) collective-permute-start(bf16[1280,256]{1,0:T(8,128)(2,1)S(1)} %get-tuple-element.36.refs_6_.refs_8_), channel_id=1, source_target_pairs={{0,16},{2,18},{4,20},{6,22},{8,24},{10,26},{12,28},{14,30},{16,0},... | collective-permute-start | bytes 1966088 | tf_op jit(solution)/shard_map/ppermute | solution.py:15
  27.0 10.9 %collective-permute-start.9 = (bf16[8,128,128]{2,1,0:T(8,128)(2,1)S(1)}, bf16[8,128,128]{2,1,0:T(8,128)(2,1)S(1)}, u32[]{:S(2)}, u32[]{:S(2)}) collective-permute-start(bf16[8,128,128]{2,1,0:T(8,128)(2,1)S(1)} %collective-permute-done.near_ref.refs_0_), channel_id=1, source_target_pairs={{0,4},{2,6},{4,0},{6,2},{8,12},{10,14},{12,8},{14,10},{16,20},{18,... | collective-permute-start | bytes 786440 | tf_op jit(solution)/shard_map/ppermute | solution.py:15
  28.9 9.6 %collective-permute-start.5 = (bf16[8,128,128]{2,1,0:T(8,128)(2,1)S(1)}, bf16[8,128,128]{2,1,0:T(8,128)(2,1)S(1)}, u32[]{:S(2)}, u32[]{:S(2)}) collective-permute-start(bf16[8,128,128]{2,1,0:T(8,128)(2,1)S(1)} %shard_map.67), channel_id=1, source_target_pairs={{8,24},{10,26},{12,28},{14,30},{9,25},{11,27},{13,29},{15,31}} | collective-permute-start | bytes 786440 | tf_op jit(solution)/shard_map/ppermute | solution.py:24
  29.6 42.2 %collective-permute-start.17 = (bf16[768,256]{1,0:T(8,128)(2,1)S(1)}, bf16[768,256]{1,0:T(8,128)(2,1)}, u32[]{:S(2)}, u32[]{:S(2)}) collective-permute-start(bf16[768,256]{1,0:T(8,128)(2,1)S(1)} %get-tuple-element.37.refs_7_.refs_9_), channel_id=1, source_target_pairs={{16,0},{18,2},{20,4},{22,6},{24,8},{26,10},{28,12},{30,14},{17,1},... | collective-permute-start | bytes 1179656 | tf_op jit(solution)/shard_map/ppermute | solution.py:24
  32.7 52.0 %collective-permute-start.18 = (bf16[768,256]{1,0:T(8,128)(2,1)S(1)}, bf16[768,256]{1,0:T(8,128)(2,1)}, u32[]{:S(2)}, u32[]{:S(2)}) collective-permute-start(bf16[768,256]{1,0:T(8,128)(2,1)S(1)} %get-tuple-element.37.refs_7_.refs_9_), channel_id=1, source_target_pairs={{0,16},{2,18},{4,20},{6,22},{8,24},{10,26},{12,28},{14,30},{1,17},... | collective-permute-start | bytes 1179656 | tf_op jit(solution)/shard_map/ppermute | solution.py:24
  37.9 4.1 %collective-permute-start.6 = (bf16[8,128,128]{2,1,0:T(8,128)(2,1)S(1)}, bf16[8,128,128]{2,1,0:T(8,128)(2,1)S(1)}, u32[]{:S(2)}, u32[]{:S(2)}) collective-permute-start(bf16[8,128,128]{2,1,0:T(8,128)(2,1)S(1)} %shard_map.67), channel_id=1, source_target_pairs={{8,16},{10,18},{12,20},{14,22},{9,17},{11,19},{13,21},{15,23}} | collective-permute-start | bytes 786440 | tf_op jit(solution)/shard_map/ppermute | solution.py:24
  38.6 69.8 %collective-permute-start.24 = (bf16[1280,256]{1,0:T(8,128)(2,1)S(1)}, bf16[1280,256]{1,0:T(8,128)(2,1)}, u32[]{:S(2)}, u32[]{:S(2)}) collective-permute-start(bf16[1280,256]{1,0:T(8,128)(2,1)S(1)} %get-tuple-element.36.refs_6_.refs_8_), channel_id=1, source_target_pairs={{0,2},{2,0},{4,6},{6,4},{8,10},{10,8},{12,14},{14,12},{16,18},{18,... | collective-permute-start | bytes 1966088 | tf_op jit(solution)/shard_map/ppermute | solution.py:15
  42.0 63.8 %collective-permute-start.25 = (bf16[768,256]{1,0:T(8,128)(2,1)S(1)}, bf16[768,256]{1,0:T(8,128)(2,1)}, u32[]{:S(2)}, u32[]{:S(2)}) collective-permute-start(bf16[768,256]{1,0:T(8,128)(2,1)S(1)} %get-tuple-element.37.refs_7_.refs_9_), channel_id=1, source_target_pairs={{0,2},{2,0},{4,6},{6,4},{8,10},{10,8},{12,14},{14,12},{16,18},{18,... | collective-permute-start | bytes 1179656 | tf_op jit(solution)/shard_map/ppermute | solution.py:15
  71.9 16.7 %collective-permute-start.10 = (bf16[8,128,128]{2,1,0:T(8,128)(2,1)S(1)}, bf16[8,128,128]{2,1,0:T(8,128)(2,1)S(1)}, u32[]{:S(2)}, u32[]{:S(2)}) collective-permute-start(bf16[8,128,128]{2,1,0:T(8,128)(2,1)S(1)} %get-tuple-element.35), channel_id=1, source_target_pairs={{0,8},{2,10},{4,12},{6,14},{16,24},{18,26},{20,28},{22,30},{1,9},{... | collective-permute-start | bytes 786440 | tf_op jit(solution)/shard_map/ppermute | solution.py:24
  84.7 8.0 %collective-permute-start.4 = (bf16[8,128,128]{2,1,0:T(8,128)(2,1)S(1)}, bf16[8,128,128]{2,1,0:T(8,128)(2,1)S(1)}, u32[]{:S(2)}, u32[]{:S(2)}) collective-permute-start(bf16[8,128,128]{2,1,0:T(8,128)(2,1)S(1)} %get-tuple-element.31), channel_id=1, source_target_pairs={{16,24},{18,26},{20,28},{22,30},{17,25},{19,27},{21,29},{23,31}} | collective-permute-start | bytes 786440 | tf_op jit(solution)/shard_map/ppermute | solution.py:24
  85.4 9.4 %collective-permute-start.11 = (bf16[8,128,128]{2,1,0:T(8,128)(2,1)S(1)}, bf16[8,128,128]{2,1,0:T(8,128)(2,1)S(1)}, u32[]{:S(2)}, u32[]{:S(2)}) collective-permute-start(bf16[8,128,128]{2,1,0:T(8,128)(2,1)S(1)} %shard_map.68.refs_1_), channel_id=1, source_target_pairs={{0,4},{2,6},{4,0},{6,2},{8,12},{10,14},{12,8},{14,10},{16,20},{18,... | collective-permute-start | bytes 786440 | tf_op jit(solution)/shard_map/ppermute | solution.py:15
  89.3 19.6 %collective-permute-start.27 = (bf16[768,256]{1,0:T(8,128)(2,1)}, bf16[768,256]{1,0:T(8,128)(2,1)}, u32[]{:S(2)}, u32[]{:S(2)}) collective-permute-start(bf16[768,256]{1,0:T(8,128)(2,1)} %collective-permute-done.17.down_ref), channel_id=1, source_target_pairs={{0,2},{2,0},{4,6},{6,4},{8,10},{10,8},{12,14},{14,12},{1,3},{3,1},... | collective-permute-start | bytes 1179656 | tf_op jit(solution)/shard_map/ppermute | solution.py:33
  93.4 17.0 %collective-permute-start.28 = (bf16[768,256]{1,0:T(8,128)(2,1)}, bf16[768,256]{1,0:T(8,128)(2,1)}, u32[]{:S(2)}, u32[]{:S(2)}) collective-permute-start(bf16[768,256]{1,0:T(8,128)(2,1)} %collective-permute-done.18.up_ref), channel_id=1, source_target_pairs={{16,18},{18,16},{20,22},{22,20},{24,26},{26,24},{28,30},{30,28},{1... | collective-permute-start | bytes 1179656 | tf_op jit(solution)/shard_map/ppermute | solution.py:33
  95.5 26.0 %collective-permute-start.26 = (bf16[1280,256]{1,0:T(8,128)(2,1)S(1)}, bf16[1280,256]{1,0:T(8,128)(2,1)}, u32[]{:S(2)}, u32[]{:S(2)}) collective-permute-start(bf16[1280,256]{1,0:T(8,128)(2,1)S(1)} %collective-permute-done.16.refs_8_.refs_10_), channel_id=1, source_target_pairs={{0,2},{2,0},{4,6},{6,4},{8,10},{10,8},{12,14},{14,12},{16,18},{18,... | collective-permute-start | bytes 1966088 | tf_op jit(solution)/shard_map/ppermute | solution.py:15
  105.8 9.7 %collective-permute-start.14 = (bf16[128,1024]{1,0:T(8,128)(2,1)S(1)}, bf16[128,1024]{1,0:T(8,128)(2,1)S(1)}, u32[]{:S(2)}, u32[]{:S(2)}) collective-permute-start(bf16[128,1024]{1,0:T(8,128)(2,1)S(1)} %shard_map.69.refs_0_), channel_id=1, source_target_pairs={{0,8},{2,10},{4,12},{6,14},{8,0},{10,2},{12,4},{14,6},{16,24},{18,... | collective-permute-start | bytes 786440 | tf_op jit(solution)/shard_map/ppermute | solution.py:15
  108.4 9.2 %collective-permute-start.12 = (bf16[128,1024]{1,0:T(8,128)(2,1)S(1)}, bf16[128,1024]{1,0:T(8,128)(2,1)S(1)}, u32[]{:S(2)}, u32[]{:S(2)}) collective-permute-start(bf16[128,1024]{1,0:T(8,128)(2,1)S(1)} %shard_map.72.refs_1_), channel_id=1, source_target_pairs={{0,4},{2,6},{4,0},{6,2},{8,12},{10,14},{12,8},{14,10},{16,20},{18,... | collective-permute-start | bytes 786440 | tf_op jit(solution)/shard_map/ppermute | solution.py:15
  108.9 12.6 %collective-permute-start.13 = (bf16[128,1024]{1,0:T(8,128)(2,1)S(1)}, bf16[128,1024]{1,0:T(8,128)(2,1)S(1)}, u32[]{:S(2)}, u32[]{:S(2)}) collective-permute-start(bf16[128,1024]{1,0:T(8,128)(2,1)S(1)} %shard_map.69.refs_0_), channel_id=1, source_target_pairs={{0,4},{2,6},{4,0},{6,2},{8,12},{10,14},{12,8},{14,10},{16,20},{18,... | collective-permute-start | bytes 786440 | tf_op jit(solution)/shard_map/ppermute | solution.py:15
  110.4 11.1 %collective-permute-start.15 = (bf16[128,1024]{1,0:T(8,128)(2,1)S(1)}, bf16[128,1024]{1,0:T(8,128)(2,1)S(1)}, u32[]{:S(2)}, u32[]{:S(2)}) collective-permute-start(bf16[128,1024]{1,0:T(8,128)(2,1)S(1)} %shard_map.72.refs_1_), channel_id=1, source_target_pairs={{0,8},{2,10},{4,12},{6,14},{8,0},{10,2},{12,4},{14,6},{16,24},{18,... | collective-permute-start | bytes 786440 | tf_op jit(solution)/shard_map/ppermute | solution.py:15
  115.5 8.8 %collective-permute-start.23 = (bf16[128,1024]{1,0:T(8,128)(2,1)S(1)}, bf16[128,1024]{1,0:T(8,128)(2,1)S(1)}, u32[]{:S(2)}, u32[]{:S(2)}) collective-permute-start(bf16[128,1024]{1,0:T(8,128)(2,1)S(1)} %collective-permute-done.14.refs_4_), channel_id=1, source_target_pairs={{0,4},{2,6},{4,0},{6,2},{8,12},{10,14},{12,8},{14,10},{16,20},{18,... | collective-permute-start | bytes 786440 | tf_op jit(solution)/shard_map/ppermute | solution.py:15
  117.5 6.8 %collective-permute-start.22 = (bf16[128,1024]{1,0:T(8,128)(2,1)S(1)}, bf16[128,1024]{1,0:T(8,128)(2,1)}, u32[]{:S(2)}, u32[]{:S(2)}) collective-permute-start(bf16[128,1024]{1,0:T(8,128)(2,1)S(1)} %collective-permute-done.12.refs_2_), channel_id=1, source_target_pairs={{0,8},{2,10},{4,12},{6,14},{8,0},{10,2},{12,4},{14,6},{16,24},{18,... | collective-permute-start | bytes 786440 | tf_op jit(solution)/shard_map/ppermute | solution.py:15
  128.4 2.0 %collective-permute-start.19 = (bf16[384,256]{1,0:T(8,128)(2,1)S(1)}, bf16[384,256]{1,0:T(8,128)(2,1)S(1)}, u32[]{:S(2)}, u32[]{:S(2)}) collective-permute-start(bf16[384,256]{1,0:T(8,128)(2,1)S(1)} %get-tuple-element.39), channel_id=1, source_target_pairs={{0,1},{1,0},{2,3},{3,2},{4,5},{5,4},{6,7},{7,6},{8,9},{9,8},{10,11... | collective-permute-start | bytes 589832 | tf_op jit(solution)/shard_map/ppermute | solution.py:37
  129.1 9.3 %collective-permute-start.32 = (bf16[128,512]{1,0:T(8,128)(2,1)S(1)}, bf16[128,512]{1,0:T(8,128)(2,1)S(1)}, u32[]{:S(2)}, u32[]{:S(2)}) collective-permute-start(bf16[128,512]{1,0:T(8,128)(2,1)S(1)} %get-tuple-element.48), channel_id=1, source_target_pairs={{0,12},{2,14},{4,8},{6,10},{8,4},{10,6},{12,0},{14,2},{16,28},{18,... | collective-permute-start | bytes 393224 | tf_op jit(solution)/shard_map/ppermute | solution.py:15
  130.4 6.7 %collective-permute-start.20 = (bf16[128,256]{1,0:T(8,128)(2,1)S(1)}, bf16[128,256]{1,0:T(8,128)(2,1)S(1)}, u32[]{:S(2)}, u32[]{:S(2)}) collective-permute-start(bf16[128,256]{1,0:T(8,128)(2,1)S(1)} %get-tuple-element.41), channel_id=1, source_target_pairs={{0,4},{2,6},{4,0},{6,2},{8,12},{10,14},{12,8},{14,10},{16,20},{18,... | collective-permute-start | bytes 196616 | tf_op jit(solution)/shard_map/ppermute | solution.py:15
  131.1 6.0 %collective-permute-start.21 = (bf16[128,256]{1,0:T(8,128)(2,1)S(1)}, bf16[128,256]{1,0:T(8,128)(2,1)S(1)}, u32[]{:S(2)}, u32[]{:S(2)}) collective-permute-start(bf16[128,256]{1,0:T(8,128)(2,1)S(1)} %get-tuple-element.42), channel_id=1, source_target_pairs={{0,8},{2,10},{4,12},{6,14},{8,0},{10,2},{12,4},{14,6},{16,24},{18,... | collective-permute-start | bytes 196616 | tf_op jit(solution)/shard_map/ppermute | solution.py:15
  132.8 5.6 %collective-permute-start.30 = (bf16[128,256]{1,0:T(8,128)(2,1)S(1)}, bf16[128,256]{1,0:T(8,128)(2,1)S(1)}, u32[]{:S(2)}, u32[]{:S(2)}) collective-permute-start(bf16[128,256]{1,0:T(8,128)(2,1)S(1)} %get-tuple-element.46), channel_id=1, source_target_pairs={{0,4},{2,6},{4,0},{6,2},{8,12},{10,14},{12,8},{14,10},{16,20},{18,... | collective-permute-start | bytes 196616 | tf_op jit(solution)/shard_map/ppermute | solution.py:15
  133.0 5.4 %collective-permute-start.31 = (bf16[128,256]{1,0:T(8,128)(2,1)S(1)}, bf16[128,256]{1,0:T(8,128)(2,1)S(1)}, u32[]{:S(2)}, u32[]{:S(2)}) collective-permute-start(bf16[128,256]{1,0:T(8,128)(2,1)S(1)} %get-tuple-element.47), channel_id=1, source_target_pairs={{0,8},{2,10},{4,12},{6,14},{8,0},{10,2},{12,4},{14,6},{16,24},{18,... | collective-permute-start | bytes 196616 | tf_op jit(solution)/shard_map/ppermute | solution.py:15
  (27 other events, 307.7 us)

commit v3 on v2

--- a/solution.py
+++ b/solution.py
@@ -57,13 +57,14 @@
 F32, BF16 = jnp.float32, jnp.bfloat16
 
 
-def local(kernel, scalars, operands, results):
+def local(kernel, scalars, operands, results, spare=()):
     placed = [pltpu.with_memory_space_constraint(operand, pltpu.VMEM) for operand in operands]
     return pl.pallas_call(
         kernel,
         out_shape=tuple(pltpu.VMEM(shape, dtype) for shape, dtype in results),
         in_specs=[FLAT] * len(scalars) + [HERE] * len(operands),
         out_specs=tuple(HERE for _ in results),
+        scratch_shapes=[pltpu.VMEM(shape, BF16) for shape in spare],
         compiler_params=SMALL,
     )(*scalars, *placed)
 
@@ -116,13 +117,6 @@
     return [made[2:], made[:2]]
 
 
-def merge(down, up):
-    def kernel(down_ref, up_ref, out_ref):
-        out_ref[...] = down_ref[...] + up_ref[...]
-
-    return local(kernel, [], [down, up], [(down.shape, BF16)])[0]
-
-
 def order_rows(flip, weight, split):
     depth, width = weight.shape
     half = depth // 2
@@ -160,20 +154,20 @@
 
 
 def level_scales(flip, position, level_index, level_table, roots, flags, half):
-    rows, values = level_index.shape[0], level_table.shape[1]
+    rows, values = level_index.shape[1], level_table.shape[1]
 
     def kernel(flip_ref, position_ref, index_ref, table_ref, *out_refs):
         for part, out_ref in enumerate(out_refs):
             start = pl.multiple_of(jnp.where(flip_ref[0] == part, 0, half), half)
             table = table_ref[pl.ds(start, half), :]
             for level, root in enumerate(roots):
-                chosen = index_ref[:, level : level + 1] == lax.broadcasted_iota(
-                    jnp.int32, (rows, values), 1
+                chosen = index_ref[level : level + 1, :] == lax.broadcasted_iota(
+                    jnp.int32, (values, rows), 0
                 )
                 lam = lax.dot_general(
                     chosen.astype(F32),
                     table,
-                    (((1,), (1,)), ((), ())),
+                    (((0,), (1,)), ((), ())),
                     precision=lax.Precision.HIGHEST,
                     preferred_element_type=F32,
                 )
@@ -260,7 +254,8 @@
     rows, half = tokens[0][0].shape
     width = weights[0][0].shape[1]
     counts = [len(parts) for parts in weights]
-    total_rows = rows * len(jobs)
+    merged = [parts[-1].shape for parts in weights if len(parts) == 3]
+    shape = (rows * len(jobs), width)
 
     def kernel(mine_ref, *refs):
         token_refs, refs = refs[: 2 * len(tokens)], refs[2 * len(tokens) :]
@@ -268,7 +263,12 @@
         for count in counts:
             weight_refs.append(refs[:count])
             refs = refs[count:]
-        keep_ref, give_ref = refs
+        (keep_ref, give_ref), spare = refs[:2], list(refs[2:])
+        for which, part_refs in enumerate(weight_refs):
+            if len(part_refs) == 3:
+                sum_ref = spare.pop(0)
+                sum_ref[...] = part_refs[1][...] + part_refs[2][...]
+                weight_refs[which] = (part_refs[0], sum_ref)
         ours = mine_ref[0] == 1
 
         def product(piece, part_refs):
@@ -293,9 +293,8 @@
             keep_ref[here, :] = jnp.where(ours, close, away)
             give_ref[here, :] = jnp.where(ours, away, close).astype(BF16)
 
-    shape = (total_rows, width)
-    flat = [half_piece for pair in tokens for half_piece in pair] + [part for parts in weights for part in parts]
-    return local(kernel, [mine], flat, [(shape, F32), (shape, BF16)])
+    flat = [part for pair in tokens for part in pair] + [part for parts in weights for part in parts]
+    return local(kernel, [mine], flat, [(shape, F32), (shape, BF16)], merged)
 
 
 def add_cores(keep, got, rows, groups):
@@ -335,16 +334,15 @@
                 out = lax.dynamic_update_slice_in_dim(out, part, place[at] * width, 1)
                 at += 1
         return out
-    placed = [pltpu.with_memory_space_constraint(piece, pltpu.VMEM) for piece in landed]
     return pl.pallas_call(
         copy_kernel,
         out_shape=jax.ShapeDtypeStruct((rows, width * sum(blocks)), BF16),
-        in_specs=[FLAT] + [HERE] * len(landed),
+        in_specs=[FLAT] + [pl.BlockSpec(memory_space=pl.ANY)] * len(landed),
         out_specs=pl.BlockSpec(memory_space=pltpu.HBM),
         scratch_shapes=[pltpu.SemaphoreType.DMA((sum(blocks),))],
         compiler_params=SMALL,
         name="assemble",
-    )(place, *placed)
+    )(place, *landed)
 
 
 def level_states(made, depth):
@@ -398,7 +396,7 @@
 
     turn = jnp.full((1,), flip, jnp.int32)
     made = states(turn, keys, values, half)
-    split = out_weight.shape[0] * 5 // 8
+    split = out_weight.shape[0] * 11 // 16
     parts = order_rows(turn, out_weight, split)
     far = swap(parts[0], 1 << top)
     down = lift(parts[1], 0, 1 << top, 1 << top)
@@ -419,7 +417,7 @@
     roots = [inv_root / math.sqrt(rows)] + [inv_root / math.sqrt(rows * 2**level) for level in range(depth)]
     flags = [None] + [level if level < top - 1 else None for level in range(depth)]
     spot = jnp.full((1,), position, jnp.int32)
-    scales = level_scales(turn, spot, level_index, level_table, roots, flags, half)
+    scales = level_scales(turn, spot, level_index.T, level_table, roots, flags, half)
     normed = []
     for part in range(2):
         total = first_reads(turn, queries, keys, values, scales[part], first[part], half, part)
@@ -438,28 +436,31 @@
     tokens = [pieces[mask] for mask in token_masks]
     mine = ((position >> top & 1) == core).astype(jnp.int32)[None]
     column_masks = masks_of(column_bits)
-    staged = {mask: both if len(both) == 2 else (both[0], merge(both[1], both[2])) for mask, both in weights_of.items()}
     width, count, low = out_weight.shape[1], len(token_masks), (1 << top) - 1
-    keep, give = project(mine, tokens[:-1], [staged[0], staged[1 << top]], [(at, 0, 1) for at in range(count - 1)])
-    got = swap_cores(give)
     out, blocks = [], []
-    sums = add_cores(keep, got, rows, [[at] for at in range(count - 1)])
-    for mask, piece in zip(token_masks, sums):
-        out.append(swap(piece, mask) if mask else piece)
-        blocks.append(mask)
-    jobs, groups_of = [], [[] for _ in range(count)]
+
+    def leave(keep, give, groups_of, covers):
+        got = swap_cores(give)
+        chosen = [piece for piece in range(len(groups_of)) if groups_of[piece]]
+        sums = add_cores(keep, got, rows, [groups_of[piece] for piece in chosen])
+        for piece, part in zip(chosen, sums):
+            mask = token_masks[piece]
+            out.append(swap(part, mask) if mask else part)
+            blocks.extend(mask | cover for cover in covers[piece])
+
+    early = [(at, 0, 1) for at in range(count - 1)]
+    keep, give = project(mine, tokens[:-1], [weights_of[0], weights_of[1 << top]], early)
+    leave(keep, give, [[at] for at in range(count - 1)], [[0]] * (count - 1))
+    jobs, groups_of, covers = [], [[] for _ in range(count)], [[] for _ in range(count)]
     for at, mask in enumerate(column_masks):
         for piece in range(count):
             if at or piece == count - 1:
                 groups_of[piece].append(len(jobs))
+                covers[piece].append(mask)
                 jobs.append((piece, 2 * at, 2 * at + 1))
-    weights = [staged[full] for mask in column_masks for full in (mask, mask | 1 << top)]
+    weights = [weights_of[full] for mask in column_masks for full in (mask, mask | 1 << top)]
     keep, give = project(mine, tokens, weights, jobs)
-    got = swap_cores(give)
-    for piece, part in enumerate(add_cores(keep, got, rows, groups_of)):
-        mask = token_masks[piece]
-        out.append(swap(part, mask) if mask else part)
-        blocks += [mask | column_mask for column_mask in column_masks[piece < count - 1 :]]
+    leave(keep, give, groups_of, covers)
     place = jnp.stack([position & low ^ block for block in blocks]).astype(jnp.int32)
     return assemble(place, out, width)
 

time: 142 us -> 150 us (1.056)
  the two profiles are of different devices: /device:TPU:0 before, /device:TPU:17 now
where the time goes in v3:
time: 150 us
  waiting for transfers between devices  89.2 us (59%)
  starting transfers between devices  37.5 us (25%)
  Pallas kernels  15.8 us (11%)
  local copies, waits for them, and re-layouts  7.17 us (5%)
    ppermute x7, waiting for transfers between devices, lift(): return lax.ppermute(value, 'seq', pairs)  42.9 us
    ppermute x22, waiting for transfers between devices, swap(): return lax.ppermute(value, 'seq', pairs)  29.7 us
    ppermute x22, starting transfers between devices, swap(): return lax.ppermute(value, 'seq', pairs)  23.5 us
    ppermute x2, waiting for transfers between devices, swap_some(): return lax.ppermute(value, 'seq', pairs)  15.3 us
    pallas_call x13, Pallas kernels, local(): pl.pallas_call(kernel, out_shape=tuple((pltpu.VMEM(shape, dtype) for shap...  11.6 us
    ppermute x7, starting transfers between devices, lift(): return lax.ppermute(value, 'seq', pairs)  8.48 us
    unnamed x26, local copies, waits for them, and re-layouts  7.08 us
  transfers between devices with their start and end apart: 33, of which 17 were waited for; matrix products, arithmetic and copies ran while one was open for 0% of the time, Pallas kernels for 6%

profile of v3, /device:TPU:17, one launch (start us, length us, event | category | flops | bytes accessed | tf_op | source)
XLA Modules:
  0.0 149.9 jit_solution(8094804504362313764)
XLA Ops:
  0.0 1.6 %state.1 = (f32[8,128,128]{2,1,0:T(8,128)S(1)}, bf16[8,128,128]{2,1,0:T(8,128)(2,1)S(1)}, f32[8,128,128]{2,1,0:T(8,128)S(1)}, bf16[8,128,128]{2,1,0:T(8,128)(2,1)S(1)}) custom-call(s32[1]{0:T(128)} %bitcast.9.flip_ref, bf16[128,2048]{1,0:T(8,128)(2,1)} %key_ref.3, bf16[128,2048]{1,0:T(8,128)(2,1)} %value_ref.3), custom_call_target="tpu_custom_call" | custom-call | tf_op jit(solution)/shard_map/state/pallas_call | solution.py:104
  1.6 1.3 collective-permute-start.1
  4.1 4.7 %collective-permute-done.1.side_ref.refs_1_ = bf16[8,128,128]{2,1,0:T(8,128)(2,1)S(1)} collective-permute-done((bf16[8,128,128]{2,1,0:T(8,128)(2,1)S(1)}, bf16[8,128,128]{2,1,0:T(8,128)(2,1)S(1)}, u32[]{:S(2)}, u32[]{:S(2)}) %collective-permute-start.1) | collective-permute-done | bytes 262176 | tf_op jit(solution)/shard_map/ppermute | solution.py:15
  10.1 5.1 %collective-permute-done.2.corner_ref.refs_2_ = bf16[8,128,128]{2,1,0:T(8,128)(2,1)S(1)} collective-permute-done((bf16[8,128,128]{2,1,0:T(8,128)(2,1)S(1)}, bf16[8,128,128]{2,1,0:T(8,128)(2,1)S(1)}, u32[]{:S(2)}, u32[]{:S(2)}) %collective-permute-start.2) | collective-permute-done | bytes 262176 | tf_op jit(solution)/shard_map/ppermute | solution.py:15
  17.2 2.6 %collective-permute-start.16 = (bf16[1408,256]{1,0:T(8,128)(2,1)S(1)}, bf16[1408,256]{1,0:T(8,128)(2,1)S(1)}, u32[]{:S(2)}, u32[]{:S(2)}) collective-permute-start(bf16[1408,256]{1,0:T(8,128)(2,1)S(1)} %get-tuple-element.36.refs_6_.refs_8_), channel_id=1, source_target_pairs={{0,16},{2,18},{4,20},{6,22},{8,24},{10,26},{12,28},{14,30},{16,0},... | collective-permute-start | bytes 2162696 | tf_op jit(solution)/shard_map/ppermute | solution.py:15
  22.6 2.0 %collective-permute-start.17 = (bf16[640,256]{1,0:T(8,128)(2,1)S(1)}, bf16[640,256]{1,0:T(8,128)(2,1)S(1)}, u32[]{:S(2)}, u32[]{:S(2)}) collective-permute-start(bf16[640,256]{1,0:T(8,128)(2,1)S(1)} %get-tuple-element.37.refs_7_.refs_9_), channel_id=1, source_target_pairs={{16,0},{18,2},{20,4},{22,6},{24,8},{26,10},{28,12},{30,14},{17,1},... | collective-permute-start | bytes 983048 | tf_op jit(solution)/shard_map/ppermute | solution.py:24
  26.6 1.3 collective-permute-start.6
  27.9 3.4 %collective-permute-done.9.refs_2_.corner_ref = bf16[8,128,128]{2,1,0:T(8,128)(2,1)S(1)} collective-permute-done((bf16[8,128,128]{2,1,0:T(8,128)(2,1)S(1)}, bf16[8,128,128]{2,1,0:T(8,128)(2,1)S(1)}, u32[]{:S(2)}, u32[]{:S(2)}) %collective-permute-start.9) | collective-permute-done | bytes 262176 | tf_op jit(solution)/shard_map/ppermute | solution.py:15
  31.4 1.3 collective-permute-start.18
  33.6 30.7 %collective-permute-done.17.refs_9_.refs_11_ = bf16[640,256]{1,0:T(8,128)(2,1)S(1)} collective-permute-done((bf16[640,256]{1,0:T(8,128)(2,1)S(1)}, bf16[640,256]{1,0:T(8,128)(2,1)S(1)}, u32[]{:S(2)}, u32[]{:S(2)}) %collective-permute-start.17) | collective-permute-done | bytes 327712 | tf_op jit(solution)/shard_map/ppermute | solution.py:24
  64.3 1.3 collective-permute-start.10
  65.6 1.3 collective-permute-start.24
  68.0 1.3 collective-permute-start.4
  69.4 1.3 collective-permute-start.11
  71.9 6.1 %collective-permute-done.10.refs_0_ = bf16[8,128,128]{2,1,0:T(8,128)(2,1)S(1)} collective-permute-done((bf16[8,128,128]{2,1,0:T(8,128)(2,1)S(1)}, bf16[8,128,128]{2,1,0:T(8,128)(2,1)S(1)}, u32[]{:S(2)}, u32[]{:S(2)}) %collective-permute-start.10) | collective-permute-done | bytes 262176 | tf_op jit(solution)/shard_map/ppermute | solution.py:24
  78.8 4.9 %collective-permute-done.4.refs_0_ = bf16[8,128,128]{2,1,0:T(8,128)(2,1)S(1)} collective-permute-done((bf16[8,128,128]{2,1,0:T(8,128)(2,1)S(1)}, bf16[8,128,128]{2,1,0:T(8,128)(2,1)S(1)}, u32[]{:S(2)}, u32[]{:S(2)}) %collective-permute-start.4) | collective-permute-done | bytes 262176 | tf_op jit(solution)/shard_map/ppermute | solution.py:24
  84.9 2.1 %collective-permute-start.28 = (bf16[640,256]{1,0:T(8,128)(2,1)S(1)}, bf16[640,256]{1,0:T(8,128)(2,1)S(1)}, u32[]{:S(2)}, u32[]{:S(2)}) collective-permute-start(bf16[640,256]{1,0:T(8,128)(2,1)S(1)} %collective-permute-done.18.refs_10_.refs_12_), channel_id=1, source_target_pairs={{16,18},{18,16},{20,22},{22,20},{24,26},{26,24},{28,30},{30,28},{1... | collective-permute-start | bytes 983048 | tf_op jit(solution)/shard_map/ppermute | solution.py:33
  87.9 1.4 shard_map.70.total_ref
  92.9 2.2 %collective-permute-start.14 = (bf16[128,1024]{1,0:T(8,128)(2,1)S(1)}, bf16[128,1024]{1,0:T(8,128)(2,1)S(1)}, u32[]{:S(2)}, u32[]{:S(2)}) collective-permute-start(bf16[128,1024]{1,0:T(8,128)(2,1)S(1)} %shard_map.69.refs_0_), channel_id=1, source_target_pairs={{0,8},{2,10},{4,12},{6,14},{8,0},{10,2},{12,4},{14,6},{16,24},{18,... | collective-permute-start | bytes 786440 | tf_op jit(solution)/shard_map/ppermute | solution.py:15
  97.1 15.3 %collective-permute-done.28.refs_17_ = bf16[640,256]{1,0:T(8,128)(2,1)S(1)} collective-permute-done((bf16[640,256]{1,0:T(8,128)(2,1)S(1)}, bf16[640,256]{1,0:T(8,128)(2,1)S(1)}, u32[]{:S(2)}, u32[]{:S(2)}) %collective-permute-start.28) | collective-permute-done | bytes 327712 | tf_op jit(solution)/shard_map/ppermute | solution.py:33
  115.5 1.5 collective-permute-start.22
  116.9 2.8 %collective-permute-done.13.refs_3_ = bf16[128,1024]{1,0:T(8,128)(2,1)} collective-permute-done((bf16[128,1024]{1,0:T(8,128)(2,1)S(1)}, bf16[128,1024]{1,0:T(8,128)(2,1)}, u32[]{:S(2)}, u32[]{:S(2)}) %collective-permute-start.13) | collective-permute-done | bytes 262176 | tf_op jit(solution)/shard_map/ppermute | solution.py:15
  119.8 1.8 %collective-permute-done.15.refs_5_ = bf16[128,1024]{1,0:T(8,128)(2,1)} collective-permute-done((bf16[128,1024]{1,0:T(8,128)(2,1)S(1)}, bf16[128,1024]{1,0:T(8,128)(2,1)}, u32[]{:S(2)}, u32[]{:S(2)}) %collective-permute-start.15) | collective-permute-done | bytes 262176 | tf_op jit(solution)/shard_map/ppermute | solution.py:15
  121.6 3.8 %collective-permute-done.23.refs_7_ = bf16[128,1024]{1,0:T(8,128)(2,1)} collective-permute-done((bf16[128,1024]{1,0:T(8,128)(2,1)S(1)}, bf16[128,1024]{1,0:T(8,128)(2,1)}, u32[]{:S(2)}, u32[]{:S(2)}) %collective-permute-start.23) | collective-permute-done | bytes 262176 | tf_op jit(solution)/shard_map/ppermute | solution.py:15
  125.4 1.8 %collective-permute-done.22.refs_6_ = bf16[128,1024]{1,0:T(8,128)(2,1)} collective-permute-done((bf16[128,1024]{1,0:T(8,128)(2,1)S(1)}, bf16[128,1024]{1,0:T(8,128)(2,1)}, u32[]{:S(2)}, u32[]{:S(2)}) %collective-permute-start.22) | collective-permute-done | bytes 262176 | tf_op jit(solution)/shard_map/ppermute | solution.py:15
  131.2 3.2 %shard_map.75 = (f32[640,256]{1,0:T(8,128)S(1)}, bf16[640,256]{1,0:T(8,128)(2,1)S(1)}) custom-call(s32[1]{0:T(128)} %bitcast.8.mine_ref, bf16[128,1024]{1,0:T(8,128)(2,1)S(1)} %shard_map.69.refs_0_, bf16[128,1024]{1,0:T(8,128)(2,1)S(1)} %shard_map.72.refs_1_, bf16[128,1024]{1,0:T(8,128)(2,1)S(1)} %collective-permute-done.12.refs_2_, ...), custom_call_target="tpu_custom_call" | custom-call | tf_op jit(solution)/shard_map/pallas_call | solution.py:62
  134.4 2.6 %collective-permute-start.29 = (bf16[640,256]{1,0:T(8,128)(2,1)S(1)}, bf16[640,256]{1,0:T(8,128)(2,1)S(1)}, u32[]{:S(2)}, u32[]{:S(2)}) collective-permute-start(bf16[640,256]{1,0:T(8,128)(2,1)S(1)} %get-tuple-element.44), channel_id=1, source_target_pairs={{0,1},{1,0},{2,3},{3,2},{4,5},{5,4},{6,7},{7,6},{8,9},{9,8},{10,11... | collective-permute-start | bytes 983048 | tf_op jit(solution)/shard_map/ppermute | solution.py:37
  137.0 2.1 %shard_map.73 = (f32[384,256]{1,0:T(8,128)S(1)}, bf16[384,256]{1,0:T(8,128)(2,1)S(1)}) custom-call(s32[1]{0:T(128)} %bitcast.8.mine_ref, bf16[128,1024]{1,0:T(8,128)(2,1)S(1)} %shard_map.69.refs_0_, bf16[128,1024]{1,0:T(8,128)(2,1)S(1)} %shard_map.72.refs_1_, bf16[128,1024]{1,0:T(8,128)(2,1)S(1)} %collective-permute-done.12.refs_2_, ...), custom_call_target="tpu_custom_call" | custom-call | tf_op jit(solution)/shard_map/pallas_call | solution.py:62
  142.3 1.3 collective-permute-start.31
  143.7 3.4 %collective-permute-done.20.refs_1_ = bf16[128,256]{1,0:T(8,128)(2,1)S(1)} collective-permute-done((bf16[128,256]{1,0:T(8,128)(2,1)S(1)}, bf16[128,256]{1,0:T(8,128)(2,1)S(1)}, u32[]{:S(2)}, u32[]{:S(2)}) %collective-permute-start.20) | collective-permute-done | bytes 65568 | tf_op jit(solution)/shard_map/ppermute | solution.py:15
  147.1 1.4 collective-permute-done.30.refs_4_
  148.5 1.4 assemble.1
  (77 shorter events, 31.1 us)
Async XLA Ops:
  1.6 7.3 %collective-permute-start.1 = (bf16[8,128,128]{2,1,0:T(8,128)(2,1)S(1)}, bf16[8,128,128]{2,1,0:T(8,128)(2,1)S(1)}, u32[]{:S(2)}, u32[]{:S(2)}) collective-permute-start(bf16[8,128,128]{2,1,0:T(8,128)(2,1)S(1)} %get-tuple-element.29), channel_id=1, source_target_pairs={{0,4},{2,6},{4,0},{6,2},{8,12},{10,14},{12,8},{14,10},{16,20},{18,... | collective-permute-start | bytes 786440 | tf_op jit(solution)/shard_map/ppermute | solution.py:15
  2.9 7.2 %collective-permute-start = (bf16[8,128,128]{2,1,0:T(8,128)(2,1)S(1)}, bf16[8,128,128]{2,1,0:T(8,128)(2,1)S(1)}, u32[]{:S(2)}, u32[]{:S(2)}) collective-permute-start(bf16[8,128,128]{2,1,0:T(8,128)(2,1)S(1)} %get-tuple-element.28), channel_id=1, source_target_pairs={{0,2},{2,0},{4,6},{6,4},{8,10},{10,8},{12,14},{14,12},{16,18},{18,... | collective-permute-start | bytes 786440 | tf_op jit(solution)/shard_map/ppermute | solution.py:15
  8.9 6.3 %collective-permute-start.2 = (bf16[8,128,128]{2,1,0:T(8,128)(2,1)S(1)}, bf16[8,128,128]{2,1,0:T(8,128)(2,1)S(1)}, u32[]{:S(2)}, u32[]{:S(2)}) collective-permute-start(bf16[8,128,128]{2,1,0:T(8,128)(2,1)S(1)} %collective-permute-done.1.side_ref.refs_1_), channel_id=1, source_target_pairs={{0,2},{2,0},{4,6},{6,4},{8,10},{10,8},{12,14},{14,12},{16,18},{18,... | collective-permute-start | bytes 786440 | tf_op jit(solution)/shard_map/ppermute | solution.py:15
  15.3 7.3 %collective-permute-start.3 = (bf16[8,128,128]{2,1,0:T(8,128)(2,1)S(1)}, bf16[8,128,128]{2,1,0:T(8,128)(2,1)S(1)}, u32[]{:S(2)}, u32[]{:S(2)}) collective-permute-start(bf16[8,128,128]{2,1,0:T(8,128)(2,1)S(1)} %get-tuple-element.31), channel_id=1, source_target_pairs={{0,8},{2,10},{4,12},{6,14},{1,9},{3,11},{5,13},{7,15}} | collective-permute-start | bytes 786440 | tf_op jit(solution)/shard_map/ppermute | solution.py:24
  17.2 53.5 %collective-permute-start.16 = (bf16[1408,256]{1,0:T(8,128)(2,1)S(1)}, bf16[1408,256]{1,0:T(8,128)(2,1)S(1)}, u32[]{:S(2)}, u32[]{:S(2)}) collective-permute-start(bf16[1408,256]{1,0:T(8,128)(2,1)S(1)} %get-tuple-element.36.refs_6_.refs_8_), channel_id=1, source_target_pairs={{0,16},{2,18},{4,20},{6,22},{8,24},{10,26},{12,28},{14,30},{16,0},... | collective-permute-start | bytes 2162696 | tf_op jit(solution)/shard_map/ppermute | solution.py:15
  19.9 5.2 %collective-permute-start.7 = (bf16[8,128,128]{2,1,0:T(8,128)(2,1)S(1)}, bf16[8,128,128]{2,1,0:T(8,128)(2,1)S(1)}, u32[]{:S(2)}, u32[]{:S(2)}) collective-permute-start(bf16[8,128,128]{2,1,0:T(8,128)(2,1)S(1)} %get-tuple-element.29), channel_id=1, source_target_pairs={{0,2},{2,0},{4,6},{6,4},{8,10},{10,8},{12,14},{14,12},{16,18},{18,... | collective-permute-start | bytes 786440 | tf_op jit(solution)/shard_map/ppermute | solution.py:15
  21.1 5.5 %collective-permute-start.8 = (bf16[8,128,128]{2,1,0:T(8,128)(2,1)S(1)}, bf16[8,128,128]{2,1,0:T(8,128)(2,1)S(1)}, u32[]{:S(2)}, u32[]{:S(2)}) collective-permute-start(bf16[8,128,128]{2,1,0:T(8,128)(2,1)S(1)} %get-tuple-element.28), channel_id=1, source_target_pairs={{0,4},{2,6},{4,0},{6,2},{8,12},{10,14},{12,8},{14,10},{16,20},{18,... | collective-permute-start | bytes 786440 | tf_op jit(solution)/shard_map/ppermute | solution.py:15
  22.3 9.0 %collective-permute-start.9 = (bf16[8,128,128]{2,1,0:T(8,128)(2,1)S(1)}, bf16[8,128,128]{2,1,0:T(8,128)(2,1)S(1)}, u32[]{:S(2)}, u32[]{:S(2)}) collective-permute-start(bf16[8,128,128]{2,1,0:T(8,128)(2,1)S(1)} %collective-permute-done.near_ref.refs_0_), channel_id=1, source_target_pairs={{0,4},{2,6},{4,0},{6,2},{8,12},{10,14},{12,8},{14,10},{16,20},{18,... | collective-permute-start | bytes 786440 | tf_op jit(solution)/shard_map/ppermute | solution.py:15
  22.6 41.8 %collective-permute-start.17 = (bf16[640,256]{1,0:T(8,128)(2,1)S(1)}, bf16[640,256]{1,0:T(8,128)(2,1)S(1)}, u32[]{:S(2)}, u32[]{:S(2)}) collective-permute-start(bf16[640,256]{1,0:T(8,128)(2,1)S(1)} %get-tuple-element.37.refs_7_.refs_9_), channel_id=1, source_target_pairs={{16,0},{18,2},{20,4},{22,6},{24,8},{26,10},{28,12},{30,14},{17,1},... | collective-permute-start | bytes 983048 | tf_op jit(solution)/shard_map/ppermute | solution.py:24
  25.1 40.5 %collective-permute-start.5 = (bf16[8,128,128]{2,1,0:T(8,128)(2,1)S(1)}, bf16[8,128,128]{2,1,0:T(8,128)(2,1)S(1)}, u32[]{:S(2)}, u32[]{:S(2)}) collective-permute-start(bf16[8,128,128]{2,1,0:T(8,128)(2,1)S(1)} %shard_map.67), channel_id=1, source_target_pairs={{8,24},{10,26},{12,28},{14,30},{9,25},{11,27},{13,29},{15,31}} | collective-permute-start | bytes 786440 | tf_op jit(solution)/shard_map/ppermute | solution.py:24
  26.6 41.4 %collective-permute-start.6 = (bf16[8,128,128]{2,1,0:T(8,128)(2,1)S(1)}, bf16[8,128,128]{2,1,0:T(8,128)(2,1)S(1)}, u32[]{:S(2)}, u32[]{:S(2)}) collective-permute-start(bf16[8,128,128]{2,1,0:T(8,128)(2,1)S(1)} %shard_map.67), channel_id=1, source_target_pairs={{8,16},{10,18},{12,20},{14,22},{9,17},{11,19},{13,21},{15,23}} | collective-permute-start | bytes 786440 | tf_op jit(solution)/shard_map/ppermute | solution.py:24
  31.4 38.0 %collective-permute-start.18 = (bf16[640,256]{1,0:T(8,128)(2,1)S(1)}, bf16[640,256]{1,0:T(8,128)(2,1)S(1)}, u32[]{:S(2)}, u32[]{:S(2)}) collective-permute-start(bf16[640,256]{1,0:T(8,128)(2,1)S(1)} %get-tuple-element.37.refs_7_.refs_9_), channel_id=1, source_target_pairs={{0,16},{2,18},{4,20},{6,22},{8,24},{10,26},{12,28},{14,30},{1,17},... | collective-permute-start | bytes 983048 | tf_op jit(solution)/shard_map/ppermute | solution.py:24
  64.3 13.7 %collective-permute-start.10 = (bf16[8,128,128]{2,1,0:T(8,128)(2,1)S(1)}, bf16[8,128,128]{2,1,0:T(8,128)(2,1)S(1)}, u32[]{:S(2)}, u32[]{:S(2)}) collective-permute-start(bf16[8,128,128]{2,1,0:T(8,128)(2,1)S(1)} %get-tuple-element.35), channel_id=1, source_target_pairs={{0,8},{2,10},{4,12},{6,14},{16,24},{18,26},{20,28},{22,30},{1,9},{... | collective-permute-start | bytes 786440 | tf_op jit(solution)/shard_map/ppermute | solution.py:24
  65.6 48.7 %collective-permute-start.24 = (bf16[1408,256]{1,0:T(8,128)(2,1)S(1)}, bf16[1408,256]{1,0:T(8,128)(2,1)S(1)}, u32[]{:S(2)}, u32[]{:S(2)}) collective-permute-start(bf16[1408,256]{1,0:T(8,128)(2,1)S(1)} %get-tuple-element.36.refs_6_.refs_8_), channel_id=1, source_target_pairs={{0,2},{2,0},{4,6},{6,4},{8,10},{10,8},{12,14},{14,12},{16,18},{18,... | collective-permute-start | bytes 2162696 | tf_op jit(solution)/shard_map/ppermute | solution.py:15
  68.0 15.7 %collective-permute-start.4 = (bf16[8,128,128]{2,1,0:T(8,128)(2,1)S(1)}, bf16[8,128,128]{2,1,0:T(8,128)(2,1)S(1)}, u32[]{:S(2)}, u32[]{:S(2)}) collective-permute-start(bf16[8,128,128]{2,1,0:T(8,128)(2,1)S(1)} %get-tuple-element.31), channel_id=1, source_target_pairs={{16,24},{18,26},{20,28},{22,30},{17,25},{19,27},{21,29},{23,31}} | collective-permute-start | bytes 786440 | tf_op jit(solution)/shard_map/ppermute | solution.py:24
  69.4 15.5 %collective-permute-start.11 = (bf16[8,128,128]{2,1,0:T(8,128)(2,1)S(1)}, bf16[8,128,128]{2,1,0:T(8,128)(2,1)S(1)}, u32[]{:S(2)}, u32[]{:S(2)}) collective-permute-start(bf16[8,128,128]{2,1,0:T(8,128)(2,1)S(1)} %shard_map.68.refs_1_), channel_id=1, source_target_pairs={{0,4},{2,6},{4,0},{6,2},{8,12},{10,14},{12,8},{14,10},{16,20},{18,... | collective-permute-start | bytes 786440 | tf_op jit(solution)/shard_map/ppermute | solution.py:15
  70.7 21.5 %collective-permute-start.25 = (bf16[640,256]{1,0:T(8,128)(2,1)S(1)}, bf16[640,256]{1,0:T(8,128)(2,1)S(1)}, u32[]{:S(2)}, u32[]{:S(2)}) collective-permute-start(bf16[640,256]{1,0:T(8,128)(2,1)S(1)} %get-tuple-element.37.refs_7_.refs_9_), channel_id=1, source_target_pairs={{0,2},{2,0},{4,6},{6,4},{8,10},{10,8},{12,14},{14,12},{16,18},{18,... | collective-permute-start | bytes 983048 | tf_op jit(solution)/shard_map/ppermute | solution.py:15
  78.1 17.0 %collective-permute-start.27 = (bf16[640,256]{1,0:T(8,128)(2,1)S(1)}, bf16[640,256]{1,0:T(8,128)(2,1)S(1)}, u32[]{:S(2)}, u32[]{:S(2)}) collective-permute-start(bf16[640,256]{1,0:T(8,128)(2,1)S(1)} %collective-permute-done.17.refs_9_.refs_11_), channel_id=1, source_target_pairs={{0,2},{2,0},{4,6},{6,4},{8,10},{10,8},{12,14},{14,12},{1,3},{3,1},... | collective-permute-start | bytes 983048 | tf_op jit(solution)/shard_map/ppermute | solution.py:33
  83.7 36.1 %collective-permute-start.26 = (bf16[1408,256]{1,0:T(8,128)(2,1)S(1)}, bf16[1408,256]{1,0:T(8,128)(2,1)}, u32[]{:S(2)}, u32[]{:S(2)}) collective-permute-start(bf16[1408,256]{1,0:T(8,128)(2,1)S(1)} %collective-permute-done.16.refs_8_.refs_10_), channel_id=1, source_target_pairs={{0,2},{2,0},{4,6},{6,4},{8,10},{10,8},{12,14},{14,12},{16,18},{18,... | collective-permute-start | bytes 2162696 | tf_op jit(solution)/shard_map/ppermute | solution.py:15
  84.9 27.5 %collective-permute-start.28 = (bf16[640,256]{1,0:T(8,128)(2,1)S(1)}, bf16[640,256]{1,0:T(8,128)(2,1)S(1)}, u32[]{:S(2)}, u32[]{:S(2)}) collective-permute-start(bf16[640,256]{1,0:T(8,128)(2,1)S(1)} %collective-permute-done.18.refs_10_.refs_12_), channel_id=1, source_target_pairs={{16,18},{18,16},{20,22},{22,20},{24,26},{26,24},{28,30},{30,28},{1... | collective-permute-start | bytes 983048 | tf_op jit(solution)/shard_map/ppermute | solution.py:33
  92.9 22.4 %collective-permute-start.14 = (bf16[128,1024]{1,0:T(8,128)(2,1)S(1)}, bf16[128,1024]{1,0:T(8,128)(2,1)S(1)}, u32[]{:S(2)}, u32[]{:S(2)}) collective-permute-start(bf16[128,1024]{1,0:T(8,128)(2,1)S(1)} %shard_map.69.refs_0_), channel_id=1, source_target_pairs={{0,8},{2,10},{4,12},{6,14},{8,0},{10,2},{12,4},{14,6},{16,24},{18,... | collective-permute-start | bytes 786440 | tf_op jit(solution)/shard_map/ppermute | solution.py:15
  95.8 19.6 %collective-permute-start.12 = (bf16[128,1024]{1,0:T(8,128)(2,1)S(1)}, bf16[128,1024]{1,0:T(8,128)(2,1)S(1)}, u32[]{:S(2)}, u32[]{:S(2)}) collective-permute-start(bf16[128,1024]{1,0:T(8,128)(2,1)S(1)} %shard_map.72.refs_1_), channel_id=1, source_target_pairs={{0,4},{2,6},{4,0},{6,2},{8,12},{10,14},{12,8},{14,10},{16,20},{18,... | collective-permute-start | bytes 786440 | tf_op jit(solution)/shard_map/ppermute | solution.py:15
  113.1 6.6 %collective-permute-start.13 = (bf16[128,1024]{1,0:T(8,128)(2,1)S(1)}, bf16[128,1024]{1,0:T(8,128)(2,1)}, u32[]{:S(2)}, u32[]{:S(2)}) collective-permute-start(bf16[128,1024]{1,0:T(8,128)(2,1)S(1)} %shard_map.69.refs_0_), channel_id=1, source_target_pairs={{0,4},{2,6},{4,0},{6,2},{8,12},{10,14},{12,8},{14,10},{16,20},{18,... | collective-permute-start | bytes 786440 | tf_op jit(solution)/shard_map/ppermute | solution.py:15
  115.3 6.3 %collective-permute-start.15 = (bf16[128,1024]{1,0:T(8,128)(2,1)S(1)}, bf16[128,1024]{1,0:T(8,128)(2,1)}, u32[]{:S(2)}, u32[]{:S(2)}) collective-permute-start(bf16[128,1024]{1,0:T(8,128)(2,1)S(1)} %shard_map.72.refs_1_), channel_id=1, source_target_pairs={{0,8},{2,10},{4,12},{6,14},{8,0},{10,2},{12,4},{14,6},{16,24},{18,... | collective-permute-start | bytes 786440 | tf_op jit(solution)/shard_map/ppermute | solution.py:15
  115.3 10.1 %collective-permute-start.23 = (bf16[128,1024]{1,0:T(8,128)(2,1)S(1)}, bf16[128,1024]{1,0:T(8,128)(2,1)}, u32[]{:S(2)}, u32[]{:S(2)}) collective-permute-start(bf16[128,1024]{1,0:T(8,128)(2,1)S(1)} %collective-permute-done.14.refs_4_), channel_id=1, source_target_pairs={{0,4},{2,6},{4,0},{6,2},{8,12},{10,14},{12,8},{14,10},{16,20},{18,... | collective-permute-start | bytes 786440 | tf_op jit(solution)/shard_map/ppermute | solution.py:15
  115.5 11.7 %collective-permute-start.22 = (bf16[128,1024]{1,0:T(8,128)(2,1)S(1)}, bf16[128,1024]{1,0:T(8,128)(2,1)}, u32[]{:S(2)}, u32[]{:S(2)}) collective-permute-start(bf16[128,1024]{1,0:T(8,128)(2,1)S(1)} %collective-permute-done.12.refs_2_), channel_id=1, source_target_pairs={{0,8},{2,10},{4,12},{6,14},{8,0},{10,2},{12,4},{14,6},{16,24},{18,... | collective-permute-start | bytes 786440 | tf_op jit(solution)/shard_map/ppermute | solution.py:15
  134.4 4.8 %collective-permute-start.29 = (bf16[640,256]{1,0:T(8,128)(2,1)S(1)}, bf16[640,256]{1,0:T(8,128)(2,1)S(1)}, u32[]{:S(2)}, u32[]{:S(2)}) collective-permute-start(bf16[640,256]{1,0:T(8,128)(2,1)S(1)} %get-tuple-element.44), channel_id=1, source_target_pairs={{0,1},{1,0},{2,3},{3,2},{4,5},{5,4},{6,7},{7,6},{8,9},{9,8},{10,11... | collective-permute-start | bytes 983048 | tf_op jit(solution)/shard_map/ppermute | solution.py:37
  139.3 9.2 %collective-permute-start.32 = (bf16[128,512]{1,0:T(8,128)(2,1)S(1)}, bf16[128,512]{1,0:T(8,128)(2,1)S(1)}, u32[]{:S(2)}, u32[]{:S(2)}) collective-permute-start(bf16[128,512]{1,0:T(8,128)(2,1)S(1)} %get-tuple-element.48), channel_id=1, source_target_pairs={{0,12},{2,14},{4,8},{6,10},{8,4},{10,6},{12,0},{14,2},{16,28},{18,... | collective-permute-start | bytes 393224 | tf_op jit(solution)/shard_map/ppermute | solution.py:15
  140.6 6.5 %collective-permute-start.20 = (bf16[128,256]{1,0:T(8,128)(2,1)S(1)}, bf16[128,256]{1,0:T(8,128)(2,1)S(1)}, u32[]{:S(2)}, u32[]{:S(2)}) collective-permute-start(bf16[128,256]{1,0:T(8,128)(2,1)S(1)} %get-tuple-element.41), channel_id=1, source_target_pairs={{0,4},{2,6},{4,0},{6,2},{8,12},{10,14},{12,8},{14,10},{16,20},{18,... | collective-permute-start | bytes 196616 | tf_op jit(solution)/shard_map/ppermute | solution.py:15
  140.9 6.2 %collective-permute-start.21 = (bf16[128,256]{1,0:T(8,128)(2,1)S(1)}, bf16[128,256]{1,0:T(8,128)(2,1)S(1)}, u32[]{:S(2)}, u32[]{:S(2)}) collective-permute-start(bf16[128,256]{1,0:T(8,128)(2,1)S(1)} %get-tuple-element.42), channel_id=1, source_target_pairs={{0,8},{2,10},{4,12},{6,14},{8,0},{10,2},{12,4},{14,6},{16,24},{18,... | collective-permute-start | bytes 196616 | tf_op jit(solution)/shard_map/ppermute | solution.py:15
  142.1 6.4 %collective-permute-start.30 = (bf16[128,256]{1,0:T(8,128)(2,1)S(1)}, bf16[128,256]{1,0:T(8,128)(2,1)S(1)}, u32[]{:S(2)}, u32[]{:S(2)}) collective-permute-start(bf16[128,256]{1,0:T(8,128)(2,1)S(1)} %get-tuple-element.46), channel_id=1, source_target_pairs={{0,4},{2,6},{4,0},{6,2},{8,12},{10,14},{12,8},{14,10},{16,20},{18,... | collective-permute-start | bytes 196616 | tf_op jit(solution)/shard_map/ppermute | solution.py:15
  142.3 6.2 %collective-permute-start.31 = (bf16[128,256]{1,0:T(8,128)(2,1)S(1)}, bf16[128,256]{1,0:T(8,128)(2,1)S(1)}, u32[]{:S(2)}, u32[]{:S(2)}) collective-permute-start(bf16[128,256]{1,0:T(8,128)(2,1)S(1)} %get-tuple-element.47), channel_id=1, source_target_pairs={{0,8},{2,10},{4,12},{6,14},{8,0},{10,2},{12,4},{14,6},{16,24},{18,... | collective-permute-start | bytes 196616 | tf_op jit(solution)/shard_map/ppermute | solution.py:15
  (14 other events, 208.8 us)

commit v4 on v3

--- a/solution.py
+++ b/solution.py
@@ -33,6 +33,11 @@
     return lax.ppermute(value, "seq", pairs)
 
 
+def swap_at(value, mask, bits, want):
+    pairs = [(source, source ^ mask) for source in range(lax.axis_size("seq")) if source & bits == want]
+    return lax.ppermute(value, "seq", pairs)
+
+
 def swap_cores(value):
     return lax.ppermute(value, "head", [(0, 1), (1, 0)])
 
@@ -57,7 +62,7 @@
 F32, BF16 = jnp.float32, jnp.bfloat16
 
 
-def local(kernel, scalars, operands, results, spare=()):
+def local(kernel, scalars, operands, results, spare=(), params=SMALL):
     placed = [pltpu.with_memory_space_constraint(operand, pltpu.VMEM) for operand in operands]
     return pl.pallas_call(
         kernel,
@@ -65,7 +70,7 @@
         in_specs=[FLAT] * len(scalars) + [HERE] * len(operands),
         out_specs=tuple(HERE for _ in results),
         scratch_shapes=[pltpu.VMEM(shape, BF16) for shape in spare],
-        compiler_params=SMALL,
+        compiler_params=params,
     )(*scalars, *placed)
 
 
@@ -294,7 +299,8 @@
             give_ref[here, :] = jnp.where(ours, away, close).astype(BF16)
 
     flat = [part for pair in tokens for part in pair] + [part for parts in weights for part in parts]
-    return local(kernel, [mine], flat, [(shape, F32), (shape, BF16)], merged)
+    params = SMALL if len(jobs) <= 16 else pltpu.CompilerParams(vmem_limit_bytes=20 << 20)
+    return local(kernel, [mine], flat, [(shape, F32), (shape, BF16)], merged, params)
 
 
 def add_cores(keep, got, rows, groups):
@@ -356,26 +362,29 @@
     near[1] = swap(own[1], 1)
     corner[1] = swap(near[0], 2)
     first, last = [], []
+    level, below = top - 1, 1 << top - 1
     for part in range(2):
-        sent, block = block_sum(state[part], near[part], side[part], corner[part])
         early, late = [near[part], side[part], corner[part]], []
-        for level in range(2, top - 1):
-            other = swap(sent, 1 << level)
+        if part == 0 or level > 2:
+            sent, block = block_sum(state[part], near[part], side[part], corner[part])
+        for middle in range(2, level):
+            other = swap(sent, 1 << middle)
             early.append(other)
             sent, block = add_block(block, other, 1)
-        level = top - 1
         if part == 0:
-            other = lift(sent, 1 << level | 1 << top, 0, 1 << level)
-            early.append(other)
-            late.append((lift(sent, 1 << level, 1 << top, 1 << level), level + 1))
-            (sent,) = add_block(block, other, 0)
-            below = 1 << top - 1
+            lower = lift(sent, below | 1 << top, 0, below)
+            upper = lift(sent, below, 1 << top, below)
+            early.append(lower)
+            late.append((upper, level + 1))
+            (sent,) = add_block(block, lower, 0)
             after = lift(sent, 1 << top, below, 1 << top)
             close = lift(sent, 1 << top, below, 1 << top | below)
             (got,) = add_block(after, close, 0)
             late.append((got, top + 1))
         else:
-            late.append((lift(sent, 1 << level, 0, 1 << level), level + 1))
+            both = below | 1 << top
+            early.append(swap_at(lower, 2, both, below))
+            late.append((swap_at(upper, 2, both, both), level + 1))
             late.append((swap(got, 2), top + 1))
         first.append(early)
         last.append(late)
@@ -396,7 +405,7 @@
 
     turn = jnp.full((1,), flip, jnp.int32)
     made = states(turn, keys, values, half)
-    split = out_weight.shape[0] * 11 // 16
+    split = out_weight.shape[0] * 5 // 8
     parts = order_rows(turn, out_weight, split)
     far = swap(parts[0], 1 << top)
     down = lift(parts[1], 0, 1 << top, 1 << top)

time: 150 us -> 144 us (0.960)
  the two profiles are of different devices: /device:TPU:17 before, /device:TPU:0 now
where the time goes in v4:
time: 144 us; the launch traced here: 143 us
  starting transfers between devices  63.5 us (44%)
  waiting for transfers between devices  57.5 us (40%)
  Pallas kernels  14.6 us (10%)
  local copies, waits for them, and re-layouts  7.28 us (5%)
    ppermute x22, starting transfers between devices, swap(): return lax.ppermute(value, 'seq', pairs)  48.9 us
    ppermute x22, waiting for transfers between devices, swap(): return lax.ppermute(value, 'seq', pairs)  33.8 us
    ppermute x6, waiting for transfers between devices, lift(): return lax.ppermute(value, 'seq', pairs)  23.6 us
    pallas_call x12, Pallas kernels, local(): pl.pallas_call(kernel, out_shape=tuple((pltpu.VMEM(shape, dtype) for shap...  9.81 us
    ppermute x6, starting transfers between devices, lift(): return lax.ppermute(value, 'seq', pairs)  9.46 us
    unnamed x26, local copies, waits for them, and re-layouts  7.2 us
    ppermute x2, starting transfers between devices, swap_some(): return lax.ppermute(value, 'seq', pairs)  3.11 us
  transfers between devices with their start and end apart: 34, of which 12 were waited for; matrix products, arithmetic and copies ran while one was open for 0% of the time, Pallas kernels for 6%

profile of v4, /device:TPU:0, one launch (start us, length us, event | category | flops | bytes accessed | tf_op | source)
XLA Modules:
  0.0 143.1 jit_solution(14906216995265618220)
XLA Ops:
  0.0 2.1 %state.1 = (f32[8,128,128]{2,1,0:T(8,128)}, bf16[8,128,128]{2,1,0:T(8,128)(2,1)S(1)}, f32[8,128,128]{2,1,0:T(8,128)S(1)}, bf16[8,128,128]{2,1,0:T(8,128)(2,1)S(1)}) custom-call(s32[1]{0:T(128)} %bitcast.9.flip_ref, bf16[128,2048]{1,0:T(8,128)(2,1)} %key_ref.3, bf16[128,2048]{1,0:T(8,128)(2,1)} %value_ref.3), custom_call_target="tpu_custom_call" | custom-call | tf_op jit(solution)/shard_map/state/pallas_call | solution.py:109
  2.2 3.1 %collective-permute-start.1 = (bf16[8,128,128]{2,1,0:T(8,128)(2,1)S(1)}, bf16[8,128,128]{2,1,0:T(8,128)(2,1)S(1)}, u32[]{:S(2)}, u32[]{:S(2)}) collective-permute-start(bf16[8,128,128]{2,1,0:T(8,128)(2,1)S(1)} %get-tuple-element.27), channel_id=1, source_target_pairs={{0,4},{2,6},{4,0},{6,2},{8,12},{10,14},{12,8},{14,10},{16,20},{18,... | collective-permute-start | bytes 786440 | tf_op jit(solution)/shard_map/ppermute | solution.py:15
  5.2 1.5 %collective-permute-start = (bf16[8,128,128]{2,1,0:T(8,128)(2,1)S(1)}, bf16[8,128,128]{2,1,0:T(8,128)(2,1)S(1)}, u32[]{:S(2)}, u32[]{:S(2)}) collective-permute-start(bf16[8,128,128]{2,1,0:T(8,128)(2,1)S(1)} %get-tuple-element.26), channel_id=1, source_target_pairs={{0,2},{2,0},{4,6},{6,4},{8,10},{10,8},{12,14},{14,12},{16,18},{18,... | collective-permute-start | bytes 786440 | tf_op jit(solution)/shard_map/ppermute | solution.py:15
  6.7 4.8 %collective-permute-done.1.side_ref.refs_1_ = bf16[8,128,128]{2,1,0:T(8,128)(2,1)S(1)} collective-permute-done((bf16[8,128,128]{2,1,0:T(8,128)(2,1)S(1)}, bf16[8,128,128]{2,1,0:T(8,128)(2,1)S(1)}, u32[]{:S(2)}, u32[]{:S(2)}) %collective-permute-start.1) | collective-permute-done | bytes 262176 | tf_op jit(solution)/shard_map/ppermute | solution.py:15
  11.5 1.7 %collective-permute-start.2 = (bf16[8,128,128]{2,1,0:T(8,128)(2,1)S(1)}, bf16[8,128,128]{2,1,0:T(8,128)(2,1)S(1)}, u32[]{:S(2)}, u32[]{:S(2)}) collective-permute-start(bf16[8,128,128]{2,1,0:T(8,128)(2,1)S(1)} %collective-permute-done.1.side_ref.refs_1_), channel_id=1, source_target_pairs={{0,2},{2,0},{4,6},{6,4},{8,10},{10,8},{12,14},{14,12},{16,18},{18,... | collective-permute-start | bytes 786440 | tf_op jit(solution)/shard_map/ppermute | solution.py:15
  13.2 5.8 %collective-permute-done.2.corner_ref.refs_2_ = bf16[8,128,128]{2,1,0:T(8,128)(2,1)S(1)} collective-permute-done((bf16[8,128,128]{2,1,0:T(8,128)(2,1)S(1)}, bf16[8,128,128]{2,1,0:T(8,128)(2,1)S(1)}, u32[]{:S(2)}, u32[]{:S(2)}) %collective-permute-start.2) | collective-permute-done | bytes 262176 | tf_op jit(solution)/shard_map/ppermute | solution.py:15
  19.1 3.4 %collective-permute-start.3 = (bf16[8,128,128]{2,1,0:T(8,128)(2,1)S(1)}, bf16[8,128,128]{2,1,0:T(8,128)(2,1)S(1)}, u32[]{:S(2)}, u32[]{:S(2)}) collective-permute-start(bf16[8,128,128]{2,1,0:T(8,128)(2,1)S(1)} %get-tuple-element.29), channel_id=1, source_target_pairs={{0,8},{2,10},{4,12},{6,14},{1,9},{3,11},{5,13},{7,15}} | collective-permute-start | bytes 786440 | tf_op jit(solution)/shard_map/ppermute | solution.py:24
  22.6 1.6 %collective-permute-start.7 = (bf16[8,128,128]{2,1,0:T(8,128)(2,1)S(1)}, bf16[8,128,128]{2,1,0:T(8,128)(2,1)S(1)}, u32[]{:S(2)}, u32[]{:S(2)}) collective-permute-start(bf16[8,128,128]{2,1,0:T(8,128)(2,1)S(1)} %get-tuple-element.27), channel_id=1, source_target_pairs={{0,2},{2,0},{4,6},{6,4},{8,10},{10,8},{12,14},{14,12},{16,18},{18,... | collective-permute-start | bytes 786440 | tf_op jit(solution)/shard_map/ppermute | solution.py:15
  24.1 1.5 %collective-permute-start.8 = (bf16[8,128,128]{2,1,0:T(8,128)(2,1)S(1)}, bf16[8,128,128]{2,1,0:T(8,128)(2,1)S(1)}, u32[]{:S(2)}, u32[]{:S(2)}) collective-permute-start(bf16[8,128,128]{2,1,0:T(8,128)(2,1)S(1)} %get-tuple-element.26), channel_id=1, source_target_pairs={{0,4},{2,6},{4,0},{6,2},{8,12},{10,14},{12,8},{14,10},{16,20},{18,... | collective-permute-start | bytes 786440 | tf_op jit(solution)/shard_map/ppermute | solution.py:15
  25.6 1.2 order.1
  26.9 1.3 collective-permute-start.18
  28.2 3.6 %collective-permute-start.17 = (bf16[1280,256]{1,0:T(8,128)(2,1)S(1)}, bf16[1280,256]{1,0:T(8,128)(2,1)S(1)}, u32[]{:S(2)}, u32[]{:S(2)}) collective-permute-start(bf16[1280,256]{1,0:T(8,128)(2,1)S(1)} %get-tuple-element.32.refs_6_.refs_8_), channel_id=1, source_target_pairs={{0,16},{2,18},{4,20},{6,22},{8,24},{10,26},{12,28},{14,30},{16,0},... | collective-permute-start | bytes 1966088 | tf_op jit(solution)/shard_map/ppermute | solution.py:15
  33.4 2.6 %collective-permute-start.19 = (bf16[768,256]{1,0:T(8,128)(2,1)S(1)}, bf16[768,256]{1,0:T(8,128)(2,1)S(1)}, u32[]{:S(2)}, u32[]{:S(2)}) collective-permute-start(bf16[768,256]{1,0:T(8,128)(2,1)S(1)} %get-tuple-element.33.refs_7_.refs_9_), channel_id=1, source_target_pairs={{0,16},{2,18},{4,20},{6,22},{8,24},{10,26},{12,28},{14,30},{1,17},... | collective-permute-start | bytes 1179656 | tf_op jit(solution)/shard_map/ppermute | solution.py:24
  36.0 23.6 %collective-permute-done.18.refs_9_.refs_11_ = bf16[768,256]{1,0:T(8,128)(2,1)S(1)} collective-permute-done((bf16[768,256]{1,0:T(8,128)(2,1)S(1)}, bf16[768,256]{1,0:T(8,128)(2,1)S(1)}, u32[]{:S(2)}, u32[]{:S(2)}) %collective-permute-start.18) | collective-permute-done | bytes 393248 | tf_op jit(solution)/shard_map/ppermute | solution.py:24
  61.5 1.6 %collective-permute-start.26 = (bf16[768,256]{1,0:T(8,128)(2,1)S(1)}, bf16[768,256]{1,0:T(8,128)(2,1)S(1)}, u32[]{:S(2)}, u32[]{:S(2)}) collective-permute-start(bf16[768,256]{1,0:T(8,128)(2,1)S(1)} %get-tuple-element.33.refs_7_.refs_9_), channel_id=1, source_target_pairs={{0,2},{2,0},{4,6},{6,4},{8,10},{10,8},{12,14},{14,12},{16,18},{18,... | collective-permute-start | bytes 1179656 | tf_op jit(solution)/shard_map/ppermute | solution.py:15
  63.1 4.7 %collective-permute-done.9.refs_2_ = bf16[8,128,128]{2,1,0:T(8,128)(2,1)S(1)} collective-permute-done((bf16[8,128,128]{2,1,0:T(8,128)(2,1)S(1)}, bf16[8,128,128]{2,1,0:T(8,128)(2,1)S(1)}, u32[]{:S(2)}, u32[]{:S(2)}) %collective-permute-start.9) | collective-permute-done | bytes 262176 | tf_op jit(solution)/shard_map/ppermute | solution.py:15
  69.1 4.4 %collective-permute-done.17.refs_8_.refs_10_ = bf16[1280,256]{1,0:T(8,128)(2,1)S(1)} collective-permute-done((bf16[1280,256]{1,0:T(8,128)(2,1)S(1)}, bf16[1280,256]{1,0:T(8,128)(2,1)S(1)}, u32[]{:S(2)}, u32[]{:S(2)}) %collective-permute-start.17) | collective-permute-done | bytes 655392 | tf_op jit(solution)/shard_map/ppermute | solution.py:15
  74.1 2.4 %collective-permute-start.28 = (bf16[768,256]{1,0:T(8,128)(2,1)S(1)}, bf16[768,256]{1,0:T(8,128)(2,1)S(1)}, u32[]{:S(2)}, u32[]{:S(2)}) collective-permute-start(bf16[768,256]{1,0:T(8,128)(2,1)S(1)} %collective-permute-done.18.refs_9_.refs_11_), channel_id=1, source_target_pairs={{0,2},{2,0},{4,6},{6,4},{8,10},{10,8},{12,14},{14,12},{1,3},{3,1},... | collective-permute-start | bytes 1179656 | tf_op jit(solution)/shard_map/ppermute | solution.py:33
  77.2 4.6 %collective-permute-done.12.refs_1_ = bf16[8,128,128]{2,1,0:T(8,128)(2,1)S(1)} collective-permute-done((bf16[8,128,128]{2,1,0:T(8,128)(2,1)S(1)}, bf16[8,128,128]{2,1,0:T(8,128)(2,1)S(1)}, u32[]{:S(2)}, u32[]{:S(2)}) %collective-permute-start.12) | collective-permute-done | bytes 262176 | tf_op jit(solution)/shard_map/ppermute | solution.py:15
  87.7 18.4 %collective-permute-start.15 = (bf16[128,1024]{1,0:T(8,128)(2,1)S(1)}, bf16[128,1024]{1,0:T(8,128)(2,1)S(1)}, u32[]{:S(2)}, u32[]{:S(2)}) collective-permute-start(bf16[128,1024]{1,0:T(8,128)(2,1)S(1)} %shard_map.69.refs_0_), channel_id=1, source_target_pairs={{0,8},{2,10},{4,12},{6,14},{8,0},{10,2},{12,4},{14,6},{16,24},{18,... | collective-permute-start | bytes 786440 | tf_op jit(solution)/shard_map/ppermute | solution.py:15
  108.2 1.5 %collective-permute-start.14 = (bf16[128,1024]{1,0:T(8,128)(2,1)S(1)}, bf16[128,1024]{1,0:T(8,128)(2,1)}, u32[]{:S(2)}, u32[]{:S(2)}) collective-permute-start(bf16[128,1024]{1,0:T(8,128)(2,1)S(1)} %shard_map.69.refs_0_), channel_id=1, source_target_pairs={{0,4},{2,6},{4,0},{6,2},{8,12},{10,14},{12,8},{14,10},{16,20},{18,... | collective-permute-start | bytes 786440 | tf_op jit(solution)/shard_map/ppermute | solution.py:15
  110.5 4.0 %collective-permute-start.16 = (bf16[128,1024]{1,0:T(8,128)(2,1)S(1)}, bf16[128,1024]{1,0:T(8,128)(2,1)}, u32[]{:S(2)}, u32[]{:S(2)}) collective-permute-start(bf16[128,1024]{1,0:T(8,128)(2,1)S(1)} %shard_map.71.refs_1_), channel_id=1, source_target_pairs={{0,8},{2,10},{4,12},{6,14},{8,0},{10,2},{12,4},{14,6},{16,24},{18,... | collective-permute-start | bytes 786440 | tf_op jit(solution)/shard_map/ppermute | solution.py:15
  114.5 1.5 %collective-permute-start.24 = (bf16[128,1024]{1,0:T(8,128)(2,1)S(1)}, bf16[128,1024]{1,0:T(8,128)(2,1)}, u32[]{:S(2)}, u32[]{:S(2)}) collective-permute-start(bf16[128,1024]{1,0:T(8,128)(2,1)S(1)} %collective-permute-done.15.refs_4_), channel_id=1, source_target_pairs={{0,4},{2,6},{4,0},{6,2},{8,12},{10,14},{12,8},{14,10},{16,20},{18,... | collective-permute-start | bytes 786440 | tf_op jit(solution)/shard_map/ppermute | solution.py:15
  116.1 3.7 %collective-permute-done.14.refs_3_ = bf16[128,1024]{1,0:T(8,128)(2,1)} collective-permute-done((bf16[128,1024]{1,0:T(8,128)(2,1)S(1)}, bf16[128,1024]{1,0:T(8,128)(2,1)}, u32[]{:S(2)}, u32[]{:S(2)}) %collective-permute-start.14) | collective-permute-done | bytes 262176 | tf_op jit(solution)/shard_map/ppermute | solution.py:15
  119.8 2.8 %collective-permute-done.24.refs_7_ = bf16[128,1024]{1,0:T(8,128)(2,1)} collective-permute-done((bf16[128,1024]{1,0:T(8,128)(2,1)S(1)}, bf16[128,1024]{1,0:T(8,128)(2,1)}, u32[]{:S(2)}, u32[]{:S(2)}) %collective-permute-start.24) | collective-permute-done | bytes 262176 | tf_op jit(solution)/shard_map/ppermute | solution.py:15
  126.7 3.0 %shard_map.74 = (f32[640,256]{1,0:T(8,128)S(1)}, bf16[640,256]{1,0:T(8,128)(2,1)S(1)}) custom-call(s32[1]{0:T(128)} %bitcast.8.mine_ref, bf16[128,1024]{1,0:T(8,128)(2,1)S(1)} %shard_map.69.refs_0_, bf16[128,1024]{1,0:T(8,128)(2,1)S(1)} %shard_map.71.refs_1_, bf16[128,1024]{1,0:T(8,128)(2,1)S(1)} %collective-permute-done.13.refs_2_, ...), custom_call_target="tpu_custom_call" | custom-call | tf_op jit(solution)/shard_map/pallas_call | solution.py:67
  129.8 2.0 %shard_map.72 = (f32[384,256]{1,0:T(8,128)S(1)}, bf16[384,256]{1,0:T(8,128)(2,1)S(1)}) custom-call(s32[1]{0:T(128)} %bitcast.8.mine_ref, bf16[128,1024]{1,0:T(8,128)(2,1)S(1)} %shard_map.69.refs_0_, bf16[128,1024]{1,0:T(8,128)(2,1)S(1)} %shard_map.71.refs_1_, bf16[128,1024]{1,0:T(8,128)(2,1)S(1)} %collective-permute-done.13.refs_2_, ...), custom_call_target="tpu_custom_call" | custom-call | tf_op jit(solution)/shard_map/pallas_call | solution.py:67
  132.5 2.2 %collective-permute-start.33 = (bf16[128,512]{1,0:T(8,128)(2,1)S(1)}, bf16[128,512]{1,0:T(8,128)(2,1)S(1)}, u32[]{:S(2)}, u32[]{:S(2)}) collective-permute-start(bf16[128,512]{1,0:T(8,128)(2,1)S(1)} %get-tuple-element.44), channel_id=1, source_target_pairs={{0,12},{2,14},{4,8},{6,10},{8,4},{10,6},{12,0},{14,2},{16,28},{18,... | collective-permute-start | bytes 393224 | tf_op jit(solution)/shard_map/ppermute | solution.py:15
  136.8 2.0 %collective-permute-start.32 = (bf16[128,256]{1,0:T(8,128)(2,1)S(1)}, bf16[128,256]{1,0:T(8,128)(2,1)S(1)}, u32[]{:S(2)}, u32[]{:S(2)}) collective-permute-start(bf16[128,256]{1,0:T(8,128)(2,1)S(1)} %get-tuple-element.43), channel_id=1, source_target_pairs={{0,8},{2,10},{4,12},{6,14},{8,0},{10,2},{12,4},{14,6},{16,24},{18,... | collective-permute-start | bytes 196616 | tf_op jit(solution)/shard_map/ppermute | solution.py:15
  138.9 1.5 %collective-permute-done.21.refs_1_ = bf16[128,256]{1,0:T(8,128)(2,1)S(1)} collective-permute-done((bf16[128,256]{1,0:T(8,128)(2,1)S(1)}, bf16[128,256]{1,0:T(8,128)(2,1)S(1)}, u32[]{:S(2)}, u32[]{:S(2)}) %collective-permute-start.21) | collective-permute-done | bytes 65568 | tf_op jit(solution)/shard_map/ppermute | solution.py:15
  140.4 1.3 collective-permute-done.31.refs_4_
  141.7 1.4 assemble.1
  (78 shorter events, 21.9 us)
Async XLA Ops:
  2.2 9.4 %collective-permute-start.1 = (bf16[8,128,128]{2,1,0:T(8,128)(2,1)S(1)}, bf16[8,128,128]{2,1,0:T(8,128)(2,1)S(1)}, u32[]{:S(2)}, u32[]{:S(2)}) collective-permute-start(bf16[8,128,128]{2,1,0:T(8,128)(2,1)S(1)} %get-tuple-element.27), channel_id=1, source_target_pairs={{0,4},{2,6},{4,0},{6,2},{8,12},{10,14},{12,8},{14,10},{16,20},{18,... | collective-permute-start | bytes 786440 | tf_op jit(solution)/shard_map/ppermute | solution.py:15
  5.2 8.0 %collective-permute-start = (bf16[8,128,128]{2,1,0:T(8,128)(2,1)S(1)}, bf16[8,128,128]{2,1,0:T(8,128)(2,1)S(1)}, u32[]{:S(2)}, u32[]{:S(2)}) collective-permute-start(bf16[8,128,128]{2,1,0:T(8,128)(2,1)S(1)} %get-tuple-element.26), channel_id=1, source_target_pairs={{0,2},{2,0},{4,6},{6,4},{8,10},{10,8},{12,14},{14,12},{16,18},{18,... | collective-permute-start | bytes 786440 | tf_op jit(solution)/shard_map/ppermute | solution.py:15
  11.5 7.5 %collective-permute-start.2 = (bf16[8,128,128]{2,1,0:T(8,128)(2,1)S(1)}, bf16[8,128,128]{2,1,0:T(8,128)(2,1)S(1)}, u32[]{:S(2)}, u32[]{:S(2)}) collective-permute-start(bf16[8,128,128]{2,1,0:T(8,128)(2,1)S(1)} %collective-permute-done.1.side_ref.refs_1_), channel_id=1, source_target_pairs={{0,2},{2,0},{4,6},{6,4},{8,10},{10,8},{12,14},{14,12},{16,18},{18,... | collective-permute-start | bytes 786440 | tf_op jit(solution)/shard_map/ppermute | solution.py:15
  19.1 12.7 %collective-permute-start.3 = (bf16[8,128,128]{2,1,0:T(8,128)(2,1)S(1)}, bf16[8,128,128]{2,1,0:T(8,128)(2,1)S(1)}, u32[]{:S(2)}, u32[]{:S(2)}) collective-permute-start(bf16[8,128,128]{2,1,0:T(8,128)(2,1)S(1)} %get-tuple-element.29), channel_id=1, source_target_pairs={{0,8},{2,10},{4,12},{6,14},{1,9},{3,11},{5,13},{7,15}} | collective-permute-start | bytes 786440 | tf_op jit(solution)/shard_map/ppermute | solution.py:24
  22.6 10.1 %collective-permute-start.7 = (bf16[8,128,128]{2,1,0:T(8,128)(2,1)S(1)}, bf16[8,128,128]{2,1,0:T(8,128)(2,1)S(1)}, u32[]{:S(2)}, u32[]{:S(2)}) collective-permute-start(bf16[8,128,128]{2,1,0:T(8,128)(2,1)S(1)} %get-tuple-element.27), channel_id=1, source_target_pairs={{0,2},{2,0},{4,6},{6,4},{8,10},{10,8},{12,14},{14,12},{16,18},{18,... | collective-permute-start | bytes 786440 | tf_op jit(solution)/shard_map/ppermute | solution.py:15
  24.1 9.3 %collective-permute-start.8 = (bf16[8,128,128]{2,1,0:T(8,128)(2,1)S(1)}, bf16[8,128,128]{2,1,0:T(8,128)(2,1)S(1)}, u32[]{:S(2)}, u32[]{:S(2)}) collective-permute-start(bf16[8,128,128]{2,1,0:T(8,128)(2,1)S(1)} %get-tuple-element.26), channel_id=1, source_target_pairs={{0,4},{2,6},{4,0},{6,2},{8,12},{10,14},{12,8},{14,10},{16,20},{18,... | collective-permute-start | bytes 786440 | tf_op jit(solution)/shard_map/ppermute | solution.py:15
  26.9 32.7 %collective-permute-start.18 = (bf16[768,256]{1,0:T(8,128)(2,1)S(1)}, bf16[768,256]{1,0:T(8,128)(2,1)S(1)}, u32[]{:S(2)}, u32[]{:S(2)}) collective-permute-start(bf16[768,256]{1,0:T(8,128)(2,1)S(1)} %get-tuple-element.33.refs_7_.refs_9_), channel_id=1, source_target_pairs={{16,0},{18,2},{20,4},{22,6},{24,8},{26,10},{28,12},{30,14},{17,1},... | collective-permute-start | bytes 1179656 | tf_op jit(solution)/shard_map/ppermute | solution.py:24
  28.2 45.4 %collective-permute-start.17 = (bf16[1280,256]{1,0:T(8,128)(2,1)S(1)}, bf16[1280,256]{1,0:T(8,128)(2,1)S(1)}, u32[]{:S(2)}, u32[]{:S(2)}) collective-permute-start(bf16[1280,256]{1,0:T(8,128)(2,1)S(1)} %get-tuple-element.32.refs_6_.refs_8_), channel_id=1, source_target_pairs={{0,16},{2,18},{4,20},{6,22},{8,24},{10,26},{12,28},{14,30},{16,0},... | collective-permute-start | bytes 1966088 | tf_op jit(solution)/shard_map/ppermute | solution.py:15
  31.9 28.3 %collective-permute-start.5 = (bf16[8,128,128]{2,1,0:T(8,128)(2,1)S(1)}, bf16[8,128,128]{2,1,0:T(8,128)(2,1)S(1)}, u32[]{:S(2)}, u32[]{:S(2)}) collective-permute-start(bf16[8,128,128]{2,1,0:T(8,128)(2,1)S(1)} %shard_map.67), channel_id=1, source_target_pairs={{8,24},{10,26},{12,28},{14,30},{9,25},{11,27},{13,29},{15,31}} | collective-permute-start | bytes 786440 | tf_op jit(solution)/shard_map/ppermute | solution.py:24
  32.7 28.1 %collective-permute-start.6 = (bf16[8,128,128]{2,1,0:T(8,128)(2,1)S(1)}, bf16[8,128,128]{2,1,0:T(8,128)(2,1)S(1)}, u32[]{:S(2)}, u32[]{:S(2)}) collective-permute-start(bf16[8,128,128]{2,1,0:T(8,128)(2,1)S(1)} %shard_map.67), channel_id=1, source_target_pairs={{8,16},{10,18},{12,20},{14,22},{9,17},{11,19},{13,21},{15,23}} | collective-permute-start | bytes 786440 | tf_op jit(solution)/shard_map/ppermute | solution.py:24
  33.4 28.1 %collective-permute-start.19 = (bf16[768,256]{1,0:T(8,128)(2,1)S(1)}, bf16[768,256]{1,0:T(8,128)(2,1)S(1)}, u32[]{:S(2)}, u32[]{:S(2)}) collective-permute-start(bf16[768,256]{1,0:T(8,128)(2,1)S(1)} %get-tuple-element.33.refs_7_.refs_9_), channel_id=1, source_target_pairs={{0,16},{2,18},{4,20},{6,22},{8,24},{10,26},{12,28},{14,30},{1,17},... | collective-permute-start | bytes 1179656 | tf_op jit(solution)/shard_map/ppermute | solution.py:24
  59.6 8.1 %collective-permute-start.9 = (bf16[8,128,128]{2,1,0:T(8,128)(2,1)S(1)}, bf16[8,128,128]{2,1,0:T(8,128)(2,1)S(1)}, u32[]{:S(2)}, u32[]{:S(2)}) collective-permute-start(bf16[8,128,128]{2,1,0:T(8,128)(2,1)S(1)} %collective-permute-done.near_ref.refs_0_), channel_id=1, source_target_pairs={{0,4},{2,6},{4,0},{6,2},{8,12},{10,14},{12,8},{14,10},{16,20},{18,... | collective-permute-start | bytes 786440 | tf_op jit(solution)/shard_map/ppermute | solution.py:15
  60.1 8.3 %collective-permute-start.4 = (bf16[8,128,128]{2,1,0:T(8,128)(2,1)S(1)}, bf16[8,128,128]{2,1,0:T(8,128)(2,1)S(1)}, u32[]{:S(2)}, u32[]{:S(2)}) collective-permute-start(bf16[8,128,128]{2,1,0:T(8,128)(2,1)S(1)} %get-tuple-element.29), channel_id=1, source_target_pairs={{16,24},{18,26},{20,28},{22,30},{17,25},{19,27},{21,29},{23,31}} | collective-permute-start | bytes 786440 | tf_op jit(solution)/shard_map/ppermute | solution.py:24
  60.8 45.3 %collective-permute-start.25 = (bf16[1280,256]{1,0:T(8,128)(2,1)S(1)}, bf16[1280,256]{1,0:T(8,128)(2,1)S(1)}, u32[]{:S(2)}, u32[]{:S(2)}) collective-permute-start(bf16[1280,256]{1,0:T(8,128)(2,1)S(1)} %get-tuple-element.32.refs_6_.refs_8_), channel_id=1, source_target_pairs={{0,2},{2,0},{4,6},{6,4},{8,10},{10,8},{12,14},{14,12},{16,18},{18,... | collective-permute-start | bytes 1966088 | tf_op jit(solution)/shard_map/ppermute | solution.py:15
  61.5 25.4 %collective-permute-start.26 = (bf16[768,256]{1,0:T(8,128)(2,1)S(1)}, bf16[768,256]{1,0:T(8,128)(2,1)S(1)}, u32[]{:S(2)}, u32[]{:S(2)}) collective-permute-start(bf16[768,256]{1,0:T(8,128)(2,1)S(1)} %get-tuple-element.33.refs_7_.refs_9_), channel_id=1, source_target_pairs={{0,2},{2,0},{4,6},{6,4},{8,10},{10,8},{12,14},{14,12},{16,18},{18,... | collective-permute-start | bytes 1179656 | tf_op jit(solution)/shard_map/ppermute | solution.py:15
  67.8 6.3 %collective-permute-start.10 = (bf16[8,128,128]{2,1,0:T(8,128)(2,1)S(1)}, bf16[8,128,128]{2,1,0:T(8,128)(2,1)S(1)}, u32[]{:S(2)}, u32[]{:S(2)}) collective-permute-start(bf16[8,128,128]{2,1,0:T(8,128)(2,1)S(1)} %collective-permute-done.3.refs_3_.other_ref), channel_id=1, source_target_pairs={{8,12},{10,14},{12,8},{14,10},{9,13},{11,15},{13,9},{15,11}} | collective-permute-start | bytes 786440 | tf_op jit(solution)/shard_map/ppermute | solution.py:38
  68.4 8.1 %collective-permute-start.11 = (bf16[8,128,128]{2,1,0:T(8,128)(2,1)S(1)}, bf16[8,128,128]{2,1,0:T(8,128)(2,1)S(1)}, u32[]{:S(2)}, u32[]{:S(2)}) collective-permute-start(bf16[8,128,128]{2,1,0:T(8,128)(2,1)S(1)} %collective-permute-done.4.refs_0_), channel_id=1, source_target_pairs={{24,28},{26,30},{28,24},{30,26},{25,29},{27,31},{29,25},{31,27}} | collective-permute-start | bytes 786440 | tf_op jit(solution)/shard_map/ppermute | solution.py:38
  73.6 8.2 %collective-permute-start.12 = (bf16[8,128,128]{2,1,0:T(8,128)(2,1)S(1)}, bf16[8,128,128]{2,1,0:T(8,128)(2,1)S(1)}, u32[]{:S(2)}, u32[]{:S(2)}) collective-permute-start(bf16[8,128,128]{2,1,0:T(8,128)(2,1)S(1)} %shard_map.68.refs_1_), channel_id=1, source_target_pairs={{0,4},{2,6},{4,0},{6,2},{8,12},{10,14},{12,8},{14,10},{16,20},{18,... | collective-permute-start | bytes 786440 | tf_op jit(solution)/shard_map/ppermute | solution.py:15
  74.1 33.4 %collective-permute-start.28 = (bf16[768,256]{1,0:T(8,128)(2,1)S(1)}, bf16[768,256]{1,0:T(8,128)(2,1)S(1)}, u32[]{:S(2)}, u32[]{:S(2)}) collective-permute-start(bf16[768,256]{1,0:T(8,128)(2,1)S(1)} %collective-permute-done.18.refs_9_.refs_11_), channel_id=1, source_target_pairs={{0,2},{2,0},{4,6},{6,4},{8,10},{10,8},{12,14},{14,12},{1,3},{3,1},... | collective-permute-start | bytes 1179656 | tf_op jit(solution)/shard_map/ppermute | solution.py:33
  76.5 33.2 %collective-permute-start.29 = (bf16[768,256]{1,0:T(8,128)(2,1)S(1)}, bf16[768,256]{1,0:T(8,128)(2,1)S(1)}, u32[]{:S(2)}, u32[]{:S(2)}) collective-permute-start(bf16[768,256]{1,0:T(8,128)(2,1)S(1)} %collective-permute-done.19.refs_10_.refs_12_), channel_id=1, source_target_pairs={{16,18},{18,16},{20,22},{22,20},{24,26},{26,24},{28,30},{30,28},{1... | collective-permute-start | bytes 1179656 | tf_op jit(solution)/shard_map/ppermute | solution.py:33
  81.8 38.0 %collective-permute-start.27 = (bf16[1280,256]{1,0:T(8,128)(2,1)S(1)}, bf16[1280,256]{1,0:T(8,128)(2,1)}, u32[]{:S(2)}, u32[]{:S(2)}) collective-permute-start(bf16[1280,256]{1,0:T(8,128)(2,1)S(1)} %collective-permute-done.17.refs_8_.refs_10_), channel_id=1, source_target_pairs={{0,2},{2,0},{4,6},{6,4},{8,10},{10,8},{12,14},{14,12},{16,18},{18,... | collective-permute-start | bytes 1966088 | tf_op jit(solution)/shard_map/ppermute | solution.py:15
  87.7 26.8 %collective-permute-start.15 = (bf16[128,1024]{1,0:T(8,128)(2,1)S(1)}, bf16[128,1024]{1,0:T(8,128)(2,1)S(1)}, u32[]{:S(2)}, u32[]{:S(2)}) collective-permute-start(bf16[128,1024]{1,0:T(8,128)(2,1)S(1)} %shard_map.69.refs_0_), channel_id=1, source_target_pairs={{0,8},{2,10},{4,12},{6,14},{8,0},{10,2},{12,4},{14,6},{16,24},{18,... | collective-permute-start | bytes 786440 | tf_op jit(solution)/shard_map/ppermute | solution.py:15
  107.0 9.2 %collective-permute-start.13 = (bf16[128,1024]{1,0:T(8,128)(2,1)S(1)}, bf16[128,1024]{1,0:T(8,128)(2,1)S(1)}, u32[]{:S(2)}, u32[]{:S(2)}) collective-permute-start(bf16[128,1024]{1,0:T(8,128)(2,1)S(1)} %shard_map.71.refs_1_), channel_id=1, source_target_pairs={{0,4},{2,6},{4,0},{6,2},{8,12},{10,14},{12,8},{14,10},{16,20},{18,... | collective-permute-start | bytes 786440 | tf_op jit(solution)/shard_map/ppermute | solution.py:15
  108.2 11.6 %collective-permute-start.14 = (bf16[128,1024]{1,0:T(8,128)(2,1)S(1)}, bf16[128,1024]{1,0:T(8,128)(2,1)}, u32[]{:S(2)}, u32[]{:S(2)}) collective-permute-start(bf16[128,1024]{1,0:T(8,128)(2,1)S(1)} %shard_map.69.refs_0_), channel_id=1, source_target_pairs={{0,4},{2,6},{4,0},{6,2},{8,12},{10,14},{12,8},{14,10},{16,20},{18,... | collective-permute-start | bytes 786440 | tf_op jit(solution)/shard_map/ppermute | solution.py:15
  110.5 9.3 %collective-permute-start.16 = (bf16[128,1024]{1,0:T(8,128)(2,1)S(1)}, bf16[128,1024]{1,0:T(8,128)(2,1)}, u32[]{:S(2)}, u32[]{:S(2)}) collective-permute-start(bf16[128,1024]{1,0:T(8,128)(2,1)S(1)} %shard_map.71.refs_1_), channel_id=1, source_target_pairs={{0,8},{2,10},{4,12},{6,14},{8,0},{10,2},{12,4},{14,6},{16,24},{18,... | collective-permute-start | bytes 786440 | tf_op jit(solution)/shard_map/ppermute | solution.py:15
  114.5 8.1 %collective-permute-start.24 = (bf16[128,1024]{1,0:T(8,128)(2,1)S(1)}, bf16[128,1024]{1,0:T(8,128)(2,1)}, u32[]{:S(2)}, u32[]{:S(2)}) collective-permute-start(bf16[128,1024]{1,0:T(8,128)(2,1)S(1)} %collective-permute-done.15.refs_4_), channel_id=1, source_target_pairs={{0,4},{2,6},{4,0},{6,2},{8,12},{10,14},{12,8},{14,10},{16,20},{18,... | collective-permute-start | bytes 786440 | tf_op jit(solution)/shard_map/ppermute | solution.py:15
  116.1 6.5 %collective-permute-start.23 = (bf16[128,1024]{1,0:T(8,128)(2,1)S(1)}, bf16[128,1024]{1,0:T(8,128)(2,1)}, u32[]{:S(2)}, u32[]{:S(2)}) collective-permute-start(bf16[128,1024]{1,0:T(8,128)(2,1)S(1)} %collective-permute-done.13.refs_2_), channel_id=1, source_target_pairs={{0,8},{2,10},{4,12},{6,14},{8,0},{10,2},{12,4},{14,6},{16,24},{18,... | collective-permute-start | bytes 786440 | tf_op jit(solution)/shard_map/ppermute | solution.py:15
  132.5 9.2 %collective-permute-start.33 = (bf16[128,512]{1,0:T(8,128)(2,1)S(1)}, bf16[128,512]{1,0:T(8,128)(2,1)S(1)}, u32[]{:S(2)}, u32[]{:S(2)}) collective-permute-start(bf16[128,512]{1,0:T(8,128)(2,1)S(1)} %get-tuple-element.44), channel_id=1, source_target_pairs={{0,12},{2,14},{4,8},{6,10},{8,4},{10,6},{12,0},{14,2},{16,28},{18,... | collective-permute-start | bytes 393224 | tf_op jit(solution)/shard_map/ppermute | solution.py:15
  134.7 5.7 %collective-permute-start.21 = (bf16[128,256]{1,0:T(8,128)(2,1)S(1)}, bf16[128,256]{1,0:T(8,128)(2,1)S(1)}, u32[]{:S(2)}, u32[]{:S(2)}) collective-permute-start(bf16[128,256]{1,0:T(8,128)(2,1)S(1)} %get-tuple-element.37), channel_id=1, source_target_pairs={{0,4},{2,6},{4,0},{6,2},{8,12},{10,14},{12,8},{14,10},{16,20},{18,... | collective-permute-start | bytes 196616 | tf_op jit(solution)/shard_map/ppermute | solution.py:15
  135.3 5.1 %collective-permute-start.22 = (bf16[128,256]{1,0:T(8,128)(2,1)S(1)}, bf16[128,256]{1,0:T(8,128)(2,1)S(1)}, u32[]{:S(2)}, u32[]{:S(2)}) collective-permute-start(bf16[128,256]{1,0:T(8,128)(2,1)S(1)} %get-tuple-element.38), channel_id=1, source_target_pairs={{0,8},{2,10},{4,12},{6,14},{8,0},{10,2},{12,4},{14,6},{16,24},{18,... | collective-permute-start | bytes 196616 | tf_op jit(solution)/shard_map/ppermute | solution.py:15
  136.2 5.4 %collective-permute-start.31 = (bf16[128,256]{1,0:T(8,128)(2,1)S(1)}, bf16[128,256]{1,0:T(8,128)(2,1)S(1)}, u32[]{:S(2)}, u32[]{:S(2)}) collective-permute-start(bf16[128,256]{1,0:T(8,128)(2,1)S(1)} %get-tuple-element.42), channel_id=1, source_target_pairs={{0,4},{2,6},{4,0},{6,2},{8,12},{10,14},{12,8},{14,10},{16,20},{18,... | collective-permute-start | bytes 196616 | tf_op jit(solution)/shard_map/ppermute | solution.py:15
  136.8 4.9 %collective-permute-start.32 = (bf16[128,256]{1,0:T(8,128)(2,1)S(1)}, bf16[128,256]{1,0:T(8,128)(2,1)S(1)}, u32[]{:S(2)}, u32[]{:S(2)}) collective-permute-start(bf16[128,256]{1,0:T(8,128)(2,1)S(1)} %get-tuple-element.43), channel_id=1, source_target_pairs={{0,8},{2,10},{4,12},{6,14},{8,0},{10,2},{12,4},{14,6},{16,24},{18,... | collective-permute-start | bytes 196616 | tf_op jit(solution)/shard_map/ppermute | solution.py:15
  (15 other events, 208.4 us)
